TPU v7x, 32 devices: a whole 2x2x4 slice. The times are simulated.
32 devices in a mesh: dp: 16 (over z, x, core), tensor: 2 (over y).
Axes of the slice: x: 2, y: 2, z: 4, core: 2. Of those that a mesh axis runs over, the one named last changes fastest.
Arguments:
- hidden_in: bfloat16 [20480, 768], P('dp'), may hold values from -6 to 6
- cotangent: bfloat16 [20480, 768], P('dp'), may hold values from -6 to 6
- prompt_start: int32 [4], replicated, may hold values from 0 to 511
- cont_gap: int32 [4, 12], replicated, may hold values from 0 to 511
- seg_len: int32 [6, 3], replicated, may hold values from 256 to 5120, as said below
- dilation_rate: int32 [6, 3], replicated, may hold values from 1 to 6, as said below
- pre_gain: bfloat16 [768], replicated, may hold values from 0.5 to 1.5
- pre_bias: bfloat16 [768], replicated, may hold values from -1 to 1
- query_weight: bfloat16 [768, 768], P(None, 'tensor'), may hold values from -0.21875 to 0.21875
- query_bias: bfloat16 [768], P('tensor'), may hold values from -1 to 1
- key_weight: bfloat16 [768, 768], P(None, 'tensor'), may hold values from -0.21875 to 0.21875
- value_weight: bfloat16 [768, 768], P(None, 'tensor'), may hold values from -0.21875 to 0.21875
- value_bias: bfloat16 [768], P('tensor'), may hold values from -1 to 1
- sub_gain: bfloat16 [768], P('tensor'), may hold values from 0.5 to 1.5
- sub_bias: bfloat16 [768], P('tensor'), may hold values from -1 to 1
- out_weight: bfloat16 [768, 768], P('tensor'), may hold values from -0.21875 to 0.21875
- out_bias: bfloat16 [768], replicated, may hold values from -1 to 1
- mid_gain: bfloat16 [768], replicated, may hold values from 0.5 to 1.5
- mid_bias: bfloat16 [768], replicated, may hold values from -1 to 1
- inner_weight: bfloat16 [768, 3072], P(None, 'tensor'), may hold values from -0.21875 to 0.21875
- inner_bias: bfloat16 [3072], P('tensor'), may hold values from -1 to 1
- ffn_gain: bfloat16 [3072], P('tensor'), may hold values from 0.5 to 1.5
- ffn_bias: bfloat16 [3072], P('tensor'), may hold values from -1 to 1
- outer_weight: bfloat16 [3072, 768], P('tensor'), may hold values from -0.109375 to 0.109375
- outer_bias: bfloat16 [768], replicated, may hold values from -1 to 1
Outputs:
- output: bfloat16 [20480, 768], P('dp')
- input_grad: bfloat16 [20480, 768], P('dp')
- pre_gain_grad: float32 [768], P('dp')
- pre_bias_grad: float32 [768], P('dp')
- query_weight_grad: float32 [768, 768], P('dp', 'tensor')
- query_bias_grad: float32 [768], P(('tensor', 'dp'))
- key_weight_grad: float32 [768, 768], P('dp', 'tensor')
- value_weight_grad: float32 [768, 768], P('dp', 'tensor')
- value_bias_grad: float32 [768], P(('tensor', 'dp'))
- sub_gain_grad: float32 [768], P(('tensor', 'dp'))
- sub_bias_grad: float32 [768], P(('tensor', 'dp'))
- out_weight_grad: float32 [768, 768], P('tensor', 'dp')
- out_bias_grad: float32 [768], P('dp')
- mid_gain_grad: float32 [768], P('dp')
- mid_bias_grad: float32 [768], P('dp')
- inner_weight_grad: float32 [768, 3072], P('dp', 'tensor')
- inner_bias_grad: float32 [3072], P(('tensor', 'dp'))
- ffn_gain_grad: float32 [3072], P(('tensor', 'dp'))
- ffn_bias_grad: float32 [3072], P(('tensor', 'dp'))
- outer_weight_grad: float32 [3072, 768], P('tensor', 'dp')
- outer_bias_grad: float32 [768], P('dp')
Inputs may be any that keep to these rules, and one draw needn't show every extreme that they name: seg_len[a, c] is the segment length of configuration c of head pair a (heads 2a and 2a + 1); one segment of the last configuration holds every position of a group. dilation_rate[a, 0] = 1 for every head pair a.
All inputs are finite; a program needn't handle non-finite values.
Results may differ from a plain program's by a relative error of at most 0.017.
Values may be sent and summed in bfloat16 or wider, within the bound.
A program may use at most 256 MiB of HBM per device.

v0:
```python
import jax
import jax.numpy as jnp
from jax import lax
from jax.sharding import PartitionSpec as P

D = 768
HD = 64
FF = 3072
PROMPT = 2048
CONT = 256
GDEV = 4


EPSILON = 1e-05


def partner_2(value, axis, stride):
    return lax.ppermute(value, axis, [(i, i ^ 1 << stride) for i in range(lax.axis_size(axis))])


def contract_rows(left, right):
    return lax.dot_general(
        left, right, (((0,), (0,)), ((), ())), preferred_element_type=jnp.float32
    )


def back_project(left, right):
    return lax.dot_general(
        left, right, (((1,), (1,)), ((), ())), preferred_element_type=jnp.float32
    )


def exact_gelu(values):
    return jax.nn.gelu(values, approximate=False)


def norm_rows(values, gain, bias):
    center = jnp.mean(values, axis=-1, keepdims=True)
    spread = jnp.mean(values * values, axis=-1, keepdims=True) - center * center
    scaled = lax.rsqrt(spread + EPSILON)
    unit_rows = (values - center) * scaled
    return (unit_rows * gain + bias, unit_rows, scaled)


def local_norm_back(grad_rows, gain, unit_rows, scaled):
    shaped = grad_rows * gain
    return scaled * (
        shaped
        - jnp.mean(shaped, axis=-1, keepdims=True)
        - unit_rows * jnp.mean(shaped * unit_rows, axis=-1, keepdims=True)
    )


def multiplicity(query_at, key_at, seg_heads, rate_heads, head_ids):
    query_grid = query_at[..., None, :, None]
    key_grid = key_at[..., None, None, :]
    counted = jnp.zeros((), jnp.float32)
    for config in range(seg_heads.shape[1]):
        seg_width = seg_heads[:, config][:, None, None]
        period = rate_heads[:, config][:, None, None]
        phase_id = (head_ids % rate_heads[:, config])[:, None, None]
        in_segment = (
            (query_grid // seg_width == key_grid // seg_width)
            & (query_grid % period == phase_id)
            & (key_grid % period == phase_id)
        )
        counted = counted + in_segment.astype(jnp.float32)
    return jnp.where(key_grid <= query_grid, counted, 0.0)


def weighted_logits(scores, weights):
    return jnp.where(weights > 0, scores + jnp.log(jnp.maximum(weights, 1.0)), -jnp.inf)


def block_logits(queries, prompt_keys, own_keys, query_at, prompt_at, own_at, tables):
    seg_table, rate_table, head_ids = tables
    logits = [
        weighted_logits(
            jnp.einsum("brhe,khe->bhrk", queries, prompt_keys, preferred_element_type=jnp.float32),
            multiplicity(query_at, prompt_at, seg_table, rate_table, head_ids),
        )
    ]
    if own_keys is not None:
        logits.append(
            weighted_logits(
                jnp.einsum(
                    "brhe,bkhe->bhrk", queries, own_keys, preferred_element_type=jnp.float32
                ),
                multiplicity(query_at, own_at, seg_table, rate_table, head_ids),
            )
        )
    return logits


def attend_forward(
    queries, prompt_keys, prompt_values, own_keys, own_values, query_at, prompt_at, own_at, tables
):
    logits = block_logits(queries, prompt_keys, own_keys, query_at, prompt_at, own_at, tables)
    row_top = jnp.max(logits[0], axis=-1)
    for logit_part in logits[1:]:
        row_top = jnp.maximum(row_top, jnp.max(logit_part, axis=-1))
    row_total = jnp.sum(jnp.exp(logits[0] - row_top[..., None]), axis=-1)
    for logit_part in logits[1:]:
        row_total = row_total + jnp.sum(jnp.exp(logit_part - row_top[..., None]), axis=-1)
    log_total = row_top + jnp.log(row_total)
    attended = jnp.einsum(
        "bhrk,khe->brhe",
        jnp.exp(logits[0] - log_total[..., None]).astype(jnp.bfloat16),
        prompt_values,
        preferred_element_type=jnp.float32,
    )
    if own_keys is not None:
        attended = attended + jnp.einsum(
            "bhrk,bkhe->brhe",
            jnp.exp(logits[1] - log_total[..., None]).astype(jnp.bfloat16),
            own_values,
            preferred_element_type=jnp.float32,
        )
    return (attended, log_total)


def attend_backward(
    queries,
    prompt_keys,
    prompt_values,
    own_keys,
    own_values,
    query_at,
    prompt_at,
    own_at,
    tables,
    log_total,
    grad_out,
):
    logits = block_logits(queries, prompt_keys, own_keys, query_at, prompt_at, own_at, tables)
    probabilities = [jnp.exp(logit_part - log_total[..., None]) for logit_part in logits]
    grad_probs = [
        jnp.einsum("brhe,khe->bhrk", grad_out, prompt_values, preferred_element_type=jnp.float32)
    ]
    if own_keys is not None:
        grad_probs.append(
            jnp.einsum("brhe,bkhe->bhrk", grad_out, own_values, preferred_element_type=jnp.float32)
        )
    inner_sum = jnp.sum(probabilities[0] * grad_probs[0], axis=-1)
    for position in range(1, len(logits)):
        inner_sum = inner_sum + jnp.sum(probabilities[position] * grad_probs[position], axis=-1)
    grad_scores = [
        (probabilities[position] * (grad_probs[position] - inner_sum[..., None])).astype(
            jnp.bfloat16
        )
        for position in range(len(logits))
    ]
    grad_queries = jnp.einsum(
        "bhrk,khe->brhe", grad_scores[0], prompt_keys, preferred_element_type=jnp.float32
    )
    prompt_key_grad = jnp.einsum(
        "bhrk,brhe->khe", grad_scores[0], queries, preferred_element_type=jnp.float32
    )
    prompt_value_grad = jnp.einsum(
        "bhrk,brhe->khe",
        probabilities[0].astype(jnp.bfloat16),
        grad_out,
        preferred_element_type=jnp.float32,
    )
    own_key_grad = None
    own_value_grad = None
    if own_keys is not None:
        grad_queries = grad_queries + jnp.einsum(
            "bhrk,bkhe->brhe", grad_scores[1], own_keys, preferred_element_type=jnp.float32
        )
        own_key_grad = jnp.einsum(
            "bhrk,brhe->bkhe", grad_scores[1], queries, preferred_element_type=jnp.float32
        )
        own_value_grad = jnp.einsum(
            "bhrk,brhe->bkhe",
            probabilities[1].astype(jnp.bfloat16),
            grad_out,
            preferred_element_type=jnp.float32,
        )
    return (grad_queries, prompt_key_grad, prompt_value_grad, own_key_grad, own_value_grad)


def gather_prompt(prompt_pair, device):
    collected = prompt_pair
    for level_bit in range(GDEV.bit_length() - 1):
        partner = partner_2(collected, "dp", level_bit)
        upper_bit = device // (1 << level_bit) % 2
        collected = jnp.where(
            upper_bit == 0,
            jnp.concatenate([collected, partner], axis=1),
            jnp.concatenate([partner, collected], axis=1),
        )
    return collected


def reduce_prompt(stacked, device):
    current = stacked
    for level_bit in reversed(range(GDEV.bit_length() - 1)):
        half_rows = current.shape[1] // 2
        upper_bit = device // (1 << level_bit) % 2
        lower_part = current[:, :half_rows]
        upper_part = current[:, half_rows:]
        sent_half = jnp.where(upper_bit == 1, lower_part, upper_part)
        kept_half = jnp.where(upper_bit == 1, upper_part, lower_part)
        current = kept_half + partner_2(sent_half.astype(jnp.bfloat16), "dp", level_bit).astype(
            sent_half.dtype
        )
    return current


def body(
    hidden_in,
    cotangent,
    prompt_start,
    cont_gap,
    seg_len,
    dilation_rate,
    pre_gain,
    pre_bias,
    query_weight,
    query_bias,
    key_weight,
    value_weight,
    value_bias,
    sub_gain,
    sub_bias,
    out_weight,
    out_bias,
    mid_gain,
    mid_bias,
    inner_weight,
    inner_bias,
    ffn_gain,
    ffn_bias,
    outer_weight,
    outer_bias,
):
    device = lax.axis_index("dp")
    group_id = device // GDEV
    member = device % GDEV
    tensor_id = lax.axis_index("tensor")
    local_width = query_weight.shape[1]
    local_heads = local_width // HD
    head_ids = tensor_id * local_heads + jnp.arange(local_heads)
    seg_table = lax.dynamic_slice_in_dim(
        jnp.repeat(seg_len, 2, axis=0), tensor_id * local_heads, local_heads, 0
    )
    rate_table = lax.dynamic_slice_in_dim(
        jnp.repeat(dilation_rate, 2, axis=0), tensor_id * local_heads, local_heads, 0
    )
    tables = (seg_table, rate_table, head_ids)
    prompt_rows = PROMPT // GDEV
    cont_rows = hidden_in.shape[0] - prompt_rows
    cont_count = cont_rows // CONT
    per_block = max(1, min(cont_count, 512 // CONT))
    while cont_count % per_block:
        per_block -= 1
    block_count = cont_count // per_block
    start_at = prompt_start[group_id]
    prompt_at = start_at + jnp.arange(PROMPT)
    own_prompt_at = lax.dynamic_slice_in_dim(prompt_at, member * prompt_rows, prompt_rows)
    gap_row = lax.dynamic_index_in_dim(cont_gap, group_id, 0, keepdims=False)
    own_gaps = lax.dynamic_slice_in_dim(gap_row, member * cont_count, cont_count)
    cont_at = (start_at + PROMPT + own_gaps[:, None] + jnp.arange(CONT)[None, :]).reshape(
        block_count, per_block, CONT
    )

    def heads_view(flat_rows):
        prompt_part = flat_rows[:prompt_rows].reshape(1, prompt_rows, local_heads, HD)
        cont_part = flat_rows[prompt_rows:].reshape(block_count, per_block, CONT, local_heads, HD)
        return (prompt_part, cont_part)

    inputs = hidden_in.astype(jnp.float32)
    pre_gain_f = pre_gain.astype(jnp.float32)
    pre_normed, pre_unit, pre_scale = norm_rows(inputs, pre_gain_f, pre_bias.astype(jnp.float32))
    pre_low = pre_normed.astype(jnp.bfloat16)
    queries_low = (
        (
            jnp.dot(pre_low, query_weight, preferred_element_type=jnp.float32)
            + query_bias.astype(jnp.float32)
        )
        * 0.125
    ).astype(jnp.bfloat16)
    keys_low = jnp.dot(pre_low, key_weight, preferred_element_type=jnp.float32).astype(jnp.bfloat16)
    values_low = (
        jnp.dot(pre_low, value_weight, preferred_element_type=jnp.float32)
        + value_bias.astype(jnp.float32)
    ).astype(jnp.bfloat16)
    query_prompt, query_cont = heads_view(queries_low)
    _, key_cont = heads_view(keys_low)
    _, value_cont = heads_view(values_low)
    prompt_pair = jnp.stack([keys_low[:prompt_rows], values_low[:prompt_rows]])
    gathered = gather_prompt(prompt_pair, device)
    prompt_keys = gathered[0].reshape(PROMPT, local_heads, HD)
    prompt_values = gathered[1].reshape(PROMPT, local_heads, HD)
    prompt_attended, prompt_log = attend_forward(
        query_prompt,
        prompt_keys,
        prompt_values,
        None,
        None,
        own_prompt_at[None],
        prompt_at,
        None,
        tables,
    )

    def cont_forward(pieces):
        block_q, block_k, block_v, block_at = pieces
        return attend_forward(
            block_q,
            prompt_keys,
            prompt_values,
            block_k,
            block_v,
            block_at,
            prompt_at,
            block_at,
            tables,
        )

    cont_attended, cont_log = lax.map(cont_forward, (query_cont, key_cont, value_cont, cont_at))
    attended = jnp.concatenate(
        [
            prompt_attended.reshape(prompt_rows, local_width),
            cont_attended.reshape(cont_rows, local_width),
        ],
        axis=0,
    )
    row_sum, row_square = lax.psum(
        (jnp.sum(attended, axis=1), jnp.sum(attended * attended, axis=1)), "tensor"
    )
    sub_center = (row_sum / D)[:, None]
    sub_scale = lax.rsqrt(row_square[:, None] / D - sub_center * sub_center + EPSILON)
    sub_unit = (attended - sub_center) * sub_scale
    sub_gain_f = sub_gain.astype(jnp.float32)
    sub_low = (sub_unit * sub_gain_f + sub_bias.astype(jnp.float32)).astype(jnp.bfloat16)
    branch_part = jnp.dot(sub_low, out_weight, preferred_element_type=jnp.float32)
    mid_gain_f = mid_gain.astype(jnp.float32)
    branch = lax.psum(branch_part.astype(jnp.bfloat16), "tensor").astype(jnp.float32)
    mixed = inputs + (branch + out_bias.astype(jnp.float32))
    mid_normed, mid_unit, mid_scale = norm_rows(mixed, mid_gain_f, mid_bias.astype(jnp.float32))
    mid_low = mid_normed.astype(jnp.bfloat16)
    inner = jnp.dot(mid_low, inner_weight, preferred_element_type=jnp.float32) + inner_bias.astype(
        jnp.float32
    )
    activated = exact_gelu(inner)
    act_sum, act_square = lax.psum(
        (jnp.sum(activated, axis=1), jnp.sum(activated * activated, axis=1)), "tensor"
    )
    ffn_center = (act_sum / FF)[:, None]
    ffn_scale = lax.rsqrt(act_square[:, None] / FF - ffn_center * ffn_center + EPSILON)
    ffn_unit = (activated - ffn_center) * ffn_scale
    ffn_gain_f = ffn_gain.astype(jnp.float32)
    ffn_low = (ffn_unit * ffn_gain_f + ffn_bias.astype(jnp.float32)).astype(jnp.bfloat16)
    outer_part = jnp.dot(ffn_low, outer_weight, preferred_element_type=jnp.float32)
    outer = lax.psum(outer_part.astype(jnp.bfloat16), "tensor").astype(jnp.float32)
    output = (mixed + (outer + outer_bias.astype(jnp.float32))).astype(jnp.bfloat16)
    grad_result = cotangent.astype(jnp.float32)
    outer_bias_grad = jnp.sum(cotangent.astype(jnp.float32), axis=0)
    outer_weight_grad = contract_rows(ffn_low, cotangent)
    grad_ffn = back_project(cotangent, outer_weight)
    ffn_gain_grad = jnp.sum(grad_ffn * ffn_unit, axis=0)
    ffn_bias_grad = jnp.sum(grad_ffn, axis=0)
    ffn_shaped = grad_ffn * ffn_gain_f
    shaped_sum, shaped_cross = lax.psum(
        (jnp.sum(ffn_shaped, axis=1), jnp.sum(ffn_shaped * ffn_unit, axis=1)), "tensor"
    )
    grad_activated = ffn_scale * (
        ffn_shaped - (shaped_sum / FF)[:, None] - ffn_unit * (shaped_cross / FF)[:, None]
    )
    _, gelu_back = jax.vjp(exact_gelu, inner)
    grad_inner = gelu_back(grad_activated)[0].astype(jnp.bfloat16)
    inner_bias_grad = jnp.sum(grad_inner.astype(jnp.float32), axis=0)
    inner_weight_grad = contract_rows(mid_low, grad_inner)
    grad_mid_part = back_project(grad_inner, inner_weight)
    grad_mid = lax.psum(grad_mid_part.astype(jnp.bfloat16), "tensor").astype(jnp.float32)
    mid_gain_grad = jnp.sum(grad_mid * mid_unit, axis=0)
    mid_bias_grad = jnp.sum(grad_mid, axis=0)
    grad_mixed = grad_result + local_norm_back(grad_mid, mid_gain_f, mid_unit, mid_scale)
    grad_branch = grad_mixed.astype(jnp.bfloat16)
    out_bias_grad = jnp.sum(grad_branch.astype(jnp.float32), axis=0)
    out_weight_grad = contract_rows(sub_low, grad_branch)
    grad_sub = back_project(grad_branch, out_weight)
    sub_gain_grad = jnp.sum(grad_sub * sub_unit, axis=0)
    sub_bias_grad = jnp.sum(grad_sub, axis=0)
    sub_shaped = grad_sub * sub_gain_f
    sub_sum, sub_cross = lax.psum(
        (jnp.sum(sub_shaped, axis=1), jnp.sum(sub_shaped * sub_unit, axis=1)), "tensor"
    )
    grad_attended = (
        sub_scale * (sub_shaped - (sub_sum / D)[:, None] - sub_unit * (sub_cross / D)[:, None])
    ).astype(jnp.bfloat16)
    grad_att_prompt, grad_att_cont = heads_view(grad_attended)
    prompt_grad_q, key_acc, value_acc, _, _ = attend_backward(
        query_prompt,
        prompt_keys,
        prompt_values,
        None,
        None,
        own_prompt_at[None],
        prompt_at,
        None,
        tables,
        prompt_log,
        grad_att_prompt,
    )

    def cont_backward(running, pieces):
        block_q, block_k, block_v, block_at, block_log, block_grad = pieces
        grad_q, key_grad, value_grad, own_key_grad, own_value_grad = attend_backward(
            block_q,
            prompt_keys,
            prompt_values,
            block_k,
            block_v,
            block_at,
            prompt_at,
            block_at,
            tables,
            block_log,
            block_grad,
        )
        return (
            (running[0] + key_grad, running[1] + value_grad),
            (
                grad_q.astype(jnp.bfloat16),
                own_key_grad.astype(jnp.bfloat16),
                own_value_grad.astype(jnp.bfloat16),
            ),
        )

    (key_acc, value_acc), (cont_grad_q, cont_grad_k, cont_grad_v) = lax.scan(
        cont_backward,
        (key_acc, value_acc),
        (query_cont, key_cont, value_cont, cont_at, cont_log, grad_att_cont),
    )
    summed = reduce_prompt(
        jnp.stack([key_acc, value_acc]).reshape(2, PROMPT, local_width), device
    ).astype(jnp.bfloat16)
    grad_queries = jnp.concatenate(
        [
            prompt_grad_q.reshape(prompt_rows, local_width).astype(jnp.bfloat16),
            cont_grad_q.reshape(cont_rows, local_width),
        ],
        axis=0,
    )
    grad_query_in = (grad_queries.astype(jnp.float32) * 0.125).astype(jnp.bfloat16)
    grad_keys = jnp.concatenate([summed[0], cont_grad_k.reshape(cont_rows, local_width)], axis=0)
    grad_values = jnp.concatenate([summed[1], cont_grad_v.reshape(cont_rows, local_width)], axis=0)
    query_weight_grad = contract_rows(pre_low, grad_query_in)
    query_bias_grad = jnp.sum(grad_query_in.astype(jnp.float32), axis=0)
    key_weight_grad = contract_rows(pre_low, grad_keys)
    value_weight_grad = contract_rows(pre_low, grad_values)
    value_bias_grad = jnp.sum(grad_values.astype(jnp.float32), axis=0)
    grad_normed_part = (
        back_project(grad_query_in, query_weight)
        + back_project(grad_keys, key_weight)
        + back_project(grad_values, value_weight)
    )
    grad_normed = lax.psum(grad_normed_part.astype(jnp.bfloat16), "tensor").astype(jnp.float32)
    pre_gain_grad = jnp.sum(grad_normed * pre_unit, axis=0)
    pre_bias_grad = jnp.sum(grad_normed, axis=0)
    input_low = (grad_mixed + local_norm_back(grad_normed, pre_gain_f, pre_unit, pre_scale)).astype(
        jnp.bfloat16
    )
    (
        pre_gain_grad,
        pre_bias_grad,
        query_weight_grad,
        query_bias_grad,
        key_weight_grad,
        value_weight_grad,
        value_bias_grad,
        sub_gain_grad,
        sub_bias_grad,
        out_weight_grad,
        out_bias_grad,
        mid_gain_grad,
        mid_bias_grad,
        inner_weight_grad,
        inner_bias_grad,
        ffn_gain_grad,
        ffn_bias_grad,
        outer_weight_grad,
        outer_bias_grad,
    ) = (
        lax.psum_scatter(pre_gain_grad, "dp", scatter_dimension=0, tiled=True),
        lax.psum_scatter(pre_bias_grad, "dp", scatter_dimension=0, tiled=True),
        lax.psum_scatter(query_weight_grad, "dp", scatter_dimension=0, tiled=True),
        lax.psum_scatter(query_bias_grad, "dp", scatter_dimension=0, tiled=True),
        lax.psum_scatter(key_weight_grad, "dp", scatter_dimension=0, tiled=True),
        lax.psum_scatter(value_weight_grad, "dp", scatter_dimension=0, tiled=True),
        lax.psum_scatter(value_bias_grad, "dp", scatter_dimension=0, tiled=True),
        lax.psum_scatter(sub_gain_grad, "dp", scatter_dimension=0, tiled=True),
        lax.psum_scatter(sub_bias_grad, "dp", scatter_dimension=0, tiled=True),
        lax.psum_scatter(out_weight_grad, "dp", scatter_dimension=1, tiled=True),
        lax.psum_scatter(out_bias_grad, "dp", scatter_dimension=0, tiled=True),
        lax.psum_scatter(mid_gain_grad, "dp", scatter_dimension=0, tiled=True),
        lax.psum_scatter(mid_bias_grad, "dp", scatter_dimension=0, tiled=True),
        lax.psum_scatter(inner_weight_grad, "dp", scatter_dimension=0, tiled=True),
        lax.psum_scatter(inner_bias_grad, "dp", scatter_dimension=0, tiled=True),
        lax.psum_scatter(ffn_gain_grad, "dp", scatter_dimension=0, tiled=True),
        lax.psum_scatter(ffn_bias_grad, "dp", scatter_dimension=0, tiled=True),
        lax.psum_scatter(outer_weight_grad, "dp", scatter_dimension=1, tiled=True),
        lax.psum_scatter(outer_bias_grad, "dp", scatter_dimension=0, tiled=True),
    )
    return (
        output,
        input_low,
        pre_gain_grad,
        pre_bias_grad,
        query_weight_grad,
        query_bias_grad,
        key_weight_grad,
        value_weight_grad,
        value_bias_grad,
        sub_gain_grad,
        sub_bias_grad,
        out_weight_grad,
        out_bias_grad,
        mid_gain_grad,
        mid_bias_grad,
        inner_weight_grad,
        inner_bias_grad,
        ffn_gain_grad,
        ffn_bias_grad,
        outer_weight_grad,
        outer_bias_grad,
    )


def solution(mesh):
    placed = (
        P("dp", None),
        P("dp", None),
        P(),
        P(),
        P(),
        P(),
        P(),
        P(),
        P(None, "tensor"),
        P("tensor"),
        P(None, "tensor"),
        P(None, "tensor"),
        P("tensor"),
        P("tensor"),
        P("tensor"),
        P("tensor", None),
        P(),
        P(),
        P(),
        P(None, "tensor"),
        P("tensor"),
        P("tensor"),
        P("tensor"),
        P("tensor", None),
        P(),
    )
    return jax.shard_map(
        body,
        mesh=mesh,
        in_specs=placed,
        out_specs=(
            P("dp", None),
            P("dp", None),
            P("dp"),
            P("dp"),
            P("dp", "tensor"),
            P(("tensor", "dp")),
            P("dp", "tensor"),
            P("dp", "tensor"),
            P(("tensor", "dp")),
            P(("tensor", "dp")),
            P(("tensor", "dp")),
            P("tensor", "dp"),
            P("dp"),
            P("dp"),
            P("dp"),
            P("dp", "tensor"),
            P(("tensor", "dp")),
            P(("tensor", "dp")),
            P(("tensor", "dp")),
            P("tensor", "dp"),
            P("dp"),
        ),
        check_vma=False,
    )
```

profile of v0, /device:TPU:0, one launch (start us, length us, event | category | flops | bytes accessed | tf_op | source)
XLA Modules:
  0.0 1309.5 jit_solution(3789450561895812811)
XLA Ops:
  31.1 3.0 reshape.2942
  36.7 3.0 reshape.2943
  57.4 28.2 %collective-permute-done.1 = bf16[2,1024,384]{2,1,0:T(8,128)(2,1)S(1)} collective-permute-done((bf16[2,1024,384]{2,1,0:T(8,128)(2,1)S(1)}, bf16[2,1024,384]{2,1,0:T(8,128)(2,1)S(1)}, u32[]{:S(2)}, u32[]{:S(2)}) %collective-permute-start.1) | collective-permute-done | bytes 1572896 | tf_op jit(solution)/shard_map/ppermute | solution.py:18
  93.9 147.2 %while.32 = (s32[]{:T(128)}, f32[3,1,256,6,64]{2,0,4,3,1:T(4,128)}, f32[3,1,6,256]{3,2,1,0:T(8,128)}, s32[3,1,256]{2,1,0:T(1,128)S(1)}, s32[6,3]{0,1:T(4,128)S(1...) while((s32[]{:T(128)}, f32[3,1,256,6,64]{2,0,4,3,1:T(4,128)}, ...), condition=%wide.region_9.18_spmd.clone, body=%wide.region_4.17_spmd.clone.sunk | while | flops 992287104 | bytes 126571680 | solution.py:322
  119.1 11.7 fusion.427
  136.2 5.9 fusion.431
  143.8 9.5 dynamic_update_slice.33
  162.8 11.7 fusion.427
  179.9 5.9 fusion.431
  187.5 9.5 dynamic_update_slice.33
  206.5 11.7 fusion.427
  223.6 5.9 fusion.431
  231.2 9.5 dynamic_update_slice.33
  243.7 26.3 %fusion.327 = (f32[6,512]{1,0:T(8,128)S(1)}, f32[1,6,512,2048]{2,3,1,0:T(8,128)S(1)}) fusion(bf16[2048,6,64]{0,2,1:T(8,128)(2,1)} %get-tuple-element.1154, bf16[512,6,64]{0,2,1:T(8,128)(2,1)} %bitcast.984, pred[6,2048]{1,0:T(8,128)(4,1)} %get-tuple-element.609, pred[6,512]{1,0:T(8,128)(4,1)} %get-tuple-element.617, s32[6,2048]{1,0:T(8,128)} %get-tuple-element.600, ...), kind=kOutput, calls=%fused_computation.664 | convolution fusion | flops 931132416 | bytes 28423168 | tf_op jit(solution)/shard_map/brhe,khe->bhrk/dot_general | solution.py:79
  270.0 3.8 exponential_reduce_fusion.2
  273.8 5.1 copy-done.3
  278.9 10.2 fusion.248
  290.9 9.7 all-reduce.17
  301.9 3.9 convolution_convert_fusion.4
  313.7 52.8 %all-reduce.23.cloned.1.call-done = bf16[1280,768]{1,0:T(8,128)(2,1)} async-done(((bf16[1280,768]{1,0:T(8,128)(2,1)}), bf16[1280,768]{1,0:T(8,128)(2,1)}) %all-reduce.23.cloned.1.call-update) | async-done | bytes 1966096 | tf_op jit(solution)/shard_map/psum | solution.py:340
  366.5 3.3 fusion.257
  369.8 24.6 %fusion.322 = (f32[1280]{0:T(1024)}, f32[1280]{0:T(1024)}, f32[1280,1536]{1,0:T(8,128)}, f32[1280,1536]{1,0:T(8,128)}, f32[1280,1536]{1,0:T(8,128)}) fusion(f32[1536]{0:T(1024)S(1)} %copy-done.97, bf16[768,1536]{1,0:T(8,128)(2,1)S(1)} %copy-done, f32[768]{0:T(1024)S(1)} %copy-done.98, f32[768]{0:T(1024)S(1)} %copy-done.81, ...), kind=kOutput, calls=%fused_computation.660 | convolution fusion | flops 3162437120 | bytes 29920256 | tf_op jit(solution)/shard_map/dot_general | solution.py:344
  394.4 8.4 all-reduce.16
  403.6 10.0 multiply_reduce_fusion.1
  413.6 9.5 all-reduce.15
  424.6 15.7 %convert_reduce_fusion = (f32[1536]{0:T(1024)}, bf16[1280,1536]{1,0:T(8,128)(2,1)S(1)}, bf16[1280,1536]{1,0:T(8,128)(2,1)}) fusion(f32[1280,1536]{1,0:T(8,128)} %get-tuple-element.485, f32[1280,1536]{1,0:T(8,128)} %get-tuple-element.644, f32[1280]{0:T(1024)S(1)} %broadcast_multiply_fusion, f32[1280,1536]{1,0:T(8,128)} %get-tuple-element.484, ...), kind=kLoop, calls=%fused_computation.408 | loop fusion | flops 51116544 | bytes 39360512 | tf_op jit(solution)/shard_map/reduce_sum | solution.py:374
  442.1 4.4 convolution_convert_fusion.2
  446.6 60.1 %all-reduce.25.cloned.1.call-done = bf16[1280,768]{1,0:T(8,128)(2,1)} async-done(((bf16[1280,768]{1,0:T(8,128)(2,1)}), bf16[1280,768]{1,0:T(8,128)(2,1)}) %all-reduce.25.cloned.1.call-update) | async-done | bytes 1966096 | tf_op jit(solution)/shard_map/psum | solution.py:377
  506.8 5.0 fusion.237
  511.9 3.3 convert_reduce_fusion.5
  515.2 3.2 multiply_reduce_fusion.6
  518.3 6.9 all-reduce.14
  528.3 12.0 fusion.252
  540.3 15.5 %fusion.211 = (f32[6,512]{1,0:T(8,128)S(1)}, f32[6,2048,512]{2,1,0:T(8,128)}) fusion(f32[1,6,512,2048]{2,3,1,0:T(8,128)} %copy-done.3, f32[6,512]{1,0:T(8,128)S(1)} %log_add_fusion.1, bf16[2048,6,64]{0,2,1:T(8,128)(2,1)S(1)} %copy-done.6, bf16[512,6,64]{0,2,1:T(8,128)(2,1)S(1)} %bitcast.962), kind=kOutput, calls=%fused_computation.395 | convolution fusion | flops 824177664 | bytes 52322304 | tf_op jit(solution)/shard_map/brhe,khe->bhrk/dot_general | solution.py:138
  558.1 21.2 %fusion.216 = bf16[6,512,2048]{1,2,0:T(8,128)(2,1)} fusion(f32[6,2048,512]{2,1,0:T(8,128)} %get-tuple-element.648, f32[1,6,512,2048]{2,3,1,0:T(8,128)} %copy-done.3, f32[6,512]{1,0:T(8,128)S(1)} %get-tuple-element.647, f32[6,512]{1,0:T(8,128)S(1)} %log_add_fusion.1), kind=kLoop, calls=%fused_computation.403 | loop fusion | flops 25165824 | bytes 62939136 | tf_op jit(solution)/shard_map/reshape.237
  579.3 10.2 convolution_bitcast_fusion.3
  589.4 152.3 %while.33 = (s32[]{:T(128)}, f32[2048,6,64]{0,2,1:T(8,128)}, f32[2048,6,64]{0,2,1:T(8,128)}, bf16[3,1,256,6,64]{2,4,3,1,0:T(8,128)(2,1)}, bf16[3,1,256,6,64]{2,4...) while((s32[]{:T(128)}, f32[2048,6,64]{0,2,1:T(8,128)}, ...), condition=%wide.region_37.46_spmd.clone, body=%wide.region_34.45_spmd.clone.sunk | while | flops 2360187392 | bytes 185529552 | solution.py:433
  599.3 2.8 multiply_reduce_fusion.11
  605.0 16.2 %fusion.456 = (f32[6,256]{1,0:T(8,128)S(1)}, f32[1,6,256,2048]{3,2,1,0:T(8,128)}) fusion(f32[6,256,2048]{2,1,0:T(8,128)S(1)} %fusion.450, f32[6,256]{1,0:T(8,128)S(1)} %dynamic-slice_bitcast_fusion.2, bf16[2048,6,64]{0,2,1:T(8,128)(2,1)S(1)} %copy-done.19, bf16[3,1,256,6,64]{2,4,3,1,0:T(8,128)(2,1)S(1)} %get-tuple-element.1128, s32[]{:T(128)S(6)} %copy.192, ...), kind=kOutput, calls=%fused_computation.185.clone.1 | convolution fusion | flops 471857664 | bytes 27750404 | tf_op jit(solution)/shard_map/while/body/eval_jaxpr/brhe,khe->bhrk/dot_general | solution.py:79
  621.3 5.6 fusion.460
  626.9 6.0 bitcast_add_fusion.8
  655.6 16.2 %fusion.456 = (f32[6,256]{1,0:T(8,128)S(1)}, f32[1,6,256,2048]{3,2,1,0:T(8,128)}) fusion(f32[6,256,2048]{2,1,0:T(8,128)S(1)} %fusion.450, f32[6,256]{1,0:T(8,128)S(1)} %dynamic-slice_bitcast_fusion.2, bf16[2048,6,64]{0,2,1:T(8,128)(2,1)S(1)} %copy-done.19, bf16[3,1,256,6,64]{2,4,3,1,0:T(8,128)(2,1)S(1)} %get-tuple-element.1128, s32[]{:T(128)S(6)} %copy.192, ...), kind=kOutput, calls=%fused_computation.185.clone.1 | convolution fusion | flops 471857664 | bytes 27750404 | tf_op jit(solution)/shard_map/while/body/eval_jaxpr/brhe,khe->bhrk/dot_general | solution.py:79
  671.8 5.6 fusion.460
  677.4 6.0 bitcast_add_fusion.8
  706.1 16.2 %fusion.456 = (f32[6,256]{1,0:T(8,128)S(1)}, f32[1,6,256,2048]{3,2,1,0:T(8,128)}) fusion(f32[6,256,2048]{2,1,0:T(8,128)S(1)} %fusion.450, f32[6,256]{1,0:T(8,128)S(1)} %dynamic-slice_bitcast_fusion.2, bf16[2048,6,64]{0,2,1:T(8,128)(2,1)S(1)} %copy-done.19, bf16[3,1,256,6,64]{2,4,3,1,0:T(8,128)(2,1)S(1)} %get-tuple-element.1128, s32[]{:T(128)S(6)} %copy.192, ...), kind=kOutput, calls=%fused_computation.185.clone.1 | convolution fusion | flops 471857664 | bytes 27750404 | tf_op jit(solution)/shard_map/while/body/eval_jaxpr/brhe,khe->bhrk/dot_general | solution.py:79
  722.4 5.6 fusion.460
  728.0 6.0 bitcast_add_fusion.8
  741.7 4.5 select_convert_fusion
  747.9 7.5 convolution_convert_fusion.3
  758.6 22.4 %collective-permute-done.2 = bf16[2,1024,384]{1,2,0:T(8,128)(2,1)} collective-permute-done((bf16[2,1024,384]{1,2,0:T(8,128)(2,1)}, bf16[2,1024,384]{1,2,0:T(8,128)(2,1)}, u32[]{:S(2)}, u32[]{:S(2)}) %collective-permute-start.2) | collective-permute-done | bytes 1572896 | tf_op jit(solution)/shard_map/ppermute | solution.py:18
  792.7 4.5 fusion.311
  797.3 4.3 fusion.279
  803.9 4.2 fusion.258
  808.2 8.6 fusion.321
  817.1 8.2 fusion.328
  832.0 64.6 %all-reduce.27.cloned.1.call-done = (bf16[1280,768]{1,0:T(8,128)(2,1)}, bf16[1280,768]{1,0:T(8,128)(2,1)}) async-done(((bf16[1280,768]{1,0:T(8,128)(2,1)}, bf16[1280,768]{1,0:T(8,128)(2,1)}), (bf16[1280,768]{1,0:T(8,128)(2,1)}, bf16[1280,768]{1,0:T(8,128)(2,1)})) %all-reduce.27.cloned.1.call-update) | async-done | bytes 3932176 | tf_op jit(solution)/shard_map/psum | solution.py:357
  896.5 3.3 fusion.238
  900.0 61.5 %all-reduce.13 = (f32[768]{0:T(1024)S(1)}, f32[768]{0:T(1024)S(1)}, f32[384]{0:T(512)S(1)}, f32[384]{0:T(512)S(1)}, f32[384]{0:T(512)S(1)}, /*index=5*/f32[384]{...) all-reduce(f32[768]{0:T(1024)S(1)} %get-tuple-element.375, ...), channel_id=2, replica_groups=mesh['dp'=16,'tensor'=2] {'dp'}, use_global_device_ids=true, to_apply=%region_42.51.clone | all-reduce | flops 10752 | bytes 86016
  969.1 7.1 fusion.232
  976.2 44.5 %reduce-scatter.7.cloned.1.call-done = f32[48,384]{1,0:T(8,128)} async-done(((f32[768,384]{1,0:T(8,128)}), f32[48,384]{1,0:T(8,128)}) %reduce-scatter.7.cloned.1.call-update) | async-done | bytes 73744 | tf_op jit(solution)/shard_map/reduce_scatter | solution.py:490
  1020.7 61.6 %reduce-scatter.11.cloned.1.call-done = f32[48,384]{1,0:T(8,128)} async-done(((f32[768,384]{1,0:T(8,128)}), f32[48,384]{1,0:T(8,128)}) %reduce-scatter.11.cloned.1.call-update) | async-done | bytes 73744 | tf_op jit(solution)/shard_map/reduce_scatter | solution.py:493
  1082.2 61.7 %reduce-scatter.9.cloned.1.call-done = f32[48,384]{1,0:T(8,128)} async-done(((f32[768,384]{1,0:T(8,128)}), f32[48,384]{1,0:T(8,128)}) %reduce-scatter.9.cloned.1.call-update) | async-done | bytes 73744 | tf_op jit(solution)/shard_map/reduce_scatter | solution.py:492
  1144.0 79.6 %reduce-scatter.15.cloned.1.call-done = f32[48,1536]{1,0:T(8,128)} async-done(((f32[768,1536]{1,0:T(8,128)}), f32[48,1536]{1,0:T(8,128)}) %reduce-scatter.15.cloned.1.call-update) | async-done | bytes 294928 | tf_op jit(solution)/shard_map/reduce_scatter | solution.py:501
  1223.6 79.1 %reduce-scatter.17.cloned.1.call-done = f32[1536,48]{0,1:T(8,128)} async-done(((f32[1536,768]{0,1:T(8,128)}), f32[1536,48]{0,1:T(8,128)}) %reduce-scatter.17.cloned.1.call-update) | async-done | bytes 294928 | tf_op jit(solution)/shard_map/reduce_scatter | solution.py:505
  (556 shorter events, 219.7 us)
Async XLA Ops:
  7.2 362.6 %copy-start = (bf16[768,1536]{1,0:T(8,128)(2,1)S(1)}, bf16[768,1536]{1,0:T(8,128)(2,1)}, u32[]{:S(2)}) copy-start(bf16[768,1536]{1,0:T(8,128)(2,1)} %param.64) | copy-start | bytes 7077892
  7.2 6.8 copy-start.51
  7.2 359.2 %all-reduce.23.cloned.1.call-start = ((), (), s32[]{:S(2)}) async-start(), calls=%async_computation.6 | async-start | bytes 3932160 | tf_op jit(solution)/shard_map/psum | solution.py:340
  8.8 6.5 copy-start.78
  15.6 6.2 copy-start.55
  18.8 27.2 %collective-permute-start = (bf16[2,512,384]{2,1,0:T(8,128)(2,1)}, bf16[2,512,384]{2,1,0:T(8,128)(2,1)}, u32[]{:S(2)}, u32[]{:S(2)}) collective-permute-start(bf16[2,512,384]{2,1,0:T(8,128)(2,1)} %pad_maximum_fusion.4), channel_id=1, source_target_pairs={{0,2},{2,0},{4,6},{6,4},{8,10},{10,8},{12,14},{14,12},{16,18},{18,... | collective-permute-start | bytes 2359304 | tf_op jit(solution)/shard_map/ppermute | solution.py:18
  48.1 37.6 %collective-permute-start.1 = (bf16[2,1024,384]{2,1,0:T(8,128)(2,1)S(1)}, bf16[2,1024,384]{2,1,0:T(8,128)(2,1)S(1)}, u32[]{:S(2)}, u32[]{:S(2)}) collective-permute-start(bf16[2,1024,384]{2,1,0:T(8,128)(2,1)S(1)} %maximum_select_fusion.1), channel_id=1, source_target_pairs={{0,4},{2,6},{4,0},{6,2},{8,12},{10,14},{12,8},{14,10},{16,20},{18,... | collective-permute-start | bytes 4718600 | tf_op jit(solution)/shard_map/ppermute | solution.py:18
  93.9 149.8 %copy-start.90 = (s32[6,512]{1,0:T(8,128)S(1)}, s32[6,512]{1,0:T(8,128)}, u32[]{:S(2)}) copy-start(s32[6,512]{1,0:T(8,128)} %get-tuple-element.612) | copy-start | bytes 36868
  119.1 11.7 copy-start.13
  162.8 11.7 copy-start.13
  206.5 11.7 copy-start.13
  243.6 281.6 %copy-start.24 = (f32[48,8,3,256]{3,1,2,0:T(8,128)}, f32[48,8,3,256]{3,1,2,0:T(8,128)S(1)}, u32[]{:S(2)}) copy-start(f32[48,8,3,256]{3,1,2,0:T(8,128)S(1)} %copy.164) | copy-start | bytes 3538948
  270.0 8.9 copy-start.3
  270.0 8.9 copy-start.5
  305.9 200.8 %all-reduce.25.cloned.1.call-start = ((), (), s32[]{:S(2)}) async-start(), calls=%async_computation.7 | async-start | bytes 3932160 | tf_op jit(solution)/shard_map/psum | solution.py:377
  369.8 24.7 %copy-start.73 = (f32[1280]{0:T(1024)}, f32[1280]{0:T(1024)S(1)}, u32[]{:S(2)}) copy-start(f32[1280]{0:T(1024)S(1)} %get-tuple-element.603) | copy-start | bytes 15364
  369.8 24.7 %copy-start.76 = (f32[1280]{0:T(1024)}, f32[1280]{0:T(1024)S(1)}, u32[]{:S(2)}) copy-start(f32[1280]{0:T(1024)S(1)} %get-tuple-element.604) | copy-start | bytes 15364
  403.6 10.0 copy-start.85
  403.6 10.0 copy-start.86
  446.5 65.2 %copy-start.16 = (bf16[1280,768]{1,0:T(8,128)(2,1)S(1)}, bf16[1280,768]{1,0:T(8,128)(2,1)}, u32[]{:S(2)}) copy-start(bf16[1280,768]{1,0:T(8,128)(2,1)} %param.45) | copy-start | bytes 5898244
  446.5 65.2 %copy-start.64 = (f32[768]{0:T(1024)S(1)}, f32[768]{0:T(1024)}, u32[]{:S(2)}) copy-start(f32[768]{0:T(1024)} %convert_element_type.380) | copy-start | bytes 9220
  446.5 65.2 %copy-start.74 = (f32[1280]{0:T(1024)S(1)}, f32[1280]{0:T(1024)}, u32[]{:S(2)}) copy-start(f32[1280]{0:T(1024)} %copy-done.73) | copy-start | bytes 15364
  446.5 65.3 %copy-start.77 = (f32[1280]{0:T(1024)S(1)}, f32[1280]{0:T(1024)}, u32[]{:S(2)}) copy-start(f32[1280]{0:T(1024)} %copy-done.76) | copy-start | bytes 15364
  446.5 65.3 %copy-start.82 = (f32[768]{0:T(1024)S(1)}, f32[768]{0:T(1024)}, u32[]{:S(2)}) copy-start(f32[768]{0:T(1024)} %convert_element_type.381) | copy-start | bytes 9220
  446.6 450.0 %all-reduce.27.cloned.1.call-start = ((), (), s32[]{:S(2)}) async-start(), calls=%async_computation.14 | async-start | bytes 7864320 | tf_op jit(solution)/shard_map/psum | solution.py:357
  515.2 10.1 copy-start.28
  528.3 12.0 copy-start.6
  540.3 15.5 %slice-start.3 = ((bf16[1280,384]{0,1:T(8,128)(2,1)}), bf16[768,384]{0,1:T(8,128)(2,1)S(1)}, s32[]{:S(2)}) async-start(bf16[1280,384]{0,1:T(8,128)(2,1)} %copy-done.33), calls=%async_computation.18 | async-start | bytes 1179648 | tf_op jit(solution)/shard_map/slice | solution.py:270
  558.1 21.2 %copy-start.44 = (bf16[512,384]{0,1:T(8,128)(2,1)S(1)}, bf16[512,384]{0,1:T(8,128)(2,1)}, u32[]{:S(2)}) copy-start(bf16[512,384]{0,1:T(8,128)(2,1)} %slice.176) | copy-start | bytes 1179652
  579.3 10.2 copy-start.31
  579.3 10.2 copy-start.38
  579.3 10.2 copy-start.46
  746.2 34.8 %collective-permute-start.2 = (bf16[2,1024,384]{1,2,0:T(8,128)(2,1)}, bf16[2,1024,384]{1,2,0:T(8,128)(2,1)}, u32[]{:S(2)}, u32[]{:S(2)}) collective-permute-start(bf16[2,1024,384]{1,2,0:T(8,128)(2,1)} %select_convert_fusion), channel_id=1, source_target_pairs={{0,4},{2,6},{4,0},{6,2},{8,12},{10,14},{12,8},{14,10},{16,20},{18,... | collective-permute-start | bytes 4718600 | tf_op jit(solution)/shard_map/ppermute | solution.py:18
  747.9 9.3 copy-start.58
  747.9 36.0 %slice-start = ((s8[12582912]{0:T(1024)(128)(4,1)}), s8[4194304]{0:T(1024)(128)(4,1)S(1)}, s32[]{:S(2)}) async-start(s8[12582912]{0:T(1024)(128)(4,1)} %bitcast.940), calls=%async_computation.15 | async-start | bytes 8388608
  747.9 36.0 %slice-start.1 = ((s8[12582912]{0:T(1024)(128)(4,1)}), s8[4194304]{0:T(1024)(128)(4,1)S(1)}, s32[]{:S(2)}) async-start(s8[12582912]{0:T(1024)(128)(4,1)} %bitcast.940), calls=%async_computation.16 | async-start | bytes 8388608
  755.4 25.6 %copy-start.9 = (f32[2048,6,64]{0,2,1:T(8,128)S(1)}, f32[2048,6,64]{0,2,1:T(8,128)}, u32[]{:S(2)}) copy-start(f32[2048,6,64]{0,2,1:T(8,128)} %get-tuple-element.196) | copy-start | bytes 9437188
  755.4 25.6 %copy-start.12 = (f32[2048,6,64]{0,2,1:T(8,128)S(1)}, f32[2048,6,64]{0,2,1:T(8,128)}, u32[]{:S(2)}) copy-start(f32[2048,6,64]{0,2,1:T(8,128)} %get-tuple-element.197) | copy-start | bytes 9437188
  757.9 26.0 %slice-start.2 = ((s8[12582912]{0:T(1024)(128)(4,1)}), s8[4194304]{0:T(1024)(128)(4,1)S(1)}, s32[]{:S(2)}) async-start(s8[12582912]{0:T(1024)(128)(4,1)} %bitcast.940), calls=%async_computation.17 | async-start | bytes 8388608
  758.5 29.4 %copy-start.39 = (bf16[48,8,3,256]{3,1,2,0:T(8,128)(2,1)}, bf16[48,8,3,256]{3,1,2,0:T(8,128)(2,1)S(1)}, u32[]{:S(2)}) copy-start(bf16[48,8,3,256]{3,1,2,0:T(8,128)(2,1)S(1)} %copy.166) | copy-start | bytes 1769476
  758.6 25.3 %copy-start.20 = (bf16[2048,6,64]{0,2,1:T(8,128)(2,1)S(1)}, bf16[2048,6,64]{0,2,1:T(8,128)(2,1)}, u32[]{:S(2)}) copy-start(bf16[2048,6,64]{0,2,1:T(8,128)(2,1)} %get-tuple-element.1155) | copy-start | bytes 4718596
  783.8 3.6 collective-permute-start.3
  792.4 183.8 %reduce-scatter.13.cloned.1.call-start = ((), (), s32[]{:S(2)}) async-start(), calls=%async_computation.11 | async-start | bytes 1253376 | tf_op jit(solution)/shard_map/reduce_scatter | solution.py:497
  797.2 223.5 %reduce-scatter.7.cloned.1.call-start = ((), (), s32[]{:S(2)}) async-start(), calls=%async_computation.8 | async-start | bytes 1253376 | tf_op jit(solution)/shard_map/reduce_scatter | solution.py:490
  801.6 280.7 %reduce-scatter.11.cloned.1.call-start = ((), (), s32[]{:S(2)}) async-start(), calls=%async_computation.10 | async-start | bytes 1253376 | tf_op jit(solution)/shard_map/reduce_scatter | solution.py:493
  803.9 340.1 %reduce-scatter.9.cloned.1.call-start = ((), (), s32[]{:S(2)}) async-start(), calls=%async_computation.9 | async-start | bytes 1253376 | tf_op jit(solution)/shard_map/reduce_scatter | solution.py:492
  808.1 415.5 %reduce-scatter.15.cloned.1.call-start = ((), (), s32[]{:S(2)}) async-start(), calls=%async_computation.12 | async-start | bytes 5013504 | tf_op jit(solution)/shard_map/reduce_scatter | solution.py:501
  816.8 485.9 %reduce-scatter.17.cloned.1.call-start = ((), (), s32[]{:S(2)}) async-start(), calls=%async_computation.13 | async-start | bytes 5013504 | tf_op jit(solution)/shard_map/reduce_scatter | solution.py:505
  825.3 71.2 %copy-start.60 = (f32[1280]{0:T(1024)S(1)}, f32[1280]{0:T(1024)}, u32[]{:S(2)}) copy-start(f32[1280]{0:T(1024)} %copy-done.59) | copy-start | bytes 15364
  825.3 71.2 %copy-start.62 = (f32[1280]{0:T(1024)S(1)}, f32[1280]{0:T(1024)}, u32[]{:S(2)}) copy-start(f32[1280]{0:T(1024)} %copy-done.61) | copy-start | bytes 15364
  831.7 68.2 %copy-start.84 = (f32[1536]{0:T(1024)S(1)}, f32[1536]{0:T(1024)}, u32[]{:S(2)}) copy-start(f32[1536]{0:T(1024)} %get-tuple-element.480) | copy-start | bytes 18436
  831.7 68.2 %copy-start.88 = (f32[768]{0:T(1024)S(1)}, f32[768]{0:T(1024)}, u32[]{:S(2)}) copy-start(f32[768]{0:T(1024)} %get-tuple-element.482) | copy-start | bytes 9220
  831.7 68.2 %copy-start.89 = (f32[768]{0:T(1024)S(1)}, f32[768]{0:T(1024)}, u32[]{:S(2)}) copy-start(f32[768]{0:T(1024)} %get-tuple-element.593) | copy-start | bytes 9220
  831.7 68.2 %copy-start.91 = (f32[768]{0:T(1024)S(1)}, f32[768]{0:T(1024)}, u32[]{:S(2)}) copy-start(f32[768]{0:T(1024)} %get-tuple-element.371) | copy-start | bytes 9220
  831.7 68.2 %copy-start.92 = (f32[768]{0:T(1024)S(1)}, f32[768]{0:T(1024)}, u32[]{:S(2)}) copy-start(f32[768]{0:T(1024)} %get-tuple-element.382) | copy-start | bytes 9220
  831.7 68.2 %copy-start.94 = (f32[384]{0:T(512)S(1)}, f32[384]{0:T(512)}, u32[]{:S(2)}) copy-start(f32[384]{0:T(512)} %convert_reduce_fusion.7) | copy-start | bytes 4612
  831.7 68.2 %copy-start.95 = (f32[1536]{0:T(1024)S(1)}, f32[1536]{0:T(1024)}, u32[]{:S(2)}) copy-start(f32[1536]{0:T(1024)} %get-tuple-element.365) | copy-start | bytes 18436
  831.7 68.2 %copy-start.96 = (f32[1536]{0:T(1024)S(1)}, f32[1536]{0:T(1024)}, u32[]{:S(2)}) copy-start(f32[1536]{0:T(1024)} %get-tuple-element.368) | copy-start | bytes 18436
  831.7 68.2 %copy-start.101 = (f32[384]{0:T(512)S(1)}, f32[384]{0:T(512)}, u32[]{:S(2)}) copy-start(f32[384]{0:T(512)} %get-tuple-element.373) | copy-start | bytes 4612
  831.7 68.2 %copy-start.102 = (f32[384]{0:T(512)S(1)}, f32[384]{0:T(512)}, u32[]{:S(2)}) copy-start(f32[384]{0:T(512)} %get-tuple-element.383) | copy-start | bytes 4612
  831.7 137.4 %copy-start.66 = (f32[768]{0:T(1024)S(1)}, f32[768]{0:T(1024)}, u32[]{:S(2)}) copy-start(f32[768]{0:T(1024)} %convert_element_type.380) | copy-start | bytes 9220
  831.7 137.3 %copy-start.79 = (f32[768]{0:T(1024)S(1)}, f32[768]{0:T(1024)}, u32[]{:S(2)}) copy-start(f32[768]{0:T(1024)} %copy-done.78) | copy-start | bytes 9220
  831.8 137.3 %copy-start.93 = (f32[768]{0:T(1024)S(1)}, f32[768]{0:T(1024)}, u32[]{:S(2)}) copy-start(f32[768]{0:T(1024)} %convert_element_type.390) | copy-start | bytes 9220
  969.1 333.6 %copy-start.1 = (bf16[768,1536]{1,0:T(8,128)(2,1)S(1)}, bf16[768,1536]{1,0:T(8,128)(2,1)}, u32[]{:S(2)}) copy-start(bf16[768,1536]{1,0:T(8,128)(2,1)} %param.64) | copy-start | bytes 7077892
  (81 other events, 266.0 us)
Sparse Core Ops, SparseCore 0:
  306.0 60.3 all-reduce.22
  446.7 60.0 all-reduce.24
  792.5 103.9 all-reduce.26
  901.0 57.9 reduce-scatter.12
  963.5 57.0 reduce-scatter.6
  1025.2 57.0 reduce-scatter.10
  1086.9 57.0 reduce-scatter.8
  1148.9 74.6 reduce-scatter.14
  1228.1 74.5 reduce-scatter.16
where the time goes:
time: 1310 us
  waiting for transfers between devices  555 us (42%)
  matrix products  344 us (26%)
  other arithmetic  178 us (14%)
  blocking collectives  96.1 us (7%)
  local copies, waits for them, and re-layouts  94.9 us (7%)
  between operations  18.1 us (1%)
  loops' own time  17.6 us (1%)
    dot_general x7, matrix products, block_logits(): jnp.einsum('brhe,khe->bhrk', queries, prompt_keys, preferred_element_type...  110 us
    reduce_scatter x1, waiting for transfers between devices, body(): lax.psum_scatter(inner_weight_grad, 'dp', scatter_dimension=0, tiled=True)  79.6 us
    reduce_scatter x1, waiting for transfers between devices, body(): lax.psum_scatter(outer_weight_grad, 'dp', scatter_dimension=1, tiled=True)  79.1 us
    psum x1, waiting for transfers between devices, body(): lax.psum(outer_part.astype(jnp.bfloat16), 'tensor').astype(jnp.float32)  64.6 us
    reduce_scatter x1, waiting for transfers between devices, body(): lax.psum_scatter(key_weight_grad, 'dp', scatter_dimension=0, tiled=True)  61.7 us
    reduce_scatter x1, waiting for transfers between devices, body(): lax.psum_scatter(value_weight_grad, 'dp', scatter_dimension=0, tiled=True)  61.6 us
    unnamed x1, blocking collectives  61.5 us
    psum x1, waiting for transfers between devices, body(): lax.psum(grad_mid_part.astype(jnp.bfloat16), 'tensor').astype(jnp.float32)  60.1 us
  transfers between devices with their start and end apart: 13, of which 10 were waited for; matrix products, arithmetic and copies ran while one was open for 8% of the time, Pallas kernels for 0%

commit v1 on v0

v1 whole, which is shorter than its diff:
```python
import jax
import jax.numpy as jnp
from jax import lax
from jax.experimental import pallas as pl
from jax.experimental.pallas import tpu as pltpu
from jax.sharding import PartitionSpec as P

HD = 64
PROMPT = 2048
CONT = 256
GDEV = 4
TILE = 256
CHUNK = PROMPT // GDEV
PTILES = CHUNK // TILE
LOG2E = 1.4426950408889634
BF = jnp.bfloat16
F32 = jnp.float32
TAB = 10


def dot_nt(a, b):
    return lax.dot_general(a, b, (((1,), (1,)), ((), ())), preferred_element_type=F32)


def dot_nn(a, b):
    return lax.dot_general(a, b, (((1,), (0,)), ((), ())), preferred_element_type=F32)


def low_half(rows):
    return lax.broadcasted_iota(jnp.int32, (rows, 128), 1) < HD


def codes(at, tab, pair, miss):
    def cell(i):
        return tab[pair * TAB + i]

    first = jnp.floor((at + 0.5) * cell(0))
    second = jnp.floor((at + 0.5) * cell(1))
    rest1 = at - cell(2) * jnp.floor((at + 0.5) * cell(3))
    rest2 = at - cell(4) * jnp.floor((at + 0.5) * cell(5))
    return [
        first,
        jnp.where(rest1 == cell(6), second, miss),
        jnp.where(rest1 == cell(7), second, miss),
        jnp.where(rest2 == cell(8), 1.0, 0.0),
        jnp.where(rest2 == cell(9), 1.0, 0.0),
    ]


def fwd_kernel(info, tab, q_ref, kp_ref, vp_ref, ko_ref, vo_ref, o_ref, e_ref, li_ref, t_s, kc_s):
    pair = pl.program_id(0)
    step = pl.program_id(1)
    member = info[0]
    low = low_half(TILE)
    q = q_ref[...]
    zero = jnp.zeros_like(q)
    qs = [jnp.where(low, q, zero), jnp.where(low, zero, q)]
    row = lax.broadcasted_iota(jnp.int32, (TILE, 128), 0).astype(F32)
    at_q = info[2 + step].astype(F32) + row
    qc = codes(at_q, tab, pair, -2.0)

    @pl.when(step == 0)
    def _():
        at_k = info[1].astype(F32) + lax.broadcasted_iota(jnp.int32, (8, PROMPT), 1).astype(F32)
        for i, c in enumerate(codes(at_k, tab, pair, -1.0)):
            kc_s[i] = c

    def logits(mx, keys, kc, causal, at, width):
        out = []
        for h in range(2):
            s = dot_nt(qs[h], keys)
            top = mx[h]
            for g in range(width // 128):
                lanes = slice(g * 128, (g + 1) * 128)
                w = jnp.where(qc[0] == kc[0][:, lanes], 1.0, 0.0)
                w = w + jnp.where(qc[1 + h] == kc[1 + h][:, lanes], 1.0, 0.0)
                w = w + qc[3 + h] * kc[3 + h][:, lanes]
                if causal is not None:
                    w = jnp.where(causal[:, lanes], w, 0.0)
                t = s[:, lanes] * LOG2E + jnp.log2(w)
                t_s[h, :, pl.ds(at + g * 128, 128)] = t
                top = jnp.maximum(top, t)
            out.append(top)
        return tuple(out)

    def weigh(carry, vals, m, at, width):
        sums, accs = carry
        ns, na = [], []
        for h in range(2):
            total = sums[h]
            parts = []
            for g in range(width // 128):
                e = jnp.exp2(t_s[h, :, pl.ds(at + g * 128, 128)] - m[h])
                total = total + e
                parts.append(e.astype(BF))
            el = jnp.concatenate(parts, axis=1)
            e_ref[h, :, pl.ds(at, width)] = el
            ns.append(total)
            na.append(accs[h] + dot_nn(el, vals))
        return (tuple(ns), tuple(na))

    def finish(carry):
        sums, accs = carry
        li = [1.0 / jnp.sum(s, axis=1, keepdims=True) for s in sums]
        lfull = jnp.where(low, li[0], li[1])
        li_ref[...] = lfull
        o_ref[...] = (jnp.where(low, accs[0], accs[1]) * lfull).astype(BF)

    def tops(mx):
        return [jnp.broadcast_to(jnp.max(x, axis=1, keepdims=True), (TILE, 128)) for x in mx]

    neg = jnp.full((TILE, 128), -jnp.inf, F32)
    zf = jnp.zeros((TILE, 128), F32)

    def key_codes(at, width):
        return [kc_s[i, 0:1, pl.ds(at, width)] for i in range(5)]

    @pl.when(step < PTILES)
    def _():
        def one(j, mx):
            at = pl.multiple_of(j * CHUNK, CHUNK)
            held = pl.multiple_of((j ^ member) * CHUNK, CHUNK)
            return logits(mx, kp_ref[pl.ds(held, CHUNK), :], key_codes(at, CHUNK), None, held, CHUNK)

        mx = lax.fori_loop(0, member, one, (neg, neg))
        at = pl.multiple_of(member * CHUNK, CHUNK)
        rows = lax.broadcasted_iota(jnp.int32, (TILE, CHUNK), 0) + step * TILE
        cols = lax.broadcasted_iota(jnp.int32, (TILE, CHUNK), 1)
        mx = logits(mx, kp_ref[0:CHUNK, :], key_codes(at, CHUNK), cols <= rows, 0, CHUNK)
        m = tops(mx)

        def two(j, carry):
            held = pl.multiple_of((j ^ member) * CHUNK, CHUNK)
            return weigh(carry, vp_ref[pl.ds(held, CHUNK), :], m, held, CHUNK)

        finish(lax.fori_loop(0, member + 1, two, ((zf, zf), (zf, zf))))

    @pl.when(step >= PTILES)
    def _():
        mx = (neg, neg)
        for j in range(GDEV):
            at = pl.multiple_of((j ^ member) * CHUNK, CHUNK)
            mx = logits(mx, kp_ref[j * CHUNK : (j + 1) * CHUNK, :], key_codes(at, CHUNK), None, j * CHUNK, CHUNK)
        rows = lax.broadcasted_iota(jnp.int32, (TILE, CONT), 0)
        cols = lax.broadcasted_iota(jnp.int32, (TILE, CONT), 1)
        at_k = info[2 + step].astype(F32) + lax.broadcasted_iota(jnp.int32, (8, CONT), 1).astype(F32)
        own = [c[0:1] for c in codes(at_k, tab, pair, -1.0)]
        mx = logits(mx, ko_ref[...], own, cols <= rows, PROMPT, CONT)
        m = tops(mx)
        carry = ((zf, zf), (zf, zf))
        for j in range(GDEV):
            carry = weigh(carry, vp_ref[j * CHUNK : (j + 1) * CHUNK, :], m, j * CHUNK, CHUNK)
        finish(weigh(carry, vo_ref[...], m, PROMPT, CONT))


def attend(info, tab, q, k, v, kp, vp):
    rows, width = q.shape
    pairs = width // 128
    span = PROMPT + CONT
    tile = pl.BlockSpec((TILE, 128), lambda a, t, s, f: (t, a))
    whole = pl.BlockSpec((PROMPT, 128), lambda a, t, s, f: (0, a))
    return pl.pallas_call(
        fwd_kernel,
        grid_spec=pltpu.PrefetchScalarGridSpec(
            num_scalar_prefetch=2,
            grid=(pairs, rows // TILE),
            in_specs=[tile, whole, whole, tile, tile],
            out_specs=[tile, pl.BlockSpec((2, TILE, span), lambda a, t, s, f: (a, t, 0)), tile],
            scratch_shapes=[pltpu.VMEM((2, TILE, span), F32), pltpu.VMEM((5, 8, PROMPT), F32)],
        ),
        out_shape=[
            jax.ShapeDtypeStruct((rows, width), BF),
            jax.ShapeDtypeStruct((2 * pairs, rows, span), BF),
            jax.ShapeDtypeStruct((rows, width), F32),
        ],
        compiler_params=pltpu.CompilerParams(vmem_limit_bytes=48 << 20),
        cost_estimate=pl.CostEstimate(flops=16 * 10**9, bytes_accessed=60 * 10**6, transcendentals=0),
        name="attend",
    )(info, tab, q, kp, vp, k, v)


def bwd_kernel(info, q_ref, kp_ref, vp_ref, ko_ref, vo_ref, o_ref, li_ref, g_ref, e_ref, dq_ref, dk_ref, dv_ref, dko_ref, dvo_ref, dk_s, dv_s):
    step = pl.program_id(1)
    member = info[0]
    low = low_half(TILE)
    g = g_ref[...].astype(F32) * li_ref[...]
    prod = g * o_ref[...].astype(F32)
    zf = jnp.zeros((TILE, 128), F32)
    deltas = [
        jnp.sum(jnp.where(low, prod, zf), axis=1, keepdims=True),
        jnp.sum(jnp.where(low, zf, prod), axis=1, keepdims=True),
    ]
    gs = [jnp.where(low, g, zf).astype(BF), jnp.where(low, zf, g).astype(BF)]
    gt = jnp.transpose(g).astype(BF)
    qt = jnp.transpose(q_ref[...].astype(F32)).astype(BF)

    def grads(dq, keys, vals, at, width):
        out, dks, dvs = [], [], []
        for h in range(2):
            e = e_ref[h, :, pl.ds(at, width)]
            dp = dot_nt(gs[h], vals)
            ds = (e.astype(F32) * (dp - deltas[h])).astype(BF)
            out.append(dq[h] + dot_nn(ds, keys))
            dks.append(dot_nn(qt[h * HD : (h + 1) * HD, :], ds))
            dvs.append(dot_nn(gt[h * HD : (h + 1) * HD, :], e))
        return tuple(out), dks, dvs

    @pl.when(step == 0)
    def _():
        dk_s[...] = jnp.zeros_like(dk_s)
        dv_s[...] = jnp.zeros_like(dv_s)

    def add(at, width, dks, dvs):
        for h in range(2):
            dk_s[h * HD : (h + 1) * HD, pl.ds(at, width)] += dks[h]
            dv_s[h * HD : (h + 1) * HD, pl.ds(at, width)] += dvs[h]

    def scaled(dq):
        return (jnp.where(low, dq[0], dq[1]).astype(BF).astype(F32) * 0.125).astype(BF)

    @pl.when(step < PTILES)
    def _():
        def one(j, dq):
            at = pl.multiple_of((j ^ member) * CHUNK, CHUNK)
            dq, dks, dvs = grads(dq, kp_ref[pl.ds(at, CHUNK), :], vp_ref[pl.ds(at, CHUNK), :], at, CHUNK)
            add(at, CHUNK, dks, dvs)
            return dq

        dq_ref[...] = scaled(lax.fori_loop(0, member + 1, one, (zf, zf)))
        dko_ref[...] = jnp.zeros_like(dko_ref)
        dvo_ref[...] = jnp.zeros_like(dvo_ref)

    @pl.when(step >= PTILES)
    def _():
        dq = (zf, zf)
        for j in range(GDEV):
            span = slice(j * CHUNK, (j + 1) * CHUNK)
            dq, dks, dvs = grads(dq, kp_ref[span, :], vp_ref[span, :], j * CHUNK, CHUNK)
            add(j * CHUNK, CHUNK, dks, dvs)
        dq, dks, dvs = grads(dq, ko_ref[...], vo_ref[...], PROMPT, CONT)
        dq_ref[...] = scaled(dq)
        dko_ref[...] = jnp.transpose(jnp.concatenate(dks, axis=0)).astype(BF)
        dvo_ref[...] = jnp.transpose(jnp.concatenate(dvs, axis=0)).astype(BF)

    @pl.when(step == pl.num_programs(1) - 1)
    def _():
        for j in range(GDEV):
            span = slice(j * CHUNK, (j + 1) * CHUNK)
            dk_ref[span, :] = jnp.transpose(dk_s[:, span]).astype(BF)
            dv_ref[span, :] = jnp.transpose(dv_s[:, span]).astype(BF)


def attend_back(info, q, k, v, kp, vp, o, li, g, e):
    rows, width = q.shape
    pairs = width // 128
    span = PROMPT + CONT
    tile = pl.BlockSpec((TILE, 128), lambda a, t, s: (t, a))
    whole = pl.BlockSpec((PROMPT, 128), lambda a, t, s: (0, a))
    return pl.pallas_call(
        bwd_kernel,
        grid_spec=pltpu.PrefetchScalarGridSpec(
            num_scalar_prefetch=1,
            grid=(pairs, rows // TILE),
            in_specs=[tile, whole, whole, tile, tile, tile, tile, tile, pl.BlockSpec((2, TILE, span), lambda a, t, s: (a, t, 0))],
            out_specs=[tile, whole, whole, tile, tile],
            scratch_shapes=[pltpu.VMEM((128, PROMPT), F32), pltpu.VMEM((128, PROMPT), F32)],
        ),
        out_shape=[
            jax.ShapeDtypeStruct((rows, width), BF),
            jax.ShapeDtypeStruct((PROMPT, width), BF),
            jax.ShapeDtypeStruct((PROMPT, width), BF),
            jax.ShapeDtypeStruct((rows, width), BF),
            jax.ShapeDtypeStruct((rows, width), BF),
        ],
        compiler_params=pltpu.CompilerParams(vmem_limit_bytes=48 << 20),
        cost_estimate=pl.CostEstimate(flops=30 * 10**9, bytes_accessed=60 * 10**6, transcendentals=0),
        name="attend_back",
    )(info, q, kp, vp, k, v, o, li, g, e)


D = 768
FF = 3072
EPSILON = 1e-05


def flip(value, axis, bit):
    return lax.ppermute(value, axis, [(i, i ^ (1 << bit)) for i in range(lax.axis_size(axis))])


def contract_rows(left, right):
    return lax.dot_general(left, right, (((0,), (0,)), ((), ())), preferred_element_type=F32)


def back_project(left, right):
    return lax.dot_general(left, right, (((1,), (1,)), ((), ())), preferred_element_type=F32)


def dense(left, right):
    return jnp.dot(left, right, preferred_element_type=F32)


def exact_gelu(values):
    return jax.nn.gelu(values, approximate=False)


def norm_rows(values, gain, bias):
    center = jnp.mean(values, axis=-1, keepdims=True)
    spread = jnp.mean(values * values, axis=-1, keepdims=True) - center * center
    scaled = lax.rsqrt(spread + EPSILON)
    unit_rows = (values - center) * scaled
    return (unit_rows * gain + bias, unit_rows, scaled)


def norm_back(grad_rows, gain, unit_rows, scaled):
    shaped = grad_rows * gain
    return scaled * (
        shaped
        - jnp.mean(shaped, axis=-1, keepdims=True)
        - unit_rows * jnp.mean(shaped * unit_rows, axis=-1, keepdims=True)
    )


def in_order(which, mine, other, axis):
    return jnp.where(
        which == 0,
        jnp.concatenate([mine, other], axis=axis),
        jnp.concatenate([other, mine], axis=axis),
    )


def fetch(weight, core, axis):
    half = weight.shape[axis] // 2
    sent = lax.dynamic_slice_in_dim(weight, core * half, half, axis)
    got = flip(sent, "tensor", 0)
    return in_order(core, got, flip(got, "dp", 0), axis)


def halving(value, device):
    bits = lax.axis_size("dp").bit_length() - 1
    rows, columns = value.shape
    current = value
    for bit in range(bits):
        upper = device // (1 << bit) % 2
        left = bits - bit
        view = current.reshape((1 << (left - 1), 2, -1, columns))
        kept = lax.dynamic_index_in_dim(view, upper, 1, keepdims=False)
        sent = lax.dynamic_index_in_dim(view, 1 - upper, 1, keepdims=False)
        got = flip(sent, "dp", bit)
        current = (kept.astype(F32) + got.astype(F32)).astype(BF)
    return current.reshape(rows >> bits, columns)


def body(
    hidden_in,
    cotangent,
    prompt_start,
    cont_gap,
    seg_len,
    dilation_rate,
    pre_gain,
    pre_bias,
    query_weight,
    query_bias,
    key_weight,
    value_weight,
    value_bias,
    sub_gain,
    sub_bias,
    out_weight,
    out_bias,
    mid_gain,
    mid_bias,
    inner_weight,
    inner_bias,
    ffn_gain,
    ffn_bias,
    outer_weight,
    outer_bias,
):
    device = lax.axis_index("dp")
    ranks = lax.axis_size("dp")
    group_id = device // GDEV
    member = device % GDEV
    tensor_id = lax.axis_index("tensor")
    core = device % 2
    width = query_weight.shape[1]
    units = inner_weight.shape[1]
    pairs = width // 128
    rows = hidden_in.shape[0]
    half = rows // 2
    prompt_rows = CHUNK
    cont_count = (rows - prompt_rows) // CONT

    start_at = lax.dynamic_index_in_dim(prompt_start, group_id, 0, keepdims=False)
    gap_row = lax.dynamic_index_in_dim(cont_gap, group_id, 0, keepdims=False)
    own_gaps = lax.dynamic_slice_in_dim(gap_row, member * cont_count, cont_count)
    info = jnp.concatenate(
        [
            jnp.stack([member, start_at]),
            start_at + member * prompt_rows + TILE * jnp.arange(PTILES),
            start_at + PROMPT + own_gaps,
        ]
    ).astype(jnp.int32)
    seg = lax.dynamic_slice_in_dim(seg_len, tensor_id * pairs, pairs, 0)
    rate = lax.dynamic_slice_in_dim(dilation_rate, tensor_id * pairs, pairs, 0)
    head = 2 * (tensor_id * pairs + jnp.arange(pairs))
    tab = jnp.stack(
        [
            1.0 / seg[:, 0].astype(F32),
            1.0 / seg[:, 1].astype(F32),
            rate[:, 1].astype(F32),
            1.0 / rate[:, 1].astype(F32),
            rate[:, 2].astype(F32),
            1.0 / rate[:, 2].astype(F32),
            (head % rate[:, 1]).astype(F32),
            ((head + 1) % rate[:, 1]).astype(F32),
            (head % rate[:, 2]).astype(F32),
            ((head + 1) % rate[:, 2]).astype(F32),
        ],
        axis=1,
    ).reshape(-1)

    inner_other = fetch(inner_weight, core, 1)
    outer_other = fetch(outer_weight, core, 0)
    out_other = fetch(out_weight, core, 0)
    vectors = jnp.concatenate([inner_bias, ffn_gain, ffn_bias, sub_gain, sub_bias])
    vectors_other = flip(vectors, "tensor", 0)
    splits = [units, 2 * units, 3 * units, 3 * units + width]
    ib_o, fg_o, fb_o, sg_o, sb_o = jnp.split(vectors_other, splits)
    both = lambda mine, other: jnp.concatenate([mine, other]).astype(F32)
    inner_bias_f = both(inner_bias, ib_o)
    ffn_gain_f, ffn_bias_f = both(ffn_gain, fg_o), both(ffn_bias, fb_o)
    sub_gain_f, sub_bias_f = both(sub_gain, sg_o), both(sub_bias, sb_o)
    inner_all = jnp.concatenate([inner_weight, inner_other], axis=1)
    outer_all = jnp.concatenate([outer_weight, outer_other], axis=0)
    out_all = jnp.concatenate([out_weight, out_other], axis=0)

    inputs = hidden_in.astype(F32)
    pre_gain_f = pre_gain.astype(F32)
    pre_normed, pre_unit, pre_scale = norm_rows(inputs, pre_gain_f, pre_bias.astype(F32))
    pre_low = pre_normed.astype(BF)
    keys = dense(pre_low, key_weight).astype(BF)
    values = (dense(pre_low, value_weight) + value_bias.astype(F32)).astype(BF)
    own_pair = jnp.stack([keys[:prompt_rows], values[:prompt_rows]])
    far = flip(own_pair, "dp", 1)
    near_own = flip(own_pair, "dp", 0)
    near_far = flip(far, "dp", 0)
    prompt_pair = jnp.concatenate([own_pair, near_own, far, near_far], axis=1)
    queries = ((dense(pre_low, query_weight) + query_bias.astype(F32)) * 0.125).astype(BF)
    attended, weighed, inverse = attend(info, tab, queries, keys, values, prompt_pair[0], prompt_pair[1])

    own_at = tensor_id * half
    other_at = (1 - tensor_id) * half
    att_mine = lax.dynamic_slice_in_dim(attended, own_at, half)
    att_got = flip(lax.dynamic_slice_in_dim(attended, other_at, half), "tensor", 0)
    att_rows = jnp.concatenate([att_mine, att_got], axis=1).astype(F32)
    hidden_rows = lax.dynamic_slice_in_dim(hidden_in, own_at, half).astype(F32)
    cot_rows = lax.dynamic_slice_in_dim(cotangent, own_at, half)

    sub_normed, sub_unit, sub_scale = norm_rows(att_rows, sub_gain_f, sub_bias_f)
    sub_low = sub_normed.astype(BF)
    mixed = hidden_rows + (dense(sub_low, out_all) + out_bias.astype(F32))
    mid_gain_f = mid_gain.astype(F32)
    mid_normed, mid_unit, mid_scale = norm_rows(mixed, mid_gain_f, mid_bias.astype(F32))
    mid_low = mid_normed.astype(BF)
    inner = dense(mid_low, inner_all) + inner_bias_f
    activated = exact_gelu(inner)
    ffn_normed, ffn_unit, ffn_scale = norm_rows(activated, ffn_gain_f, ffn_bias_f)
    ffn_low = ffn_normed.astype(BF)
    outer = dense(ffn_low, outer_all)
    out_half = (mixed + (outer + outer_bias.astype(F32))).astype(BF)

    grad_result = cot_rows.astype(F32)
    outer_bias_grad = jnp.sum(grad_result, axis=0)
    outer_t_grad = contract_rows(cot_rows, ffn_low)
    grad_ffn = back_project(cot_rows, outer_all)
    ffn_gain_grad = jnp.sum(grad_ffn * ffn_unit, axis=0)
    ffn_bias_grad = jnp.sum(grad_ffn, axis=0)
    grad_activated = norm_back(grad_ffn, ffn_gain_f, ffn_unit, ffn_scale)
    _, gelu_back = jax.vjp(exact_gelu, inner)
    grad_inner = gelu_back(grad_activated)[0].astype(BF)
    inner_bias_grad = jnp.sum(grad_inner.astype(F32), axis=0)
    inner_grad = contract_rows(mid_low, grad_inner)
    grad_mid = back_project(grad_inner, inner_all)
    mid_gain_grad = jnp.sum(grad_mid * mid_unit, axis=0)
    mid_bias_grad = jnp.sum(grad_mid, axis=0)
    grad_mixed = grad_result + norm_back(grad_mid, mid_gain_f, mid_unit, mid_scale)
    grad_branch = grad_mixed.astype(BF)
    out_bias_grad = jnp.sum(grad_branch.astype(F32), axis=0)
    out_t_grad = contract_rows(grad_branch, sub_low)
    grad_sub = back_project(grad_branch, out_all)
    sub_gain_grad = jnp.sum(grad_sub * sub_unit, axis=0)
    sub_bias_grad = jnp.sum(grad_sub, axis=0)
    grad_att = norm_back(grad_sub, sub_gain_f, sub_unit, sub_scale).astype(BF)

    grad_mine = grad_att[:, :width]
    grad_got = flip(grad_att[:, width:], "tensor", 0)
    grad_attended = in_order(tensor_id, grad_mine, grad_got, 0)

    def columns(vector):
        per = vector.shape[0] // ranks
        block = D // ranks
        count = -(-per // block)
        padded = jnp.pad(vector.reshape(ranks, per), ((0, 0), (0, count * block - per)))
        return padded.reshape(ranks, count, block).swapaxes(1, 2).reshape(D, count)

    def vector_of(cols, per):
        return cols.T.reshape(-1)[:per]

    shared = [out_bias_grad, mid_gain_grad, mid_bias_grad, outer_bias_grad]

    def pack(at, at_w):
        parts = [inner_grad[:, at : at + units], outer_t_grad[:, at : at + units], out_t_grad[:, at_w : at_w + width]]
        small = [v[at : at + units] for v in (ffn_gain_grad, ffn_bias_grad, inner_bias_grad)]
        small = small + [v[at_w : at_w + width] for v in (sub_gain_grad, sub_bias_grad)] + shared
        cols = [columns(v) for v in small]
        used = sum(c.shape[1] for c in cols)
        fill = -(-used // 128) * 128 - used
        return jnp.concatenate([p.astype(BF) for p in parts + cols] + [jnp.zeros((D, fill), BF)], axis=1)

    early = lax.psum_scatter(
        jnp.concatenate([pack(0, 0), pack(units, width)], axis=1), "dp", scatter_dimension=0, tiled=True
    )
    early_mine, early_other = jnp.split(early, 2, axis=1)
    early_sum = early_mine.astype(F32) + flip(early_other, "tensor", 0).astype(F32)
    big = 2 * units + width
    inner_weight_grad = early_sum[:, :units]
    outer_weight_grad = early_sum[:, units : 2 * units].T
    out_weight_grad = early_sum[:, 2 * units : big].T
    tail = early_sum[:, big:]
    block = D // ranks
    per_u, per_w = units // ranks, width // ranks
    cu, cw = -(-per_u // block), -(-per_w // block)
    ffn_gain_grad = vector_of(tail[:, 0:cu], per_u)
    ffn_bias_grad = vector_of(tail[:, cu : 2 * cu], per_u)
    inner_bias_grad = vector_of(tail[:, 2 * cu : 3 * cu], per_u)
    sub_gain_grad = vector_of(tail[:, 3 * cu : 3 * cu + cw], per_w)
    sub_bias_grad = vector_of(tail[:, 3 * cu + cw : 3 * cu + 2 * cw], per_w)
    out_bias_grad, mid_gain_grad, mid_bias_grad, outer_bias_grad = [
        tail[:, 3 * cu + 2 * cw + i] for i in range(4)
    ]

    output = in_order(tensor_id, out_half, flip(out_half, "tensor", 0), 0)

    grad_query_in, key_acc, value_acc, own_key_grad, own_value_grad = attend_back(
        info, queries, keys, values, prompt_pair[0], prompt_pair[1], attended, inverse, grad_attended, weighed
    )
    acc = jnp.stack([key_acc, value_acc]).reshape(2, GDEV, prompt_rows, width)
    near = acc[:, 0::2].astype(F32) + flip(acc[:, 1::2], "dp", 0).astype(F32)
    summed = (near[:, 0] + flip(near[:, 1].astype(BF), "dp", 1).astype(F32)).astype(BF)
    grad_keys = jnp.concatenate([summed[0], own_key_grad[prompt_rows:]], axis=0)
    grad_values = jnp.concatenate([summed[1], own_value_grad[prompt_rows:]], axis=0)

    query_weight_grad = contract_rows(pre_low, grad_query_in)
    key_weight_grad = contract_rows(pre_low, grad_keys)
    value_weight_grad = contract_rows(pre_low, grad_values)
    query_bias_grad = jnp.sum(grad_query_in.astype(F32), axis=0)
    value_bias_grad = jnp.sum(grad_values.astype(F32), axis=0)
    grad_normed_part = (
        back_project(grad_query_in, query_weight)
        + back_project(grad_keys, key_weight)
        + back_project(grad_values, value_weight)
    )
    grad_normed_low = grad_normed_part.astype(BF)
    grad_normed = grad_normed_low.astype(F32) + flip(grad_normed_low, "tensor", 0).astype(F32)
    pre_gain_grad = jnp.sum(grad_normed * pre_unit, axis=0)
    pre_bias_grad = jnp.sum(grad_normed, axis=0)
    grad_mixed_low = grad_mixed.astype(BF)
    grad_mixed_all = in_order(tensor_id, grad_mixed_low, flip(grad_mixed_low, "tensor", 0), 0).astype(F32)
    input_low = (grad_mixed_all + norm_back(grad_normed, pre_gain_f, pre_unit, pre_scale)).astype(BF)

    cols = [columns(v) for v in (query_bias_grad, value_bias_grad, pre_gain_grad, pre_bias_grad)]
    used = sum(c.shape[1] for c in cols)
    fill = -(-used // 128) * 128 - used
    late = halving(
        jnp.concatenate(
            [p.astype(BF) for p in [query_weight_grad, key_weight_grad, value_weight_grad] + cols]
            + [jnp.zeros((D, fill), BF)],
            axis=1,
        ),
        device,
    ).astype(F32)
    tail = late[:, 3 * width :]
    return (
        output,
        input_low,
        tail[:, 2 * cw],
        tail[:, 2 * cw + 1],
        late[:, :width],
        vector_of(tail[:, 0:cw], per_w),
        late[:, width : 2 * width],
        late[:, 2 * width : 3 * width],
        vector_of(tail[:, cw : 2 * cw], per_w),
        sub_gain_grad,
        sub_bias_grad,
        out_weight_grad,
        out_bias_grad,
        mid_gain_grad,
        mid_bias_grad,
        inner_weight_grad,
        inner_bias_grad,
        ffn_gain_grad,
        ffn_bias_grad,
        outer_weight_grad,
        outer_bias_grad,
    )


def solution(mesh):
    placed = (
        P("dp", None),
        P("dp", None),
        P(),
        P(),
        P(),
        P(),
        P(),
        P(),
        P(None, "tensor"),
        P("tensor"),
        P(None, "tensor"),
        P(None, "tensor"),
        P("tensor"),
        P("tensor"),
        P("tensor"),
        P("tensor", None),
        P(),
        P(),
        P(),
        P(None, "tensor"),
        P("tensor"),
        P("tensor"),
        P("tensor"),
        P("tensor", None),
        P(),
    )
    return jax.shard_map(
        body,
        mesh=mesh,
        in_specs=placed,
        out_specs=(
            P("dp", None),
            P("dp", None),
            P("dp"),
            P("dp"),
            P("dp", "tensor"),
            P(("tensor", "dp")),
            P("dp", "tensor"),
            P("dp", "tensor"),
            P(("tensor", "dp")),
            P(("tensor", "dp")),
            P(("tensor", "dp")),
            P("tensor", "dp"),
            P("dp"),
            P("dp"),
            P("dp"),
            P("dp", "tensor"),
            P(("tensor", "dp")),
            P(("tensor", "dp")),
            P(("tensor", "dp")),
            P("tensor", "dp"),
            P("dp"),
        ),
        check_vma=False,
    )
```

time: 1310 us -> 518 us (0.40)
  waiting for transfers between devices: 555 us -> 107 us
  matrix products: 344 us -> 79.3 us
  other arithmetic: 178 us -> 52.8 us
  blocking collectives: 96.1 us -> 0 us
  Pallas kernels: 0 us -> 88.6 us
  starting transfers between devices: 5.63 us -> 55.2 us
  loops' own time: 17.6 us -> 0 us
  local copies, waits for them, and re-layouts: 94.9 us -> 112 us
    reduce_scatter x6 -> x1, waiting for transfers between devices: 326 us -> 0.01 us  [body(): lax.psum_scatter(jnp.concatenate([pack(0, 0), pack(units, width)], axis=1...]
    dot_general x54 -> x6, matrix products: 290 us -> 37.6 us  [dense(): return jnp.dot(left, right, preferred_element_type=F32)]
    psum x3 -> x0, waiting for transfers between devices: 177 us -> none  [the longest x1 64.6 us: body(): lax.psum(outer_part.astype(jnp.bfloat16), 'tensor').astype(jnp.float32)]
    pallas_call x0 -> x2, Pallas kernels: none -> 88.6 us  [the longest x1 47.4 us: attend_back(): pl.pallas_call(bwd_kernel, grid_spec=pltpu.PrefetchScalarGridSpec(num_sca...]
    unnamed x1 -> x0, blocking collectives: 61.5 us -> none
    ppermute x4 -> x22, waiting for transfers between devices: 50.7 us -> 107 us  [flip(): lax.ppermute(value, axis, [(i, i ^ 1 << bit) for i in range(lax.axis_size...]
    ppermute x4 -> x22, starting transfers between devices: 4.79 us -> 55.2 us  [flip(): lax.ppermute(value, axis, [(i, i ^ 1 << bit) for i in range(lax.axis_size...]
    another operation x8 -> x2, other arithmetic: 39 us -> 3.21 us  [the longest x1 2.24 us: body(): acc = jnp.stack([key_acc, value_acc]).reshape(2, GDEV, prompt_rows, width)]
  transfers between devices with their start and end apart: 13 -> 23, of which waited for: 10 -> 10; matrix products, arithmetic and copies ran while one was open for 8% -> 32% of each run, Pallas kernels for 0% -> 17%
where the time goes in v1:
time: 518 us; the launch traced here: 511 us
  local copies, waits for them, and re-layouts  112 us (22%)
  waiting for transfers between devices  107 us (21%)
  Pallas kernels  88.6 us (17%)
  matrix products  79.3 us (15%)
  starting transfers between devices  55.2 us (11%)
  other arithmetic  52.8 us (10%)
  between operations  16.5 us (3%)
    ppermute x22, waiting for transfers between devices, flip(): lax.ppermute(value, axis, [(i, i ^ 1 << bit) for i in range(lax.axis_size...  107 us
    ppermute x22, starting transfers between devices, flip(): lax.ppermute(value, axis, [(i, i ^ 1 << bit) for i in range(lax.axis_size...  55.2 us
    pallas_call x1, Pallas kernels, attend_back(): pl.pallas_call(bwd_kernel, grid_spec=pltpu.PrefetchScalarGridSpec(num_sca...  47.4 us
    pallas_call x1, Pallas kernels, attend(): pl.pallas_call(fwd_kernel, grid_spec=pltpu.PrefetchScalarGridSpec(num_sca...  41.2 us
    dot_general x6, matrix products, dense(): return jnp.dot(left, right, preferred_element_type=F32)  37.6 us
    convert_element_type x20, local copies, waits for them, and re-layouts, pack(): p.astype(BF)  25.8 us
    dot_general x6, matrix products, back_project(): lax.dot_general(left, right, (((1,), (1,)), ((), ())), preferred_element_...  24.5 us
    concatenate x1, local copies, waits for them, and re-layouts, body(): jnp.concatenate([pack(0, 0), pack(units, width)], axis=1)  23.1 us
  transfers between devices with their start and end apart: 23, of which 10 were waited for; matrix products, arithmetic and copies ran while one was open for 32% of the time, Pallas kernels for 17%

profile of v1, /device:TPU:0, one launch (start us, length us, event | category | flops | bytes accessed | tf_op | source)
XLA Modules:
  0.0 511.1 jit_solution(8265408343599696986)
XLA Ops:
  9.5 2.2 convert_reduce_fusion
  17.4 2.9 collective-permute-start.1
  21.8 1.5 collective-permute-start.4
  24.5 2.5 constant_dynamic-slice_fusion.1
  27.0 1.5 collective-permute-start.9
  32.0 6.2 %collective-permute-done.1 = bf16[2,512,384]{2,1,0:T(8,128)(2,1)} collective-permute-done((bf16[2,512,384]{2,1,0:T(8,128)(2,1)}, bf16[2,512,384]{2,1,0:T(8,128)(2,1)}, u32[]{:S(2)}, u32[]{:S(2)}) %collective-permute-start.1) | collective-permute-done | bytes 786464 | tf_op jit(solution)/shard_map/ppermute | solution.py:287
  38.2 2.4 constant_dynamic-slice_fusion.2
  40.6 2.2 fusion.30.q_ref
  43.7 1.8 collective-permute-start.7
  45.6 2.8 pad_maximum_fusion.2
  50.7 41.2 %attend.1 = (bf16[1280,384]{1,0:T(8,128)(2,1)S(1)}, bf16[6,1280,2304]{2,1,0:T(8,128)(2,1)}, f32[1280,384]{1,0:T(8,128)}) custom-call(s32[7]{0:T(128)S(1)} %pad_add_fusion.info, f32[30]{0:T(128)S(1)} %reshape.599.tab, bf16[1280,384]{1,0:T(8,128)(2,1)S(1)} %copy-done.9, bf16[2048,384]{1,0:T(8,128)(2,1)S(1)} %get-tuple-element.83.kp_ref, ...), custom_call_target="tpu_custom_call" | custom-call | flops 16000000000 | bytes 60000000 | tf_op jit(solution)/shard_map/attend/pallas_call | solution.py:162
  92.4 5.4 %collective-permute-start.6 = (bf16[192,768]{1,0:T(8,128)(2,1)}, bf16[192,768]{1,0:T(8,128)(2,1)S(1)}, u32[]{:S(2)}, u32[]{:S(2)}) collective-permute-start(bf16[192,768]{1,0:T(8,128)(2,1)} %collective-permute-done.5), channel_id=1, source_target_pairs={{0,2},{2,0},{4,6},{6,4},{8,10},{10,8},{12,14},{14,12},{16,18},{18,... | collective-permute-start | bytes 884744 | tf_op jit(solution)/shard_map/ppermute | solution.py:287
  104.7 2.0 copy-done.38
  106.7 23.4 %fusion.84 = (f32[640]{0:T(1024)S(1)}, f32[640]{0:T(1024)S(1)}, f32[640,3072]{1,0:T(8,128)S(1)}, f32[640,3072]{1,0:T(8,128)S(1)}, f32[640,3072]{1,0:T(8,128)}) fusion(f32[3072]{0:T(1024)S(1)} %maximum_convert_fusion, bf16[768,1536]{1,0:T(8,128)(2,1)S(1)} %maximum_select_fusion, bf16[768,1536]{1,0:T(8,128)(2,1)S(1)} %copy-done.38, ...), kind=kOutput, calls=%fused_computation.220 | convolution fusion | flops 3165486080 | bytes 30306304 | tf_op jit(solution)/shard_map/dot_general | solution.py:299
  130.1 2.0 maximum_select_fusion.1
  132.1 12.2 %multiply_reduce_fusion = (bf16[3072]{0:T(1024)(128)(2,1)S(1)}, f32[640]{0:T(1024)S(1)}, f32[640]{0:T(1024)S(1)}, bf16[3072]{0:T(1024)(128)(2,1)S(1)}, bf16[640,3072]{1,0:T(8,128)(2,1)}, /*index=5*/f32[640,3072]{1,0:T(8,128)}) fusion(f32[640,3072]{1,0:T(8,128)S(1)} %get-tuple-element.75, f32[640]{0:T(1024)S(1)} %get-tuple-element.118, ...), kind=kOutput, calls=%fused_computation.2 | convolution fusion | flops 3052921856 | bytes 25409540 | tf_op jit(solution)/shard_map/dot_general | solution.py:295
  144.3 10.0 %fusion.87 = (bf16[3072]{0:T(1024)(128)(2,1)S(1)}, bf16[640,3072]{1,0:T(8,128)(2,1)S(1)}) fusion(f32[640,3072]{1,0:T(8,128)S(1)} %get-tuple-element.76, f32[640]{0:T(1024)S(1)} %broadcast_multiply_fusion.3, f32[640,3072]{1,0:T(8,128)S(1)} %get-tuple-element.75, f32[640]{0:T(1024)S(1)} %get-tuple-element.117, f32[640]{0:T(1024)S(1)} %broadcast_multiply_fusion.4, ...), kind=kLoop, calls=%fused_computation.223 | loop fusion | flops 45216768 | bytes 35430400 | tf_op jit(solution)/shard_map/reduce_sum | solution.py:482
  154.3 5.9 %multiply_reduce_fusion.4 = (bf16[768]{0:T(1024)(128)(2,1)}, f32[640]{0:T(1024)S(1)}, f32[640]{0:T(1024)S(1)}, bf16[768]{0:T(1024)(128)(2,1)}, f32[640,768]{1,0:T(8,128)S(1)}) fusion(f32[640,768]{1,0:T(8,128)S(1)} %copy-done.27, f32[640]{0:T(1024)S(1)} %get-tuple-element.120, f32[640]{0:T(1024)S(1)} %get-tuple-element.119, ...), kind=kOutput, calls=%fused_computation.86 | convolution fusion | flops 3033756928 | bytes 12599296 | tf_op jit(solution)/shard_map/dot_general | solution.py:295
  160.3 4.8 convolution_convert_fusion.1
  166.2 1.8 fusion.90
  169.8 4.1 convolution_convert_fusion
  173.9 2.5 fusion.89
  176.5 2.0 fusion.86
  193.3 1.6 copy.119
  194.8 1.6 copy.122
  196.4 1.6 copy.118
  197.9 1.6 copy.120
  199.5 1.6 copy.123
  201.9 1.5 convert_element_type.596
  203.4 1.5 convert_element_type.597
  204.9 1.5 convert_element_type.599
  206.4 1.5 convert_element_type.598
  214.1 1.6 convert_element_type.592
  219.0 23.1 %concatenate.142 = bf16[768,7168]{1,0:T(8,128)(2,1)} concatenate(bf16[768,1536]{1,0:T(8,128)(2,1)} %get-tuple-element.81, bf16[768,1536]{1,0:T(8,128)(2,1)} %get-tuple-element.79, bf16[768,384]{1,0:T(8,128)(2,1)} %get-tuple-element.86, bf16[768,2]{1,0:T(8,128)(2,1)} %bitcast.103, bf16[768,2]{1,0:T(8,128)(2,1)} %bitcast.101, bf16[768,2]{1,0:T(8,128)(2,1)} %bitcast.104, ...), dimensions={1} | concatenate | bytes 22020096 | tf_op jit(solution)/shard_map/concatenate | solution.py:522
  243.2 2.5 maximum_select_fusion.4.g_ref
  246.9 47.4 %attend_back.1 = (bf16[1280,384]{1,0:T(8,128)(2,1)S(1)}, bf16[2048,384]{1,0:T(8,128)(2,1)}, bf16[2048,384]{1,0:T(8,128)(2,1)}, bf16[1280,384]{1,0:T(8,128)(2,1)S(1)}, bf16[1280,384]{1,0:T(8,128)(2,1)S(1)}) custom-call(s32[7]{0:T(128)S(1)} %pad_add_fusion.info, bf16[1280,384]{1,0:T(8,128)(2,1)S(1)} %copy-done.10, bf16[2048,384]{1,0:T(8,128)(2,1)} %copy-done.1, ...), custom_call_target="tpu_custom_call" | custom-call | flops 30000001024 | bytes 60000000 | tf_op jit(solution)/shard_map/attend_back/pallas_call | solution.py:259
  294.3 2.2 pad_maximum_fusion.3
  296.7 5.5 %collective-permute-start.14 = (bf16[2,2,512,384]{3,2,0,1:T(8,128)(2,1)S(1)}, bf16[2,2,512,384]{3,2,0,1:T(8,128)(2,1)S(1)}, u32[]{:S(2)}, u32[]{:S(2)}) collective-permute-start(bf16[2,2,512,384]{3,2,0,1:T(8,128)(2,1)S(1)} %slice.310), channel_id=1, source_target_pairs={{0,2},{2,0},{4,6},{6,4},{8,10},{10,8},{12,14},{14,12},{16,18},{18,... | collective-permute-start | bytes 4718600 | tf_op jit(solution)/shard_map/ppermute | solution.py:287
  302.2 3.0 collective-permute-done.14
  305.6 21.4 %collective-permute-start.15 = (bf16[2,512,384]{2,1,0:T(8,128)(2,1)S(1)}, bf16[2,512,384]{2,1,0:T(8,128)(2,1)S(1)}, u32[]{:S(2)}, u32[]{:S(2)}) collective-permute-start(bf16[2,512,384]{2,1,0:T(8,128)(2,1)S(1)} %fusion.48), channel_id=1, source_target_pairs={{0,4},{2,6},{4,0},{6,2},{8,12},{10,14},{12,8},{14,10},{16,20},{18,... | collective-permute-start | bytes 2359304 | tf_op jit(solution)/shard_map/ppermute | solution.py:287
  328.5 31.1 %collective-permute-done.15 = bf16[2,512,384]{2,1,0:T(8,128)(2,1)S(1)} collective-permute-done((bf16[2,512,384]{2,1,0:T(8,128)(2,1)S(1)}, bf16[2,512,384]{2,1,0:T(8,128)(2,1)S(1)}, u32[]{:S(2)}, u32[]{:S(2)}) %collective-permute-start.15) | collective-permute-done | bytes 786464 | tf_op jit(solution)/shard_map/ppermute | solution.py:287
  361.2 2.6 fusion.22
  363.8 1.6 collective-permute-start.16
  366.5 2.8 convolution_convert_fusion.6
  371.2 2.9 convolution_convert_fusion.5
  377.1 31.0 %collective-permute-done.16 = bf16[1280,768]{1,0:T(8,128)(2,1)} collective-permute-done((bf16[1280,768]{1,0:T(8,128)(2,1)}, bf16[1280,768]{1,0:T(8,128)(2,1)}, u32[]{:S(2)}, u32[]{:S(2)}) %collective-permute-start.16) | collective-permute-done | bytes 1966112 | tf_op jit(solution)/shard_map/ppermute | solution.py:287
  408.1 4.5 fusion.18
  415.4 1.5 copy.116
  416.9 1.5 copy.115
  419.2 4.8 concatenate.141
  423.9 2.2 dynamic-slice_bitcast_fusion
  426.8 8.2 %add_convert_fusion.3 = bf16[640,768]{1,0:T(8,128)(2,1)} fusion(f32[640,768]{1,0:T(8,128)} %copy-done.26, bf16[640,3072]{1,0:T(8,128)(2,1)} %get-tuple-element.77, bf16[1536,768]{1,0:T(8,128)(2,1)} %copy-done.20, bf16[1536,768]{1,0:T(8,128)(2,1)} %param.48, f32[768]{0:T(1024)S(1)} %convert_element_type.513), kind=kOutput, calls=%fused_computation.89 | convolution fusion | flops 3030810624 | bytes 11602944 | tf_op jit(solution)/shard_map/dot_general | solution.py:299
  435.1 1.6 collective-permute-start.11
  436.7 1.7 fusion.44
  440.3 2.1 collective-permute-start.18
  443.0 16.9 %collective-permute-done.11 = bf16[640,768]{1,0:T(8,128)(2,1)} collective-permute-done((bf16[640,768]{1,0:T(8,128)(2,1)}, bf16[640,768]{1,0:T(8,128)(2,1)}, u32[]{:S(2)}, u32[]{:S(2)}) %collective-permute-start.11) | collective-permute-done | bytes 983072 | tf_op jit(solution)/shard_map/ppermute | solution.py:287
  460.0 4.0 maximum_select_fusion.2
  465.2 2.4 collective-permute-start.19
  467.5 5.5 %collective-permute-done.19 = bf16[2,48,1280]{2,1,0:T(8,128)(2,1)S(1)} collective-permute-done((bf16[2,48,1280]{2,1,0:T(8,128)(2,1)S(1)}, bf16[2,48,1280]{2,1,0:T(8,128)(2,1)S(1)}, u32[]{:S(2)}, u32[]{:S(2)}) %collective-permute-start.19) | collective-permute-done | bytes 245792 | tf_op jit(solution)/shard_map/ppermute | solution.py:287
  473.1 2.8 collective-permute-start.20
  475.9 4.6 collective-permute-done.12
  480.5 5.9 %fusion.17 = bf16[1280,768]{1,0:T(8,128)(2,1)} fusion(bf16[1280,768]{1,0:T(8,128)(2,1)S(1)} %copy-done.13, bf16[1280,768]{1,0:T(8,128)(2,1)} %collective-permute-done.16, bf16[1280,768]{1,0:T(8,128)(2,1)} %fusion.22, bf16[640,768]{1,0:T(8,128)(2,1)S(1)} %collective-permute-done.12, bf16[640,768]{1,0:T(8,128)(2,1)S(1)} %copy-done.15, ...), kind=kLoop, calls=%fused_computation.43 | loop fusion | flops 22609920 | bytes 9853953 | tf_op jit(solution)/shard_map/convert_element_type | solution.py:570
  488.2 1.7 collective-permute-start.21
  491.3 6.7 %collective-permute-done.21 = bf16[48,3584]{1,0:T(8,128)(2,1)S(1)} collective-permute-done((bf16[48,3584]{1,0:T(8,128)(2,1)S(1)}, bf16[48,3584]{1,0:T(8,128)(2,1)S(1)}, u32[]{:S(2)}, u32[]{:S(2)}) %collective-permute-start.21) | collective-permute-done | bytes 344096 | tf_op jit(solution)/shard_map/ppermute | solution.py:287
  (294 shorter events, 80.1 us)
Async XLA Ops:
  7.2 33.4 %copy-start = (bf16[768,384]{1,0:T(8,128)(2,1)S(1)}, bf16[768,384]{1,0:T(8,128)(2,1)}, u32[]{:S(2)}) copy-start(bf16[768,384]{1,0:T(8,128)(2,1)} %param.33) | copy-start | bytes 1769476
  7.2 4.5 copy-start.11
  7.2 480.0 %reduce-scatter.2.cloned.1.call-start = ((), (), s32[]{:S(2)}) async-start(), calls=%async_computation.1 | async-start | bytes 11698176 | tf_op jit(solution)/shard_map/reduce_scatter | solution.py:521
  8.8 3.7 copy-start.49
  15.4 4.9 copy-start.54
  15.4 5.3 %copy-start.55 = (bf16[1536]{0:T(1024)(128)(2,1)S(1)}, bf16[1536]{0:T(1024)(128)(2,1)}, u32[]{:S(2)}) copy-start(bf16[1536]{0:T(1024)(128)(2,1)} %param.46) | copy-start | bytes 9220
  15.5 5.6 %copy-start.56 = (bf16[1536]{0:T(1024)(128)(2,1)S(1)}, bf16[1536]{0:T(1024)(128)(2,1)}, u32[]{:S(2)}) copy-start(bf16[1536]{0:T(1024)(128)(2,1)} %param.47) | copy-start | bytes 9220
  15.5 5.8 %copy-start.57 = (bf16[384]{0:T(512)(128)(2,1)S(1)}, bf16[384]{0:T(512)(128)(2,1)}, u32[]{:S(2)}) copy-start(bf16[384]{0:T(512)(128)(2,1)} %param.38) | copy-start | bytes 2308
  15.5 6.1 %copy-start.58 = (bf16[384]{0:T(512)(128)(2,1)S(1)}, bf16[384]{0:T(512)(128)(2,1)}, u32[]{:S(2)}) copy-start(bf16[384]{0:T(512)(128)(2,1)} %param.39) | copy-start | bytes 2308
  15.5 7.8 %copy-start.42 = (bf16[384,768]{1,0:T(8,128)(2,1)S(1)}, bf16[384,768]{1,0:T(8,128)(2,1)}, u32[]{:S(2)}) copy-start(bf16[384,768]{1,0:T(8,128)(2,1)} %param.40) | copy-start | bytes 1769476
  16.4 12.2 %copy-start.62 = (s32[6,3]{0,1:T(4,128)S(1)}, s32[6,3]{0,1:T(4,128)}, u32[]{:S(2)}) copy-start(s32[6,3]{0,1:T(4,128)} %param.29) | copy-start | bytes 220
  16.4 12.3 %copy-start.63 = (s32[6,3]{0,1:T(4,128)S(1)}, s32[6,3]{0,1:T(4,128)}, u32[]{:S(2)}) copy-start(s32[6,3]{0,1:T(4,128)} %param.30) | copy-start | bytes 220
  16.4 12.3 %copy-start.65 = (s32[4]{0:T(128)S(1)}, s32[4]{0:T(128)}, u32[]{:S(2)}) copy-start(s32[4]{0:T(128)} %param.27) | copy-start | bytes 52
  16.4 14.6 %copy-start.64 = (bf16[384]{0:T(512)(128)(2,1)S(1)}, bf16[384]{0:T(512)(128)(2,1)}, u32[]{:S(2)}) copy-start(bf16[384]{0:T(512)(128)(2,1)} %param.34) | copy-start | bytes 2308
  17.4 20.8 %collective-permute-start.1 = (bf16[2,512,384]{2,1,0:T(8,128)(2,1)}, bf16[2,512,384]{2,1,0:T(8,128)(2,1)}, u32[]{:S(2)}, u32[]{:S(2)}) collective-permute-start(bf16[2,512,384]{2,1,0:T(8,128)(2,1)} %pad_maximum_fusion.14), channel_id=1, source_target_pairs={{0,4},{2,6},{4,0},{6,2},{8,12},{10,14},{12,8},{14,10},{16,20},{18,... | collective-permute-start | bytes 2359304 | tf_op jit(solution)/shard_map/ppermute | solution.py:287
  20.3 25.2 %collective-permute-start = (bf16[2,512,384]{2,1,0:T(8,128)(2,1)}, bf16[2,512,384]{2,1,0:T(8,128)(2,1)}, u32[]{:S(2)}, u32[]{:S(2)}) collective-permute-start(bf16[2,512,384]{2,1,0:T(8,128)(2,1)} %pad_maximum_fusion.14), channel_id=1, source_target_pairs={{0,2},{2,0},{4,6},{6,4},{8,10},{10,8},{12,14},{14,12},{16,18},{18,... | collective-permute-start | bytes 2359304 | tf_op jit(solution)/shard_map/ppermute | solution.py:287
  21.8 22.0 %collective-permute-start.4 = (bf16[5376]{0:T(1024)(128)(2,1)S(1)}, bf16[5376]{0:T(1024)(128)(2,1)S(1)}, u32[]{:S(2)}, u32[]{:S(2)}) collective-permute-start(bf16[5376]{0:T(1024)(128)(2,1)S(1)} %dynamic-update-slice.4), channel_id=1, source_target_pairs={{0,1},{1,0},{2,3},{3,2},{4,5},{5,4},{6,7},{7,6},{8,9},{9,8},{10,11... | collective-permute-start | bytes 32264 | tf_op jit(solution)/shard_map/ppermute | solution.py:287
  24.0 68.3 %collective-permute-start.5 = (bf16[192,768]{1,0:T(8,128)(2,1)}, bf16[192,768]{1,0:T(8,128)(2,1)}, u32[]{:S(2)}, u32[]{:S(2)}) collective-permute-start(bf16[192,768]{1,0:T(8,128)(2,1)} %constant_dynamic-slice_fusion.3), channel_id=1, source_target_pairs={{0,1},{1,0},{2,3},{3,2},{4,5},{5,4},{6,7},{7,6},{8,9},{9,8},{10,11... | collective-permute-start | bytes 884744 | tf_op jit(solution)/shard_map/ppermute | solution.py:287
  24.5 16.0 %copy-start.24 = (bf16[1280,768]{1,0:T(8,128)(2,1)S(1)}, bf16[1280,768]{1,0:T(8,128)(2,1)}, u32[]{:S(2)}) copy-start(bf16[1280,768]{1,0:T(8,128)(2,1)} %copy-done.23) | copy-start | bytes 5898244
  27.0 73.4 %collective-permute-start.9 = (bf16[768,768]{1,0:T(8,128)(2,1)}, bf16[768,768]{1,0:T(8,128)(2,1)}, u32[]{:S(2)}, u32[]{:S(2)}) collective-permute-start(bf16[768,768]{1,0:T(8,128)(2,1)} %constant_dynamic-slice_fusion.1), channel_id=1, source_target_pairs={{0,1},{1,0},{2,3},{3,2},{4,5},{5,4},{6,7},{7,6},{8,9},{9,8},{10,11... | collective-permute-start | bytes 3538952 | tf_op jit(solution)/shard_map/ppermute | solution.py:287
  38.2 7.4 %collective-permute-start.2 = (bf16[2,512,384]{2,1,0:T(8,128)(2,1)}, bf16[2,512,384]{2,1,0:T(8,128)(2,1)}, u32[]{:S(2)}, u32[]{:S(2)}) collective-permute-start(bf16[2,512,384]{2,1,0:T(8,128)(2,1)} %collective-permute-done.1), channel_id=1, source_target_pairs={{0,2},{2,0},{4,6},{6,4},{8,10},{10,8},{12,14},{14,12},{16,18},{18,... | collective-permute-start | bytes 2359304 | tf_op jit(solution)/shard_map/ppermute | solution.py:287
  43.7 54.0 %collective-permute-start.7 = (bf16[768,768]{1,0:T(8,128)(2,1)}, bf16[768,768]{1,0:T(8,128)(2,1)S(1)}, u32[]{:S(2)}, u32[]{:S(2)}) collective-permute-start(bf16[768,768]{1,0:T(8,128)(2,1)} %constant_dynamic-slice_fusion.2), channel_id=1, source_target_pairs={{0,1},{1,0},{2,3},{3,2},{4,5},{5,4},{6,7},{7,6},{8,9},{9,8},{10,11... | collective-permute-start | bytes 3538952 | tf_op jit(solution)/shard_map/ppermute | solution.py:287
  49.9 42.1 %copy-start.1 = (bf16[2048,384]{1,0:T(8,128)(2,1)}, bf16[2048,384]{1,0:T(8,128)(2,1)S(1)}, u32[]{:S(2)}) copy-start(bf16[2048,384]{1,0:T(8,128)(2,1)S(1)} %get-tuple-element.83.kp_ref) | copy-start | bytes 4718596
  91.9 11.5 %copy-start.2 = (bf16[1280,384]{1,0:T(8,128)(2,1)}, bf16[1280,384]{1,0:T(8,128)(2,1)S(1)}, u32[]{:S(2)}) copy-start(bf16[1280,384]{1,0:T(8,128)(2,1)S(1)} %get-tuple-element.29.o_ref) | copy-start | bytes 2949124
  91.9 10.1 %copy-start.12 = (bf16[1280,768]{1,0:T(8,128)(2,1)S(1)}, bf16[1280,768]{1,0:T(8,128)(2,1)}, u32[]{:S(2)}) copy-start(bf16[1280,768]{1,0:T(8,128)(2,1)} %param.25) | copy-start | bytes 5898244
  91.9 10.1 %copy-start.43 = (bf16[384,768]{1,0:T(8,128)(2,1)S(1)}, bf16[384,768]{1,0:T(8,128)(2,1)}, u32[]{:S(2)}) copy-start(bf16[384,768]{1,0:T(8,128)(2,1)} %param.40) | copy-start | bytes 1769476
  92.1 9.5 %collective-permute-start.3 = (bf16[640,384]{1,0:T(8,128)(2,1)S(1)}, bf16[640,384]{1,0:T(8,128)(2,1)S(1)}, u32[]{:S(2)}, u32[]{:S(2)}) collective-permute-start(bf16[640,384]{1,0:T(8,128)(2,1)S(1)} %get-tuple-element.92), channel_id=1, source_target_pairs={{0,1},{1,0},{2,3},{3,2},{4,5},{5,4},{6,7},{7,6},{8,9},{9,8},{10,11... | collective-permute-start | bytes 1474568 | tf_op jit(solution)/shard_map/ppermute | solution.py:287
  92.4 6.8 %collective-permute-start.6 = (bf16[192,768]{1,0:T(8,128)(2,1)}, bf16[192,768]{1,0:T(8,128)(2,1)S(1)}, u32[]{:S(2)}, u32[]{:S(2)}) collective-permute-start(bf16[192,768]{1,0:T(8,128)(2,1)} %collective-permute-done.5), channel_id=1, source_target_pairs={{0,2},{2,0},{4,6},{6,4},{8,10},{10,8},{12,14},{14,12},{16,18},{18,... | collective-permute-start | bytes 884744 | tf_op jit(solution)/shard_map/ppermute | solution.py:287
  97.8 5.7 %collective-permute-start.8 = (bf16[768,768]{1,0:T(8,128)(2,1)S(1)}, bf16[768,768]{1,0:T(8,128)(2,1)S(1)}, u32[]{:S(2)}, u32[]{:S(2)}) collective-permute-start(bf16[768,768]{1,0:T(8,128)(2,1)S(1)} %collective-permute-done.7), channel_id=1, source_target_pairs={{0,2},{2,0},{4,6},{6,4},{8,10},{10,8},{12,14},{14,12},{16,18},{18,... | collective-permute-start | bytes 3538952 | tf_op jit(solution)/shard_map/ppermute | solution.py:287
  100.4 29.7 %collective-permute-start.10 = (bf16[768,768]{1,0:T(8,128)(2,1)}, bf16[768,768]{1,0:T(8,128)(2,1)S(1)}, u32[]{:S(2)}, u32[]{:S(2)}) collective-permute-start(bf16[768,768]{1,0:T(8,128)(2,1)} %collective-permute-done.9), channel_id=1, source_target_pairs={{0,2},{2,0},{4,6},{6,4},{8,10},{10,8},{12,14},{14,12},{16,18},{18,... | collective-permute-start | bytes 3538952 | tf_op jit(solution)/shard_map/ppermute | solution.py:287
  103.4 3.2 copy-start.38
  104.5 25.6 %copy-start.21 = (bf16[768,1536]{1,0:T(8,128)(2,1)}, bf16[768,1536]{1,0:T(8,128)(2,1)S(1)}, u32[]{:S(2)}) copy-start(bf16[768,1536]{1,0:T(8,128)(2,1)S(1)} %maximum_select_fusion) | copy-start | bytes 7077892
  132.1 12.2 %copy-start.20 = (bf16[1536,768]{1,0:T(8,128)(2,1)}, bf16[1536,768]{1,0:T(8,128)(2,1)S(1)}, u32[]{:S(2)}) copy-start(bf16[1536,768]{1,0:T(8,128)(2,1)S(1)} %maximum_select_fusion.1) | copy-start | bytes 7077892
  144.3 10.0 %copy-start.22 = (bf16[768,1536]{1,0:T(8,128)(2,1)S(1)}, bf16[768,1536]{1,0:T(8,128)(2,1)}, u32[]{:S(2)}) copy-start(bf16[768,1536]{1,0:T(8,128)(2,1)} %copy-done.21) | copy-start | bytes 7077892
  144.3 10.0 %copy-start.27 = (f32[640,768]{1,0:T(8,128)S(1)}, f32[640,768]{1,0:T(8,128)}, u32[]{:S(2)}) copy-start(f32[640,768]{1,0:T(8,128)} %copy-done.26) | copy-start | bytes 5898244
  166.2 3.6 copy-start.66
  183.7 35.3 %copy-start.19 = (bf16[768,384]{1,0:T(8,128)(2,1)S(1)}, bf16[768,384]{1,0:T(8,128)(2,1)}, u32[]{:S(2)}) copy-start(bf16[768,384]{1,0:T(8,128)(2,1)} %get-tuple-element.85) | copy-start | bytes 1769476
  184.8 57.5 %collective-permute-start.13 = (bf16[640,384]{1,0:T(8,128)(2,1)}, bf16[640,384]{1,0:T(8,128)(2,1)}, u32[]{:S(2)}, u32[]{:S(2)}) collective-permute-start(bf16[640,384]{1,0:T(8,128)(2,1)} %get-tuple-element.90), channel_id=1, source_target_pairs={{0,1},{1,0},{2,3},{3,2},{4,5},{5,4},{6,7},{7,6},{8,9},{9,8},{10,11... | collective-permute-start | bytes 1474568 | tf_op jit(solution)/shard_map/ppermute | solution.py:287
  242.2 3.5 copy-start.5
  242.2 3.5 copy-start.8
  296.7 8.5 %collective-permute-start.14 = (bf16[2,2,512,384]{3,2,0,1:T(8,128)(2,1)S(1)}, bf16[2,2,512,384]{3,2,0,1:T(8,128)(2,1)S(1)}, u32[]{:S(2)}, u32[]{:S(2)}) collective-permute-start(bf16[2,2,512,384]{3,2,0,1:T(8,128)(2,1)S(1)} %slice.310), channel_id=1, source_target_pairs={{0,2},{2,0},{4,6},{6,4},{8,10},{10,8},{12,14},{14,12},{16,18},{18,... | collective-permute-start | bytes 4718600 | tf_op jit(solution)/shard_map/ppermute | solution.py:287
  305.6 54.0 %collective-permute-start.15 = (bf16[2,512,384]{2,1,0:T(8,128)(2,1)S(1)}, bf16[2,512,384]{2,1,0:T(8,128)(2,1)S(1)}, u32[]{:S(2)}, u32[]{:S(2)}) collective-permute-start(bf16[2,512,384]{2,1,0:T(8,128)(2,1)S(1)} %fusion.48), channel_id=1, source_target_pairs={{0,4},{2,6},{4,0},{6,2},{8,12},{10,14},{12,8},{14,10},{16,20},{18,... | collective-permute-start | bytes 2359304 | tf_op jit(solution)/shard_map/ppermute | solution.py:287
  328.4 31.5 %copy-start.35 = (bf16[768,384]{1,0:T(8,128)(2,1)S(1)}, bf16[768,384]{1,0:T(8,128)(2,1)}, u32[]{:S(2)}) copy-start(bf16[768,384]{1,0:T(8,128)(2,1)} %param.35) | copy-start | bytes 1769476
  363.8 44.3 %collective-permute-start.16 = (bf16[1280,768]{1,0:T(8,128)(2,1)}, bf16[1280,768]{1,0:T(8,128)(2,1)}, u32[]{:S(2)}, u32[]{:S(2)}) collective-permute-start(bf16[1280,768]{1,0:T(8,128)(2,1)} %fusion.22), channel_id=1, source_target_pairs={{0,1},{1,0},{2,3},{3,2},{4,5},{5,4},{6,7},{7,6},{8,9},{9,8},{10,11... | collective-permute-start | bytes 5898248 | tf_op jit(solution)/shard_map/ppermute | solution.py:287
  371.2 3.8 copy-start.25
  375.0 33.1 %copy-start.13 = (bf16[1280,768]{1,0:T(8,128)(2,1)S(1)}, bf16[1280,768]{1,0:T(8,128)(2,1)}, u32[]{:S(2)}) copy-start(bf16[1280,768]{1,0:T(8,128)(2,1)} %param.25) | copy-start | bytes 5898244
  375.0 33.1 %copy-start.46 = (f32[1280]{0:T(1024)S(1)}, f32[1280]{0:T(1024)}, u32[]{:S(2)}) copy-start(f32[1280]{0:T(1024)} %copy-done.45) | copy-start | bytes 15364
  375.0 33.1 %copy-start.48 = (f32[1280]{0:T(1024)S(1)}, f32[1280]{0:T(1024)}, u32[]{:S(2)}) copy-start(f32[1280]{0:T(1024)} %copy-done.47) | copy-start | bytes 15364
  375.0 33.1 %copy-start.50 = (f32[768]{0:T(1024)S(1)}, f32[768]{0:T(1024)}, u32[]{:S(2)}) copy-start(f32[768]{0:T(1024)} %copy-done.49) | copy-start | bytes 9220
  377.1 42.0 %copy-start.18 = (bf16[8,2,48,384]{3,2,0,1:T(8,128)(2,1)S(1)}, bf16[8,2,48,384]{3,2,0,1:T(8,128)(2,1)}, u32[]{:S(2)}) copy-start(bf16[8,2,48,384]{3,2,0,1:T(8,128)(2,1)} %copy.110) | copy-start | bytes 1769476
  377.1 42.0 %copy-start.32 = (bf16[8,2,48,1]{3,2,0,1:T(8,128)(2,1)S(1)}, bf16[8,2,48,1]{3,2,0,1:T(8,128)(2,1)}, u32[]{:S(2)}) copy-start(bf16[8,2,48,1]{3,2,0,1:T(8,128)(2,1)} %copy.113) | copy-start | bytes 4612
  377.1 42.0 %copy-start.33 = (bf16[8,2,48,1]{3,2,0,1:T(8,128)(2,1)S(1)}, bf16[8,2,48,1]{3,2,0,1:T(8,128)(2,1)}, u32[]{:S(2)}) copy-start(bf16[8,2,48,1]{3,2,0,1:T(8,128)(2,1)} %copy.114) | copy-start | bytes 4612
  426.2 10.6 %collective-permute-start.17 = (bf16[8,48,1280]{2,1,0:T(8,128)(2,1)}, bf16[8,48,1280]{2,1,0:T(8,128)(2,1)}, u32[]{:S(2)}, u32[]{:S(2)}) collective-permute-start(bf16[8,48,1280]{2,1,0:T(8,128)(2,1)} %dynamic-slice_bitcast_fusion), channel_id=1, source_target_pairs={{0,2},{2,0},{4,6},{6,4},{8,10},{10,8},{12,14},{14,12},{16,18},{18,... | collective-permute-start | bytes 2949128 | tf_op jit(solution)/shard_map/ppermute | solution.py:287
  435.1 7.3 %copy-start.15 = (bf16[640,768]{1,0:T(8,128)(2,1)S(1)}, bf16[640,768]{1,0:T(8,128)(2,1)}, u32[]{:S(2)}) copy-start(bf16[640,768]{1,0:T(8,128)(2,1)} %copy-done.14) | copy-start | bytes 2949124
  435.1 24.9 %collective-permute-start.11 = (bf16[640,768]{1,0:T(8,128)(2,1)}, bf16[640,768]{1,0:T(8,128)(2,1)}, u32[]{:S(2)}, u32[]{:S(2)}) collective-permute-start(bf16[640,768]{1,0:T(8,128)(2,1)} %add_convert_fusion.3), channel_id=1, source_target_pairs={{0,1},{1,0},{2,3},{3,2},{4,5},{5,4},{6,7},{7,6},{8,9},{9,8},{10,11... | collective-permute-start | bytes 2949128 | tf_op jit(solution)/shard_map/ppermute | solution.py:287
  440.3 23.7 %collective-permute-start.18 = (bf16[4,48,1280]{2,1,0:T(8,128)(2,1)}, bf16[4,48,1280]{2,1,0:T(8,128)(2,1)}, u32[]{:S(2)}, u32[]{:S(2)}) collective-permute-start(bf16[4,48,1280]{2,1,0:T(8,128)(2,1)} %dynamic-slice_bitcast_fusion.1), channel_id=1, source_target_pairs={{0,4},{2,6},{4,0},{6,2},{8,12},{10,14},{12,8},{14,10},{16,20},{18,... | collective-permute-start | bytes 1474568 | tf_op jit(solution)/shard_map/ppermute | solution.py:287
  442.4 21.6 %copy-start.17 = (bf16[8,48,1280]{2,1,0:T(8,128)(2,1)S(1)}, bf16[8,48,1280]{2,1,0:T(8,128)(2,1)}, u32[]{:S(2)}) copy-start(bf16[8,48,1280]{2,1,0:T(8,128)(2,1)} %copy-done.16) | copy-start | bytes 2949124
  442.4 25.1 %copy-start.53 = (f32[1280]{0:T(1024)S(1)}, f32[1280]{0:T(1024)}, u32[]{:S(2)}) copy-start(f32[1280]{0:T(1024)} %get-tuple-element.44) | copy-start | bytes 15364
  442.4 25.1 %copy-start.52 = (f32[1280]{0:T(1024)S(1)}, f32[1280]{0:T(1024)}, u32[]{:S(2)}) copy-start(f32[1280]{0:T(1024)} %get-tuple-element.47) | copy-start | bytes 15364
  442.4 38.1 %collective-permute-start.12 = (bf16[640,768]{1,0:T(8,128)(2,1)S(1)}, bf16[640,768]{1,0:T(8,128)(2,1)S(1)}, u32[]{:S(2)}, u32[]{:S(2)}) collective-permute-start(bf16[640,768]{1,0:T(8,128)(2,1)S(1)} %copy-done.15), channel_id=1, source_target_pairs={{0,1},{1,0},{2,3},{3,2},{4,5},{5,4},{6,7},{7,6},{8,9},{9,8},{10,11... | collective-permute-start | bytes 2949128 | tf_op jit(solution)/shard_map/ppermute | solution.py:287
  464.0 16.6 %copy-start.51 = (f32[768]{0:T(1024)S(1)}, f32[768]{0:T(1024)}, u32[]{:S(2)}) copy-start(f32[768]{0:T(1024)} %copy-done.49) | copy-start | bytes 9220
  465.2 7.8 %collective-permute-start.19 = (bf16[2,48,1280]{2,1,0:T(8,128)(2,1)S(1)}, bf16[2,48,1280]{2,1,0:T(8,128)(2,1)S(1)}, u32[]{:S(2)}, u32[]{:S(2)}) collective-permute-start(bf16[2,48,1280]{2,1,0:T(8,128)(2,1)S(1)} %dynamic-slice_bitcast_fusion.2), channel_id=1, source_target_pairs={{0,8},{2,10},{4,12},{6,14},{8,0},{10,2},{12,4},{14,6},{16,24},{18,... | collective-permute-start | bytes 737288 | tf_op jit(solution)/shard_map/ppermute | solution.py:287
  473.1 13.4 %collective-permute-start.20 = (bf16[1,48,1280]{2,1,0:T(8,128)(2,1)S(1)}, bf16[1,48,1280]{2,1,0:T(8,128)(2,1)S(1)}, u32[]{:S(2)}, u32[]{:S(2)}) collective-permute-start(bf16[1,48,1280]{2,1,0:T(8,128)(2,1)S(1)} %constant_dynamic-slice_fusion), channel_id=1, source_target_pairs={{0,16},{2,18},{4,20},{6,22},{8,24},{10,26},{12,28},{14,30},{16,0},... | collective-permute-start | bytes 368648 | tf_op jit(solution)/shard_map/ppermute | solution.py:287
  488.2 9.8 %collective-permute-start.21 = (bf16[48,3584]{1,0:T(8,128)(2,1)S(1)}, bf16[48,3584]{1,0:T(8,128)(2,1)S(1)}, u32[]{:S(2)}, u32[]{:S(2)}) collective-permute-start(bf16[48,3584]{1,0:T(8,128)(2,1)S(1)} %split.34), channel_id=1, source_target_pairs={{0,1},{1,0},{2,3},{3,2},{4,5},{5,4},{6,7},{7,6},{8,9},{9,8},{10,11... | collective-permute-start | bytes 1032200 | tf_op jit(solution)/shard_map/ppermute | solution.py:287
  (26 other events, 49.1 us)
Sparse Core Ops, SparseCore 0:
  242.3 152.4 reduce-scatter.1

commit v2 on v1

--- a/solution.py
+++ b/solution.py
@@ -278,9 +278,274 @@
     )(info, q, kp, vp, k, v, o, li, g, e)
 
 
+EPSILON = 1e-05
 D = 768
-FF = 3072
-EPSILON = 1e-05
+UCH = 512
+
+
+def polynomial(x, terms):
+    out = jnp.full_like(x, terms[0])
+    for term in terms[1:]:
+        out = out * x + term
+    return out
+
+
+def error_function(x):
+    x = jnp.clip(x, -3.832506856900711, 3.832506856900711)
+    square = x * x
+    top = polynomial(
+        square,
+        (0.00022905065861350646, 0.0034082910107109506, 0.050955695062380861, 0.18520832239976145, 1.128379143519084),
+    )
+    bottom = polynomial(
+        square,
+        (
+            -1.1791602954361697e-7,
+            0.000023547966471313185,
+            0.0010179625278914885,
+            0.014070470171167667,
+            0.11098505178285362,
+            0.49746925110067538,
+            1.0,
+        ),
+    )
+    return x * top / bottom
+
+
+def gelu_pair(v):
+    phi = 0.5 + 0.5 * error_function(v * 0.7071067811865476)
+    density = jnp.exp(-0.5 * v * v) * 0.3989422804014327
+    return v * phi, phi + v * density
+
+
+def column_sum(x):
+    return jnp.sum(x, axis=0, keepdims=True)
+
+
+def mid_kernel(
+    info, att_m, att_o, hid, cot, vec_u, vec_w, vec_d, w1_own, w1_got, w1_swap, w2_own, w2_got, w2_swap, wo_own, wo_got, wo_swap,
+    out_ref, gatt_m, gatt_o, gmix_ref, packed, su_ref, sw_ref, sd_ref,
+    w1, w2, wo, act_s, shp_s, dg_s, wide_s, acc_s, gmid_s, sub_s, mid_s, low_s, midt_s, cott_s, stage, sems, out_sems,
+):
+    core = info[0]
+    units = w1_own.shape[1]
+    width = wo_own.shape[0]
+    rows = hid.shape[0]
+    full = 2 * units
+    half = units // 2
+    half_w = width // 2
+    here_u = pl.multiple_of(units + core * half, 128)
+    there_u = pl.multiple_of(units + (1 - core) * half, 128)
+    here_w = pl.multiple_of(width + core * half_w, 64)
+    there_w = pl.multiple_of(width + (1 - core) * half_w, 64)
+    loads = []
+    for i, (src, dst) in enumerate(
+        [
+            (wo_own, wo.at[pl.ds(0, width), :]),
+            (wo_got, wo.at[pl.ds(here_w, half_w), :]),
+            (wo_swap, wo.at[pl.ds(there_w, half_w), :]),
+            (w1_own, w1.at[:, pl.ds(0, units)]),
+            (w1_got, w1.at[:, pl.ds(here_u, half)]),
+            (w1_swap, w1.at[:, pl.ds(there_u, half)]),
+            (w2_own, w2.at[pl.ds(0, units), :]),
+            (w2_got, w2.at[pl.ds(here_u, half), :]),
+            (w2_swap, w2.at[pl.ds(there_u, half), :]),
+        ]
+    ):
+        copy = pltpu.make_async_copy(src, dst, sems.at[i])
+        copy.start()
+        loads.append(copy)
+
+    a0 = att_m[...].astype(F32)
+    a1 = att_o[...].astype(F32)
+    center = (jnp.sum(a0, axis=1, keepdims=True) + jnp.sum(a1, axis=1, keepdims=True)) * (1.0 / D)
+    square = (jnp.sum(a0 * a0, axis=1, keepdims=True) + jnp.sum(a1 * a1, axis=1, keepdims=True)) * (1.0 / D)
+    sub_scale = lax.rsqrt(square - center * center + EPSILON)
+    sub_s[:, 0:width] = (a0 - center) * sub_scale
+    sub_s[:, width : 2 * width] = (a1 - center) * sub_scale
+    sub_gain = vec_w[0:1, :]
+    low_s[...] = (sub_s[...] * sub_gain + vec_w[1:2, :]).astype(BF)
+    for copy in loads[0:3]:
+        copy.wait()
+    mixed = hid[...].astype(F32) + (dot_nn(low_s[...], wo[...]) + vec_d[0:1, :])
+    wide_s[...] = mixed
+    mean = jnp.mean(mixed, axis=1, keepdims=True)
+    mid_scale = lax.rsqrt(jnp.mean(mixed * mixed, axis=1, keepdims=True) - mean * mean + EPSILON)
+    mid_s[...] = (mixed - mean) * mid_scale
+    mid_gain = vec_d[1:2, :]
+    mid_full = mid_s[...] * mid_gain + vec_d[2:3, :]
+    mid_low = mid_full.astype(BF)
+    midt_s[...] = jnp.transpose(mid_full).astype(BF)
+    cot_full = cot[...].astype(F32)
+    cott_s[...] = jnp.transpose(cot_full).astype(BF)
+    sd_ref[...] = jnp.zeros_like(sd_ref)
+    sd_ref[3:4, :] = column_sum(cot_full)
+    for copy in loads[3:6]:
+        copy.wait()
+
+    def lanes_sum(x):
+        total = x[:, 0:128]
+        for i in range(1, x.shape[1] // 128):
+            total = total + x[:, i * 128 : (i + 1) * 128]
+        return total
+
+    def first(c, carry):
+        at = pl.multiple_of(c * UCH, UCH)
+        inner = dot_nn(mid_low, w1[:, pl.ds(at, UCH)]) + vec_u[2:3, pl.ds(at, UCH)]
+        act, slope = gelu_pair(inner)
+        act_s[:, pl.ds(at, UCH)] = act
+        dg_s[:, pl.ds(at, UCH)] = slope.astype(BF)
+        return carry[0] + lanes_sum(act), carry[1] + lanes_sum(act * act)
+
+    zero = jnp.zeros((rows, 128), F32)
+    act_sum, act_square = lax.fori_loop(0, full // UCH, first, (zero, zero))
+    ffn_center = jnp.sum(act_sum, axis=1, keepdims=True) * (1.0 / full)
+    ffn_scale = lax.rsqrt(
+        jnp.sum(act_square, axis=1, keepdims=True) * (1.0 / full) - ffn_center * ffn_center + EPSILON
+    )
+    for copy in loads[6:9]:
+        copy.wait()
+    acc_s[...] = jnp.zeros_like(acc_s)
+    per = units // UCH
+    wide = 2 * units + width
+
+    def column_of(c, extra):
+        return pl.multiple_of((c // per) * wide + lax.rem(c, per) * UCH + extra, 128)
+
+    def send(slot, column):
+        return pltpu.make_async_copy(stage.at[slot], packed.at[:, pl.ds(column, UCH)], out_sems.at[slot])
+
+    def put(c, value, extra):
+        slot = lax.rem(c, 2)
+
+        @pl.when(c >= 2)
+        def _():
+            send(slot, column_of(c - 2, extra)).wait()
+
+        stage[slot] = value
+        send(slot, column_of(c, extra)).start()
+
+    def drain(extra):
+        for c in range(full // UCH - 2, full // UCH):
+            send(c % 2, column_of(c, extra)).wait()
+
+    def second(c, carry):
+        at = pl.multiple_of(c * UCH, UCH)
+        unit = (act_s[:, pl.ds(at, UCH)] - ffn_center) * ffn_scale
+        act_s[:, pl.ds(at, UCH)] = unit
+        gain = vec_u[0:1, pl.ds(at, UCH)]
+        low = (unit * gain + vec_u[1:2, pl.ds(at, UCH)]).astype(BF)
+        acc_s[...] += dot_nn(low, w2[pl.ds(at, UCH), :])
+        grad = dot_nt(cot[...], w2[pl.ds(at, UCH), :])
+        cross = grad * unit
+        su_ref[0:1, pl.ds(at, UCH)] = column_sum(cross)
+        su_ref[1:2, pl.ds(at, UCH)] = column_sum(grad)
+        shaped = grad * gain
+        shp_s[:, pl.ds(at, UCH)] = shaped
+        put(c, dot_nn(cott_s[...], low).astype(BF), units)
+        return carry[0] + lanes_sum(shaped), carry[1] + lanes_sum(shaped * unit)
+
+    su_ref[...] = jnp.zeros_like(su_ref)
+    s_sum, s_cross = lax.fori_loop(0, full // UCH, second, (zero, zero))
+    drain(units)
+    shaped_mean = jnp.sum(s_sum, axis=1, keepdims=True) * (1.0 / full)
+    cross_mean = jnp.sum(s_cross, axis=1, keepdims=True) * (1.0 / full)
+    out_ref[...] = (wide_s[...] + (acc_s[...] + vec_d[3:4, :])).astype(BF)
+    gmid_s[...] = jnp.zeros_like(gmid_s)
+
+    def third(c, carry):
+        at = pl.multiple_of(c * UCH, UCH)
+        g = ffn_scale * (shp_s[:, pl.ds(at, UCH)] - shaped_mean - act_s[:, pl.ds(at, UCH)] * cross_mean)
+        low = (g * dg_s[:, pl.ds(at, UCH)].astype(F32)).astype(BF)
+        su_ref[2:3, pl.ds(at, UCH)] = column_sum(low.astype(F32))
+        gmid_s[...] += dot_nt(low, w1[:, pl.ds(at, UCH)])
+        put(c, dot_nn(midt_s[...], low).astype(BF), 0)
+        return carry
+
+    lax.fori_loop(0, full // UCH, third, 0)
+    drain(0)
+
+    grad_mid = gmid_s[...]
+    unit = mid_s[...]
+    sd_ref[1:2, :] = column_sum(grad_mid * unit)
+    sd_ref[2:3, :] = column_sum(grad_mid)
+    shaped = grad_mid * mid_gain
+    grad_mixed = cot[...].astype(F32) + mid_scale * (
+        shaped - jnp.mean(shaped, axis=1, keepdims=True) - unit * jnp.mean(shaped * unit, axis=1, keepdims=True)
+    )
+    branch = grad_mixed.astype(BF)
+    gmix_ref[...] = branch
+    branch_f = branch.astype(F32)
+    sd_ref[0:1, :] = column_sum(branch_f)
+    out_grad = dot_nn(jnp.transpose(branch_f).astype(BF), low_s[...]).astype(BF)
+    stage[0, :, 0:width] = out_grad[:, 0:width]
+    stage[1, :, 0:width] = out_grad[:, width : 2 * width]
+    last = [
+        pltpu.make_async_copy(stage.at[i, :, pl.ds(0, width)], packed.at[:, pl.ds(i * wide + 2 * units, width)], out_sems.at[i])
+        for i in range(2)
+    ]
+    for copy in last:
+        copy.start()
+    grad_sub = dot_nt(branch, wo[...])
+    unit = sub_s[...]
+    cross = grad_sub * unit
+    sw_ref[...] = jnp.zeros_like(sw_ref)
+    sw_ref[0:1, :] = column_sum(cross)
+    sw_ref[1:2, :] = column_sum(grad_sub)
+    shaped = grad_sub * sub_gain
+    grad_att = sub_scale * (
+        shaped - jnp.mean(shaped, axis=1, keepdims=True) - unit * jnp.mean(shaped * unit, axis=1, keepdims=True)
+    )
+    gatt_m[...] = grad_att[:, 0:width].astype(BF)
+    gatt_o[...] = grad_att[:, width : 2 * width].astype(BF)
+    for copy in last:
+        copy.wait()
+
+
+def middle(core, att_m, att_o, hid, cot, vec_u, vec_w, vec_d, w1, w2, wo):
+    rows = hid.shape[0]
+    units = w1[0].shape[1]
+    width = wo[0].shape[0]
+    vmem = pl.BlockSpec(memory_space=pltpu.VMEM)
+    hbm = pl.BlockSpec(memory_space=pl.ANY)
+    shape = jax.ShapeDtypeStruct
+    return pl.pallas_call(
+        mid_kernel,
+        in_specs=[pl.BlockSpec(memory_space=pltpu.SMEM)] + [vmem] * 7 + [hbm] * 9,
+        out_specs=[vmem] * 4 + [hbm] + [vmem] * 3,
+        out_shape=[
+            shape((rows, D), BF),
+            shape((rows, width), BF),
+            shape((rows, width), BF),
+            shape((rows, D), BF),
+            shape((D, 2 * (2 * units + width)), BF),
+            shape((8, 2 * units), F32),
+            shape((8, 2 * width), F32),
+            shape((8, D), F32),
+        ],
+        scratch_shapes=[
+            pltpu.VMEM((D, 2 * units), BF),
+            pltpu.VMEM((2 * units, D), BF),
+            pltpu.VMEM((2 * width, D), BF),
+            pltpu.VMEM((rows, 2 * units), F32),
+            pltpu.VMEM((rows, 2 * units), F32),
+            pltpu.VMEM((rows, 2 * units), BF),
+            pltpu.VMEM((rows, D), F32),
+            pltpu.VMEM((rows, D), F32),
+            pltpu.VMEM((rows, D), F32),
+            pltpu.VMEM((rows, 2 * width), F32),
+            pltpu.VMEM((rows, D), F32),
+            pltpu.VMEM((rows, 2 * width), BF),
+            pltpu.VMEM((D, rows), BF),
+            pltpu.VMEM((D, rows), BF),
+            pltpu.VMEM((2, D, UCH), BF),
+            pltpu.SemaphoreType.DMA((9,)),
+            pltpu.SemaphoreType.DMA((2,)),
+        ],
+        compiler_params=pltpu.CompilerParams(vmem_limit_bytes=62 << 20),
+        cost_estimate=pl.CostEstimate(flops=21 * 10**9, bytes_accessed=30 * 10**6, transcendentals=0),
+        name="middle",
+    )(core, att_m, att_o, hid, cot, vec_u, vec_w, vec_d, *w1, *w2, *wo)
 
 
 def flip(value, axis, bit):
@@ -297,10 +562,6 @@
 
 def dense(left, right):
     return jnp.dot(left, right, preferred_element_type=F32)
-
-
-def exact_gelu(values):
-    return jax.nn.gelu(values, approximate=False)
 
 
 def norm_rows(values, gain, bias):
@@ -330,9 +591,8 @@
 
 def fetch(weight, core, axis):
     half = weight.shape[axis] // 2
-    sent = lax.dynamic_slice_in_dim(weight, core * half, half, axis)
-    got = flip(sent, "tensor", 0)
-    return in_order(core, got, flip(got, "dp", 0), axis)
+    got = flip(lax.dynamic_slice_in_dim(weight, core * half, half, axis), "tensor", 0)
+    return (got, flip(got, "dp", 0))
 
 
 def halving(value, device):
@@ -420,20 +680,15 @@
         axis=1,
     ).reshape(-1)
 
-    inner_other = fetch(inner_weight, core, 1)
-    outer_other = fetch(outer_weight, core, 0)
-    out_other = fetch(out_weight, core, 0)
-    vectors = jnp.concatenate([inner_bias, ffn_gain, ffn_bias, sub_gain, sub_bias])
+    inner_parts = (inner_weight,) + fetch(inner_weight, core, 1)
+    outer_parts = (outer_weight,) + fetch(outer_weight, core, 0)
+    out_parts = (out_weight,) + fetch(out_weight, core, 0)
+    vectors = jnp.concatenate([ffn_gain, ffn_bias, inner_bias, sub_gain, sub_bias])
     vectors_other = flip(vectors, "tensor", 0)
-    splits = [units, 2 * units, 3 * units, 3 * units + width]
-    ib_o, fg_o, fb_o, sg_o, sb_o = jnp.split(vectors_other, splits)
-    both = lambda mine, other: jnp.concatenate([mine, other]).astype(F32)
-    inner_bias_f = both(inner_bias, ib_o)
-    ffn_gain_f, ffn_bias_f = both(ffn_gain, fg_o), both(ffn_bias, fb_o)
-    sub_gain_f, sub_bias_f = both(sub_gain, sg_o), both(sub_bias, sb_o)
-    inner_all = jnp.concatenate([inner_weight, inner_other], axis=1)
-    outer_all = jnp.concatenate([outer_weight, outer_other], axis=0)
-    out_all = jnp.concatenate([out_weight, out_other], axis=0)
+    both = jnp.stack([vectors, vectors_other]).astype(F32)
+    vec_u = both[:, : 3 * units].reshape(2, 3, units).swapaxes(0, 1).reshape(3, 2 * units)
+    vec_w = both[:, 3 * units :].reshape(2, 2, width).swapaxes(0, 1).reshape(2, 2 * width)
+    vec_d = jnp.stack([out_bias, mid_gain, mid_bias, outer_bias]).astype(F32)
 
     inputs = hidden_in.astype(F32)
     pre_gain_f = pre_gain.astype(F32)
@@ -453,92 +708,21 @@
     other_at = (1 - tensor_id) * half
     att_mine = lax.dynamic_slice_in_dim(attended, own_at, half)
     att_got = flip(lax.dynamic_slice_in_dim(attended, other_at, half), "tensor", 0)
-    att_rows = jnp.concatenate([att_mine, att_got], axis=1).astype(F32)
-    hidden_rows = lax.dynamic_slice_in_dim(hidden_in, own_at, half).astype(F32)
+    hidden_rows = lax.dynamic_slice_in_dim(hidden_in, own_at, half)
     cot_rows = lax.dynamic_slice_in_dim(cotangent, own_at, half)
-
-    sub_normed, sub_unit, sub_scale = norm_rows(att_rows, sub_gain_f, sub_bias_f)
-    sub_low = sub_normed.astype(BF)
-    mixed = hidden_rows + (dense(sub_low, out_all) + out_bias.astype(F32))
-    mid_gain_f = mid_gain.astype(F32)
-    mid_normed, mid_unit, mid_scale = norm_rows(mixed, mid_gain_f, mid_bias.astype(F32))
-    mid_low = mid_normed.astype(BF)
-    inner = dense(mid_low, inner_all) + inner_bias_f
-    activated = exact_gelu(inner)
-    ffn_normed, ffn_unit, ffn_scale = norm_rows(activated, ffn_gain_f, ffn_bias_f)
-    ffn_low = ffn_normed.astype(BF)
-    outer = dense(ffn_low, outer_all)
-    out_half = (mixed + (outer + outer_bias.astype(F32))).astype(BF)
-
-    grad_result = cot_rows.astype(F32)
-    outer_bias_grad = jnp.sum(grad_result, axis=0)
-    outer_t_grad = contract_rows(cot_rows, ffn_low)
-    grad_ffn = back_project(cot_rows, outer_all)
-    ffn_gain_grad = jnp.sum(grad_ffn * ffn_unit, axis=0)
-    ffn_bias_grad = jnp.sum(grad_ffn, axis=0)
-    grad_activated = norm_back(grad_ffn, ffn_gain_f, ffn_unit, ffn_scale)
-    _, gelu_back = jax.vjp(exact_gelu, inner)
-    grad_inner = gelu_back(grad_activated)[0].astype(BF)
-    inner_bias_grad = jnp.sum(grad_inner.astype(F32), axis=0)
-    inner_grad = contract_rows(mid_low, grad_inner)
-    grad_mid = back_project(grad_inner, inner_all)
-    mid_gain_grad = jnp.sum(grad_mid * mid_unit, axis=0)
-    mid_bias_grad = jnp.sum(grad_mid, axis=0)
-    grad_mixed = grad_result + norm_back(grad_mid, mid_gain_f, mid_unit, mid_scale)
-    grad_branch = grad_mixed.astype(BF)
-    out_bias_grad = jnp.sum(grad_branch.astype(F32), axis=0)
-    out_t_grad = contract_rows(grad_branch, sub_low)
-    grad_sub = back_project(grad_branch, out_all)
-    sub_gain_grad = jnp.sum(grad_sub * sub_unit, axis=0)
-    sub_bias_grad = jnp.sum(grad_sub, axis=0)
-    grad_att = norm_back(grad_sub, sub_gain_f, sub_unit, sub_scale).astype(BF)
-
-    grad_mine = grad_att[:, :width]
-    grad_got = flip(grad_att[:, width:], "tensor", 0)
+    out_half, grad_mine, grad_theirs, grad_mixed_low, packed, sum_u, sum_w, sum_d = middle(
+        core[None].astype(jnp.int32), att_mine, att_got, hidden_rows, cot_rows, vec_u, vec_w, vec_d, inner_parts, outer_parts, out_parts
+    )
+
+    grad_got = flip(grad_theirs, "tensor", 0)
     grad_attended = in_order(tensor_id, grad_mine, grad_got, 0)
 
-    def columns(vector):
-        per = vector.shape[0] // ranks
-        block = D // ranks
-        count = -(-per // block)
-        padded = jnp.pad(vector.reshape(ranks, per), ((0, 0), (0, count * block - per)))
-        return padded.reshape(ranks, count, block).swapaxes(1, 2).reshape(D, count)
-
-    def vector_of(cols, per):
-        return cols.T.reshape(-1)[:per]
-
-    shared = [out_bias_grad, mid_gain_grad, mid_bias_grad, outer_bias_grad]
-
-    def pack(at, at_w):
-        parts = [inner_grad[:, at : at + units], outer_t_grad[:, at : at + units], out_t_grad[:, at_w : at_w + width]]
-        small = [v[at : at + units] for v in (ffn_gain_grad, ffn_bias_grad, inner_bias_grad)]
-        small = small + [v[at_w : at_w + width] for v in (sub_gain_grad, sub_bias_grad)] + shared
-        cols = [columns(v) for v in small]
-        used = sum(c.shape[1] for c in cols)
-        fill = -(-used // 128) * 128 - used
-        return jnp.concatenate([p.astype(BF) for p in parts + cols] + [jnp.zeros((D, fill), BF)], axis=1)
-
-    early = lax.psum_scatter(
-        jnp.concatenate([pack(0, 0), pack(units, width)], axis=1), "dp", scatter_dimension=0, tiled=True
-    )
+    early = lax.psum_scatter(packed, "dp", scatter_dimension=0, tiled=True)
     early_mine, early_other = jnp.split(early, 2, axis=1)
     early_sum = early_mine.astype(F32) + flip(early_other, "tensor", 0).astype(F32)
-    big = 2 * units + width
     inner_weight_grad = early_sum[:, :units]
     outer_weight_grad = early_sum[:, units : 2 * units].T
-    out_weight_grad = early_sum[:, 2 * units : big].T
-    tail = early_sum[:, big:]
-    block = D // ranks
-    per_u, per_w = units // ranks, width // ranks
-    cu, cw = -(-per_u // block), -(-per_w // block)
-    ffn_gain_grad = vector_of(tail[:, 0:cu], per_u)
-    ffn_bias_grad = vector_of(tail[:, cu : 2 * cu], per_u)
-    inner_bias_grad = vector_of(tail[:, 2 * cu : 3 * cu], per_u)
-    sub_gain_grad = vector_of(tail[:, 3 * cu : 3 * cu + cw], per_w)
-    sub_bias_grad = vector_of(tail[:, 3 * cu + cw : 3 * cu + 2 * cw], per_w)
-    out_bias_grad, mid_gain_grad, mid_bias_grad, outer_bias_grad = [
-        tail[:, 3 * cu + 2 * cw + i] for i in range(4)
-    ]
+    out_weight_grad = early_sum[:, 2 * units :].T
 
     output = in_order(tensor_id, out_half, flip(out_half, "tensor", 0), 0)
 
@@ -565,32 +749,51 @@
     grad_normed = grad_normed_low.astype(F32) + flip(grad_normed_low, "tensor", 0).astype(F32)
     pre_gain_grad = jnp.sum(grad_normed * pre_unit, axis=0)
     pre_bias_grad = jnp.sum(grad_normed, axis=0)
-    grad_mixed_low = grad_mixed.astype(BF)
     grad_mixed_all = in_order(tensor_id, grad_mixed_low, flip(grad_mixed_low, "tensor", 0), 0).astype(F32)
     input_low = (grad_mixed_all + norm_back(grad_normed, pre_gain_f, pre_unit, pre_scale)).astype(BF)
 
-    cols = [columns(v) for v in (query_bias_grad, value_bias_grad, pre_gain_grad, pre_bias_grad)]
-    used = sum(c.shape[1] for c in cols)
-    fill = -(-used // 128) * 128 - used
+    per_u, per_w, per_d = units // ranks, width // ranks, D // ranks
+    vec = jnp.concatenate(
+        [
+            sum_u[:3].reshape(3, 2, ranks, per_u).transpose(2, 1, 0, 3).reshape(ranks, 6 * per_u),
+            sum_w[:2].reshape(2, 2, ranks, per_w).transpose(2, 1, 0, 3).reshape(ranks, 4 * per_w),
+            sum_d[:4].reshape(4, ranks, per_d).swapaxes(0, 1).reshape(ranks, 4 * per_d),
+            jnp.stack([query_bias_grad, value_bias_grad]).reshape(2, ranks, per_w).swapaxes(0, 1).reshape(ranks, 2 * per_w),
+            jnp.stack([pre_gain_grad, pre_bias_grad]).reshape(2, ranks, per_d).swapaxes(0, 1).reshape(ranks, 2 * per_d),
+        ],
+        axis=1,
+    )
+    count = vec.shape[1]
+    block = D // ranks
+    vec = jnp.pad(vec, ((0, 0), (0, block * 128 - count))).reshape(D, 128)
     late = halving(
         jnp.concatenate(
-            [p.astype(BF) for p in [query_weight_grad, key_weight_grad, value_weight_grad] + cols]
-            + [jnp.zeros((D, fill), BF)],
-            axis=1,
+            [p.astype(BF) for p in (query_weight_grad, key_weight_grad, value_weight_grad, vec)], axis=1
         ),
         device,
-    ).astype(F32)
-    tail = late[:, 3 * width :]
+    )
+    vec = late[:, 3 * width :].reshape(-1)[:count]
+    late = late[:, : 3 * width].astype(F32)
+    at_w = 6 * per_u
+    at_d = at_w + 4 * per_w
+    at_late = at_d + 4 * per_d
+    got = flip(vec[:at_late], "tensor", 0).astype(F32)
+    vec = vec.astype(F32)
+    ffn_gain_grad, ffn_bias_grad, inner_bias_grad = (vec[: 3 * per_u] + got[3 * per_u : at_w]).reshape(3, per_u)
+    sub_gain_grad, sub_bias_grad = (vec[at_w : at_w + 2 * per_w] + got[at_w + 2 * per_w : at_d]).reshape(2, per_w)
+    out_bias_grad, mid_gain_grad, mid_bias_grad, outer_bias_grad = (vec[at_d:at_late] + got[at_d:]).reshape(4, per_d)
+    query_bias_grad, value_bias_grad = vec[at_late : at_late + 2 * per_w].reshape(2, per_w)
+    pre_gain_grad, pre_bias_grad = vec[at_late + 2 * per_w :].reshape(2, per_d)
     return (
         output,
         input_low,
-        tail[:, 2 * cw],
-        tail[:, 2 * cw + 1],
+        pre_gain_grad,
+        pre_bias_grad,
         late[:, :width],
-        vector_of(tail[:, 0:cw], per_w),
+        query_bias_grad,
         late[:, width : 2 * width],
         late[:, 2 * width : 3 * width],
-        vector_of(tail[:, cw : 2 * cw], per_w),
+        value_bias_grad,
         sub_gain_grad,
         sub_bias_grad,
         out_weight_grad,
@@ -604,7 +807,6 @@
         outer_weight_grad,
         outer_bias_grad,
     )
-
 
 def solution(mesh):
     placed = (

time: 518 us -> 456 us (0.88)
  matrix products: 79.3 us -> 18.7 us
  Pallas kernels: 88.6 us -> 140 us
  local copies, waits for them, and re-layouts: 112 us -> 68.8 us
  other arithmetic: 52.8 us -> 40.2 us
  waiting for transfers between devices: 107 us -> 119 us
  starting transfers between devices: 55.2 us -> 47.4 us
    pallas_call x0 -> x1, Pallas kernels: none -> 51.7 us  [middle(): pl.pallas_call(mid_kernel, in_specs=[pl.BlockSpec(memory_space=pltpu.SMEM...]
    dot_general x6 -> x3, matrix products: 37.6 us -> 5.12 us  [dense(): return jnp.dot(left, right, preferred_element_type=F32)]
    convert_element_type x20 -> x0, local copies, waits for them, and re-layouts: 25.8 us -> none  [pack(): p.astype(BF)]
    concatenate x6 -> x3, local copies, waits for them, and re-layouts: 30.8 us -> 5.5 us  [the longest x1 3.97 us: body(): jnp.concatenate([p.astype(BF) for p in (query_weight_grad, key_weight_gra...]
    dot_general x6 -> x3, matrix products: 24.5 us -> 4.95 us  [back_project(): lax.dot_general(left, right, (((1,), (1,)), ((), ())), preferred_element_...]
    reduce_sum x2 -> x0, other arithmetic: 12 us -> none  [the longest x1 9.96 us: body(): inner_bias_grad = jnp.sum(grad_inner.astype(F32), axis=0)]
    ppermute x22 -> x23, waiting for transfers between devices: 107 us -> 119 us  [flip(): lax.ppermute(value, axis, [(i, i ^ 1 << bit) for i in range(lax.axis_size...]
    another operation x1 -> x14, local copies, waits for them, and re-layouts: 0.71 us -> 10.5 us  [the longest x4 5.05 us: body(): vec_d = jnp.stack([out_bias, mid_gain, mid_bias, outer_bias]).astype(F32)]
  transfers between devices with their start and end apart: 23 -> 24, of which waited for: 10 -> 13; matrix products, arithmetic and copies ran while one was open for 32% -> 25% of each run, Pallas kernels for 17% -> 20%
where the time goes in v2:
time: 456 us; the launch traced here: 450 us
  Pallas kernels  140 us (31%)
  waiting for transfers between devices  119 us (26%)
  local copies, waits for them, and re-layouts  68.8 us (15%)
  starting transfers between devices  47.4 us (10%)
  other arithmetic  40.2 us (9%)
  matrix products  18.7 us (4%)
  between operations  16.2 us (4%)
    ppermute x23, waiting for transfers between devices, flip(): lax.ppermute(value, axis, [(i, i ^ 1 << bit) for i in range(lax.axis_size...  119 us
    pallas_call x1, Pallas kernels, middle(): pl.pallas_call(mid_kernel, in_specs=[pl.BlockSpec(memory_space=pltpu.SMEM...  51.7 us
    ppermute x23, starting transfers between devices, flip(): lax.ppermute(value, axis, [(i, i ^ 1 << bit) for i in range(lax.axis_size...  47.4 us
    pallas_call x1, Pallas kernels, attend_back(): pl.pallas_call(bwd_kernel, grid_spec=pltpu.PrefetchScalarGridSpec(num_sca...  47.2 us
    pallas_call x1, Pallas kernels, attend(): pl.pallas_call(fwd_kernel, grid_spec=pltpu.PrefetchScalarGridSpec(num_sca...  41.2 us
    unnamed x104, local copies, waits for them, and re-layouts  15.7 us
  transfers between devices with their start and end apart: 24, of which 13 were waited for; matrix products, arithmetic and copies ran while one was open for 25% of the time, Pallas kernels for 20%

profile of v2, /device:TPU:0, one launch (start us, length us, event | category | flops | bytes accessed | tf_op | source)
XLA Modules:
  0.0 450.2 jit_solution(18381830608022009085)
XLA Ops:
  7.3 2.3 convert_reduce_fusion
  16.3 2.9 collective-permute-start.1
  19.2 2.5 constant_dynamic-slice_fusion.3
  21.7 1.5 collective-permute-start.5
  24.9 1.6 dynamic-update-slice
  26.5 1.5 dynamic-update-slice.1
  28.0 1.4 dynamic-update-slice.2
  29.4 1.4 dynamic-update-slice.3
  30.9 1.4 dynamic-update-slice.4
  32.3 1.5 collective-permute-start.4
  35.1 1.3 copy.72
  49.3 1.4 maximum_convert_fusion.1.vec_d
  50.6 2.6 constant_dynamic-slice_fusion.4
  58.5 17.5 %collective-permute-done.4 = bf16[5376]{0:T(1024)(128)(2,1)} collective-permute-done((bf16[5376]{0:T(1024)(128)(2,1)}, bf16[5376]{0:T(1024)(128)(2,1)}, u32[]{:S(2)}, u32[]{:S(2)}) %collective-permute-start.4) | collective-permute-done | bytes 10784 | tf_op jit(solution)/shard_map/ppermute | solution.py:552
  76.0 1.5 collective-permute-start.9
  77.5 2.7 fusion.20.q_ref
  81.0 3.6 collective-permute-done.9.wo_got
  85.2 2.6 pad_maximum_fusion
  87.9 1.5 slice_bitcast_fusion.1
  89.4 41.2 %attend.1 = (bf16[1280,384]{1,0:T(8,128)(2,1)S(1)}, bf16[6,1280,2304]{2,1,0:T(8,128)(2,1)}, f32[1280,384]{1,0:T(8,128)}) custom-call(s32[7]{0:T(128)S(1)} %pad_add_fusion.info, f32[30]{0:T(128)S(1)} %reshape.219.tab, bf16[1280,384]{1,0:T(8,128)(2,1)S(1)} %fusion.20.q_ref, bf16[2048,384]{1,0:T(8,128)(2,1)S(1)} %get-tuple-element.60.kp_ref, ...), custom_call_target="tpu_custom_call" | custom-call | flops 16000000000 | bytes 60000000 | tf_op jit(solution)/shard_map/attend/pallas_call | solution.py:162
  131.6 1.5 collective-permute-start.3
  134.4 6.5 %collective-permute-done.3.att_o = bf16[640,384]{1,0:T(8,128)(2,1)S(1)} collective-permute-done((bf16[640,384]{1,0:T(8,128)(2,1)S(1)}, bf16[640,384]{1,0:T(8,128)(2,1)S(1)}, u32[]{:S(2)}, u32[]{:S(2)}) %collective-permute-start.3) | collective-permute-done | bytes 491552 | tf_op jit(solution)/shard_map/ppermute | solution.py:552
  141.7 51.7 %middle.1 = (bf16[640,768]{1,0:T(8,128)(2,1)}, bf16[640,384]{1,0:T(8,128)(2,1)}, bf16[640,384]{1,0:T(8,128)(2,1)}, bf16[640,768]{1,0:T(8,128)(2,1)}, bf16[768,69...) custom-call(s32[1]{0:T(128)} %bitcast.info, ...), custom_call_target="tpu_custom_call" | custom-call | flops 20999999488 | bytes 30000000 | tf_op jit(solution)/shard_map/middle/pallas_call | solution.py:512
  193.4 1.6 collective-permute-start.13
  195.0 9.0 %collective-permute-done.13 = bf16[640,384]{1,0:T(8,128)(2,1)S(1)} collective-permute-done((bf16[640,384]{1,0:T(8,128)(2,1)}, bf16[640,384]{1,0:T(8,128)(2,1)S(1)}, u32[]{:S(2)}, u32[]{:S(2)}) %collective-permute-start.13) | collective-permute-done | bytes 491552 | tf_op jit(solution)/shard_map/ppermute | solution.py:552
  205.4 47.2 %attend_back.1 = (bf16[1280,384]{1,0:T(8,128)(2,1)S(1)}, bf16[2048,384]{1,0:T(8,128)(2,1)}, bf16[2048,384]{1,0:T(8,128)(2,1)}, bf16[1280,384]{1,0:T(8,128)(2,1)S(1)}, bf16[1280,384]{1,0:T(8,128)(2,1)S(1)}) custom-call(s32[7]{0:T(128)S(1)} %pad_add_fusion.info, bf16[1280,384]{1,0:T(8,128)(2,1)S(1)} %copy-done.9, bf16[2048,384]{1,0:T(8,128)(2,1)} %copy-done.1, ...), custom_call_target="tpu_custom_call" | custom-call | flops 30000001024 | bytes 60000000 | tf_op jit(solution)/shard_map/attend_back/pallas_call | solution.py:259
  252.6 2.2 pad_maximum_fusion.1
  255.0 6.2 %collective-permute-start.14 = (bf16[2,2,512,384]{3,2,0,1:T(8,128)(2,1)S(1)}, bf16[2,2,512,384]{3,2,0,1:T(8,128)(2,1)S(1)}, u32[]{:S(2)}, u32[]{:S(2)}) collective-permute-start(bf16[2,2,512,384]{3,2,0,1:T(8,128)(2,1)S(1)} %slice.154), channel_id=1, source_target_pairs={{0,2},{2,0},{4,6},{6,4},{8,10},{10,8},{12,14},{14,12},{16,18},{18,... | collective-permute-start | bytes 4718600 | tf_op jit(solution)/shard_map/ppermute | solution.py:552
  261.2 3.0 collective-permute-done.14
  264.6 20.2 %collective-permute-start.15 = (bf16[2,512,384]{2,1,0:T(8,128)(2,1)S(1)}, bf16[2,512,384]{2,1,0:T(8,128)(2,1)S(1)}, u32[]{:S(2)}, u32[]{:S(2)}) collective-permute-start(bf16[2,512,384]{2,1,0:T(8,128)(2,1)S(1)} %fusion.25), channel_id=1, source_target_pairs={{0,4},{2,6},{4,0},{6,2},{8,12},{10,14},{12,8},{14,10},{16,20},{18,... | collective-permute-start | bytes 2359304 | tf_op jit(solution)/shard_map/ppermute | solution.py:552
  286.8 25.0 %collective-permute-done.15 = bf16[2,512,384]{2,1,0:T(8,128)(2,1)S(1)} collective-permute-done((bf16[2,512,384]{2,1,0:T(8,128)(2,1)S(1)}, bf16[2,512,384]{2,1,0:T(8,128)(2,1)S(1)}, u32[]{:S(2)}, u32[]{:S(2)}) %collective-permute-start.15) | collective-permute-done | bytes 786464 | tf_op jit(solution)/shard_map/ppermute | solution.py:552
  314.0 2.5 fusion.16
  316.5 1.4 collective-permute-start.16
  317.9 1.5 slice.233
  319.4 1.4 reshape.224
  320.9 1.4 copy.81
  322.2 1.5 reshape.225
  323.7 1.3 slice.234
  325.0 1.4 reshape.228
  326.4 1.3 copy.82
  327.7 1.4 reshape.229
  330.5 1.4 reshape.226
  331.8 1.3 copy.83
  333.2 1.4 reshape.227
  335.3 1.4 stack.93
  336.7 3.4 convolution_convert_fusion.3
  341.6 3.5 convolution_convert_fusion.2
  345.1 1.8 convolution_convert_fusion.1
  346.9 14.6 %collective-permute-done.16 = bf16[1280,768]{1,0:T(8,128)(2,1)} collective-permute-done((bf16[1280,768]{1,0:T(8,128)(2,1)}, bf16[1280,768]{1,0:T(8,128)(2,1)}, u32[]{:S(2)}, u32[]{:S(2)}) %collective-permute-start.16) | collective-permute-done | bytes 1966112 | tf_op jit(solution)/shard_map/ppermute | solution.py:552
  361.5 4.7 %fusion.12 = (bf16[768]{0:T(1024)(128)(2,1)S(1)}, f32[1280]{0:T(1024)}, f32[1280]{0:T(1024)}, bf16[768]{0:T(1024)(128)(2,1)S(1)}) fusion(bf16[1280,768]{1,0:T(8,128)(2,1)S(1)} %copy-done.11, bf16[1280,768]{1,0:T(8,128)(2,1)} %collective-permute-done.16, bf16[1280,768]{1,0:T(8,128)(2,1)} %fusion.16, f32[1280]{0:T(1024)S(1)} %get-tuple-element.74, ...), kind=kLoop, calls=%fused_computation.17 | loop fusion | flops 12775424 | bytes 5924864 | tf_op jit(solution)/shard_map/reduce_sum | solution.py:750
  366.9 2.6 pad_maximum_fusion.2
  369.5 4.0 copy.65
  374.9 1.5 collective-permute-start.11
  377.5 1.7 fusion.21
  380.4 1.5 collective-permute-start.12
  381.9 17.9 %collective-permute-done.11 = bf16[640,768]{1,0:T(8,128)(2,1)} collective-permute-done((bf16[640,768]{1,0:T(8,128)(2,1)}, bf16[640,768]{1,0:T(8,128)(2,1)}, u32[]{:S(2)}, u32[]{:S(2)}) %collective-permute-start.11) | collective-permute-done | bytes 983072 | tf_op jit(solution)/shard_map/ppermute | solution.py:552
  399.8 3.8 maximum_select_fusion
  405.0 7.0 %collective-permute-done.19 = bf16[2,48,1280]{2,1,0:T(8,128)(2,1)S(1)} collective-permute-done((bf16[2,48,1280]{2,1,0:T(8,128)(2,1)S(1)}, bf16[2,48,1280]{2,1,0:T(8,128)(2,1)S(1)}, u32[]{:S(2)}, u32[]{:S(2)}) %collective-permute-start.19) | collective-permute-done | bytes 245792 | tf_op jit(solution)/shard_map/ppermute | solution.py:552
  412.2 1.5 collective-permute-start.20
  413.6 6.7 %collective-permute-done.12 = bf16[640,768]{1,0:T(8,128)(2,1)S(1)} collective-permute-done((bf16[640,768]{1,0:T(8,128)(2,1)}, bf16[640,768]{1,0:T(8,128)(2,1)S(1)}, u32[]{:S(2)}, u32[]{:S(2)}) %collective-permute-start.12) | collective-permute-done | bytes 983072 | tf_op jit(solution)/shard_map/ppermute | solution.py:552
  420.3 5.9 %fusion.11 = bf16[1280,768]{1,0:T(8,128)(2,1)} fusion(bf16[1280,768]{1,0:T(8,128)(2,1)S(1)} %copy-done.11, bf16[1280,768]{1,0:T(8,128)(2,1)} %collective-permute-done.16, bf16[1280,768]{1,0:T(8,128)(2,1)} %fusion.16, bf16[640,768]{1,0:T(8,128)(2,1)S(1)} %collective-permute-done.12, bf16[640,768]{1,0:T(8,128)(2,1)S(1)} %copy-done.18, ...), kind=kLoop, calls=%fused_computation.16 | loop fusion | flops 22609920 | bytes 9853953 | tf_op jit(solution)/shard_map/convert_element_type | solution.py:753
  426.3 1.5 collective-permute-start.21
  432.3 1.5 collective-permute-start.22
  434.9 5.6 %collective-permute-done.22 = bf16[48,3456]{1,0:T(8,128)(2,1)S(1)} collective-permute-done((bf16[48,3456]{1,0:T(8,128)(2,1)S(1)}, bf16[48,3456]{1,0:T(8,128)(2,1)S(1)}, u32[]{:S(2)}, u32[]{:S(2)}) %collective-permute-start.22) | collective-permute-done | bytes 331808 | tf_op jit(solution)/shard_map/ppermute | solution.py:552
  (211 shorter events, 54.3 us)
Async XLA Ops:
  7.2 70.3 %copy-start = (bf16[768,384]{1,0:T(8,128)(2,1)S(1)}, bf16[768,384]{1,0:T(8,128)(2,1)}, u32[]{:S(2)}) copy-start(bf16[768,384]{1,0:T(8,128)(2,1)} %param.33) | copy-start | bytes 1769476
  7.2 2.5 copy-start.10
  7.2 2.4 copy-start.41
  7.2 2.4 copy-start.42
  7.2 2.5 copy-start.43
  7.2 424.0 %reduce-scatter.2.cloned.1.call-start = ((), (), s32[]{:S(2)}) async-start(), calls=%async_computation.1 | async-start | bytes 11280384 | tf_op jit(solution)/shard_map/reduce_scatter | solution.py:720
  10.8 1.5 copy-start.21
  12.3 77.1 %copy-start.3 = (bf16[1280,384]{1,0:T(8,128)(2,1)}, bf16[1280,384]{1,0:T(8,128)(2,1)S(1)}, u32[]{:S(2)}) copy-start(bf16[1280,384]{1,0:T(8,128)(2,1)S(1)} %convolution_convert_fusion.ko_ref) | copy-start | bytes 2949124
  14.6 1.7 copy-start.14
  16.3 37.0 %collective-permute-start.1 = (bf16[2,512,384]{2,1,0:T(8,128)(2,1)}, bf16[2,512,384]{2,1,0:T(8,128)(2,1)}, u32[]{:S(2)}, u32[]{:S(2)}) collective-permute-start(bf16[2,512,384]{2,1,0:T(8,128)(2,1)} %pad_maximum_fusion.5), channel_id=1, source_target_pairs={{0,4},{2,6},{4,0},{6,2},{8,12},{10,14},{12,8},{14,10},{16,20},{18,... | collective-permute-start | bytes 2359304 | tf_op jit(solution)/shard_map/ppermute | solution.py:552
  19.2 66.0 %collective-permute-start = (bf16[2,512,384]{2,1,0:T(8,128)(2,1)}, bf16[2,512,384]{2,1,0:T(8,128)(2,1)}, u32[]{:S(2)}, u32[]{:S(2)}) collective-permute-start(bf16[2,512,384]{2,1,0:T(8,128)(2,1)} %pad_maximum_fusion.5), channel_id=1, source_target_pairs={{0,2},{2,0},{4,6},{6,4},{8,10},{10,8},{12,14},{14,12},{16,18},{18,... | collective-permute-start | bytes 2359304 | tf_op jit(solution)/shard_map/ppermute | solution.py:552
  19.2 4.0 copy-start.23
  21.7 62.9 %collective-permute-start.5 = (bf16[768,768]{1,0:T(8,128)(2,1)}, bf16[768,768]{1,0:T(8,128)(2,1)}, u32[]{:S(2)}, u32[]{:S(2)}) collective-permute-start(bf16[768,768]{1,0:T(8,128)(2,1)} %constant_dynamic-slice_fusion.3), channel_id=1, source_target_pairs={{0,1},{1,0},{2,3},{3,2},{4,5},{5,4},{6,7},{7,6},{8,9},{9,8},{10,11... | collective-permute-start | bytes 3538952 | tf_op jit(solution)/shard_map/ppermute | solution.py:552
  24.4 60.7 %collective-permute-start.7 = (bf16[768,768]{1,0:T(8,128)(2,1)}, bf16[768,768]{1,0:T(8,128)(2,1)}, u32[]{:S(2)}, u32[]{:S(2)}) collective-permute-start(bf16[768,768]{1,0:T(8,128)(2,1)} %constant_dynamic-slice_fusion.2), channel_id=1, source_target_pairs={{0,1},{1,0},{2,3},{3,2},{4,5},{5,4},{6,7},{7,6},{8,9},{9,8},{10,11... | collective-permute-start | bytes 3538952 | tf_op jit(solution)/shard_map/ppermute | solution.py:552
  32.3 43.7 %collective-permute-start.4 = (bf16[5376]{0:T(1024)(128)(2,1)}, bf16[5376]{0:T(1024)(128)(2,1)}, u32[]{:S(2)}, u32[]{:S(2)}) collective-permute-start(bf16[5376]{0:T(1024)(128)(2,1)} %dynamic-update-slice.4), channel_id=1, source_target_pairs={{0,1},{1,0},{2,3},{3,2},{4,5},{5,4},{6,7},{7,6},{8,9},{9,8},{10,11... | collective-permute-start | bytes 32264 | tf_op jit(solution)/shard_map/ppermute | solution.py:552
  50.6 2.6 copy-start.33
  50.6 2.6 copy-start.34
  50.6 2.7 copy-start.37
  50.6 2.7 copy-start.38
  53.3 31.9 %collective-permute-start.2 = (bf16[2,512,384]{2,1,0:T(8,128)(2,1)}, bf16[2,512,384]{2,1,0:T(8,128)(2,1)S(1)}, u32[]{:S(2)}, u32[]{:S(2)}) collective-permute-start(bf16[2,512,384]{2,1,0:T(8,128)(2,1)} %collective-permute-done.1), channel_id=1, source_target_pairs={{0,2},{2,0},{4,6},{6,4},{8,10},{10,8},{12,14},{14,12},{16,18},{18,... | collective-permute-start | bytes 2359304 | tf_op jit(solution)/shard_map/ppermute | solution.py:552
  58.5 26.8 %copy-start.13 = (bf16[1,512,384]{2,1,0:T(8,128)(2,1)S(1)}, bf16[1,512,384]{2,1,0:T(8,128)(2,1)}, u32[]{:S(2)}) copy-start(bf16[1,512,384]{2,1,0:T(8,128)(2,1)} %copy-done.12) | copy-start | bytes 1179652
  58.5 26.8 %copy-start.15 = (bf16[1,512,384]{2,1,0:T(8,128)(2,1)S(1)}, bf16[1,512,384]{2,1,0:T(8,128)(2,1)}, u32[]{:S(2)}) copy-start(bf16[1,512,384]{2,1,0:T(8,128)(2,1)} %copy-done.14) | copy-start | bytes 1179652
  76.0 8.6 %collective-permute-start.9 = (bf16[192,768]{1,0:T(8,128)(2,1)S(1)}, bf16[192,768]{1,0:T(8,128)(2,1)S(1)}, u32[]{:S(2)}, u32[]{:S(2)}) collective-permute-start(bf16[192,768]{1,0:T(8,128)(2,1)S(1)} %constant_dynamic-slice_fusion.1), channel_id=1, source_target_pairs={{0,1},{1,0},{2,3},{3,2},{4,5},{5,4},{6,7},{7,6},{8,9},{9,8},{10,11... | collective-permute-start | bytes 884744 | tf_op jit(solution)/shard_map/ppermute | solution.py:552
  80.2 9.1 %copy-start.8 = (bf16[1280,384]{1,0:T(8,128)(2,1)}, bf16[1280,384]{1,0:T(8,128)(2,1)S(1)}, u32[]{:S(2)}) copy-start(bf16[1280,384]{1,0:T(8,128)(2,1)S(1)} %fusion.20.q_ref) | copy-start | bytes 2949124
  84.6 3.3 copy-start.45
  84.6 49.8 %collective-permute-start.10 = (bf16[192,768]{1,0:T(8,128)(2,1)S(1)}, bf16[192,768]{1,0:T(8,128)(2,1)S(1)}, u32[]{:S(2)}, u32[]{:S(2)}) collective-permute-start(bf16[192,768]{1,0:T(8,128)(2,1)S(1)} %collective-permute-done.9.wo_got), channel_id=1, source_target_pairs={{0,2},{2,0},{4,6},{6,4},{8,10},{10,8},{12,14},{14,12},{16,18},{18,... | collective-permute-start | bytes 884744 | tf_op jit(solution)/shard_map/ppermute | solution.py:552
  84.6 57.1 %collective-permute-start.6 = (bf16[768,768]{1,0:T(8,128)(2,1)}, bf16[768,768]{1,0:T(8,128)(2,1)}, u32[]{:S(2)}, u32[]{:S(2)}) collective-permute-start(bf16[768,768]{1,0:T(8,128)(2,1)} %collective-permute-done.5.w1_got), channel_id=1, source_target_pairs={{0,2},{2,0},{4,6},{6,4},{8,10},{10,8},{12,14},{14,12},{16,18},{18,... | collective-permute-start | bytes 3538952 | tf_op jit(solution)/shard_map/ppermute | solution.py:552
  85.1 56.6 %collective-permute-start.8 = (bf16[768,768]{1,0:T(8,128)(2,1)}, bf16[768,768]{1,0:T(8,128)(2,1)}, u32[]{:S(2)}, u32[]{:S(2)}) collective-permute-start(bf16[768,768]{1,0:T(8,128)(2,1)} %collective-permute-done.7.w2_got), channel_id=1, source_target_pairs={{0,2},{2,0},{4,6},{6,4},{8,10},{10,8},{12,14},{14,12},{16,18},{18,... | collective-permute-start | bytes 3538952 | tf_op jit(solution)/shard_map/ppermute | solution.py:552
  87.9 1.5 copy-start.6
  89.4 41.2 %copy-start.1 = (bf16[2048,384]{1,0:T(8,128)(2,1)}, bf16[2048,384]{1,0:T(8,128)(2,1)S(1)}, u32[]{:S(2)}) copy-start(bf16[2048,384]{1,0:T(8,128)(2,1)S(1)} %get-tuple-element.60.kp_ref) | copy-start | bytes 4718596
  130.6 62.8 %copy-start.2 = (bf16[1280,384]{1,0:T(8,128)(2,1)}, bf16[1280,384]{1,0:T(8,128)(2,1)S(1)}, u32[]{:S(2)}) copy-start(bf16[1280,384]{1,0:T(8,128)(2,1)S(1)} %get-tuple-element.37.o_ref) | copy-start | bytes 2949124
  131.6 9.3 %collective-permute-start.3 = (bf16[640,384]{1,0:T(8,128)(2,1)S(1)}, bf16[640,384]{1,0:T(8,128)(2,1)S(1)}, u32[]{:S(2)}, u32[]{:S(2)}) collective-permute-start(bf16[640,384]{1,0:T(8,128)(2,1)S(1)} %get-tuple-element.63), channel_id=1, source_target_pairs={{0,1},{1,0},{2,3},{3,2},{4,5},{5,4},{6,7},{7,6},{8,9},{9,8},{10,11... | collective-permute-start | bytes 1474568 | tf_op jit(solution)/shard_map/ppermute | solution.py:552
  134.4 7.3 %copy-start.46 = (bf16[192,768]{1,0:T(8,128)(2,1)}, bf16[192,768]{1,0:T(8,128)(2,1)S(1)}, u32[]{:S(2)}) copy-start(bf16[192,768]{1,0:T(8,128)(2,1)S(1)} %collective-permute-done.10.wo_swap) | copy-start | bytes 884740
  193.4 10.6 %collective-permute-start.13 = (bf16[640,384]{1,0:T(8,128)(2,1)}, bf16[640,384]{1,0:T(8,128)(2,1)S(1)}, u32[]{:S(2)}, u32[]{:S(2)}) collective-permute-start(bf16[640,384]{1,0:T(8,128)(2,1)} %get-tuple-element.42), channel_id=1, source_target_pairs={{0,1},{1,0},{2,3},{3,2},{4,5},{5,4},{6,7},{7,6},{8,9},{9,8},{10,11... | collective-permute-start | bytes 1474568 | tf_op jit(solution)/shard_map/ppermute | solution.py:552
  195.0 9.1 %copy-start.25 = (bf16[640,384]{1,0:T(8,128)(2,1)S(1)}, bf16[640,384]{1,0:T(8,128)(2,1)}, u32[]{:S(2)}) copy-start(bf16[640,384]{1,0:T(8,128)(2,1)} %get-tuple-element.41) | copy-start | bytes 1474564
  195.0 10.4 %copy-start.9 = (bf16[1280,384]{1,0:T(8,128)(2,1)S(1)}, bf16[1280,384]{1,0:T(8,128)(2,1)}, u32[]{:S(2)}) copy-start(bf16[1280,384]{1,0:T(8,128)(2,1)} %copy-done.8) | copy-start | bytes 2949124
  195.0 10.3 %copy-start.4 = (bf16[1280,384]{1,0:T(8,128)(2,1)S(1)}, bf16[1280,384]{1,0:T(8,128)(2,1)}, u32[]{:S(2)}) copy-start(bf16[1280,384]{1,0:T(8,128)(2,1)} %copy-done.3) | copy-start | bytes 2949124
  195.0 10.3 %copy-start.7 = (bf16[1280,384]{1,0:T(8,128)(2,1)S(1)}, bf16[1280,384]{1,0:T(8,128)(2,1)}, u32[]{:S(2)}) copy-start(bf16[1280,384]{1,0:T(8,128)(2,1)} %copy-done.5) | copy-start | bytes 2949124
  255.0 9.2 %collective-permute-start.14 = (bf16[2,2,512,384]{3,2,0,1:T(8,128)(2,1)S(1)}, bf16[2,2,512,384]{3,2,0,1:T(8,128)(2,1)S(1)}, u32[]{:S(2)}, u32[]{:S(2)}) collective-permute-start(bf16[2,2,512,384]{3,2,0,1:T(8,128)(2,1)S(1)} %slice.154), channel_id=1, source_target_pairs={{0,2},{2,0},{4,6},{6,4},{8,10},{10,8},{12,14},{14,12},{16,18},{18,... | collective-permute-start | bytes 4718600 | tf_op jit(solution)/shard_map/ppermute | solution.py:552
  264.6 47.2 %collective-permute-start.15 = (bf16[2,512,384]{2,1,0:T(8,128)(2,1)S(1)}, bf16[2,512,384]{2,1,0:T(8,128)(2,1)S(1)}, u32[]{:S(2)}, u32[]{:S(2)}) collective-permute-start(bf16[2,512,384]{2,1,0:T(8,128)(2,1)S(1)} %fusion.25), channel_id=1, source_target_pairs={{0,4},{2,6},{4,0},{6,2},{8,12},{10,14},{12,8},{14,10},{16,20},{18,... | collective-permute-start | bytes 2359304 | tf_op jit(solution)/shard_map/ppermute | solution.py:552
  286.8 25.9 %copy-start.20 = (bf16[768,384]{1,0:T(8,128)(2,1)S(1)}, bf16[768,384]{1,0:T(8,128)(2,1)}, u32[]{:S(2)}) copy-start(bf16[768,384]{1,0:T(8,128)(2,1)} %param.35) | copy-start | bytes 1769476
  316.5 45.0 %collective-permute-start.16 = (bf16[1280,768]{1,0:T(8,128)(2,1)}, bf16[1280,768]{1,0:T(8,128)(2,1)}, u32[]{:S(2)}, u32[]{:S(2)}) collective-permute-start(bf16[1280,768]{1,0:T(8,128)(2,1)} %fusion.16), channel_id=1, source_target_pairs={{0,1},{1,0},{2,3},{3,2},{4,5},{5,4},{6,7},{7,6},{8,9},{9,8},{10,11... | collective-permute-start | bytes 5898248 | tf_op jit(solution)/shard_map/ppermute | solution.py:552
  336.7 3.4 copy-start.39
  336.7 3.4 copy-start.40
  341.6 3.5 copy-start.17
  345.1 16.5 %copy-start.11 = (bf16[1280,768]{1,0:T(8,128)(2,1)S(1)}, bf16[1280,768]{1,0:T(8,128)(2,1)}, u32[]{:S(2)}) copy-start(bf16[1280,768]{1,0:T(8,128)(2,1)} %param.25) | copy-start | bytes 5898244
  345.1 16.5 %copy-start.28 = (f32[768]{0:T(1024)S(1)}, f32[768]{0:T(1024)}, u32[]{:S(2)}) copy-start(f32[768]{0:T(1024)} %copy-done.27) | copy-start | bytes 9220
  346.9 19.6 %copy-start.26 = (bf16[16,576]{1,0:T(8,128)(2,1)S(1)}, bf16[16,576]{1,0:T(8,128)(2,1)}, u32[]{:S(2)}) copy-start(bf16[16,576]{1,0:T(8,128)(2,1)} %reshape.225) | copy-start | bytes 55300
  346.9 19.6 %copy-start.32 = (bf16[16,192]{1,0:T(8,128)(2,1)S(1)}, bf16[16,192]{1,0:T(8,128)(2,1)}, u32[]{:S(2)}) copy-start(bf16[16,192]{1,0:T(8,128)(2,1)} %reshape.229) | copy-start | bytes 18436
  346.9 19.6 %copy-start.35 = (bf16[16,96]{1,0:T(8,128)(2,1)S(1)}, bf16[16,96]{1,0:T(8,128)(2,1)}, u32[]{:S(2)}) copy-start(bf16[16,96]{1,0:T(8,128)(2,1)} %reshape.227) | copy-start | bytes 9220
  346.9 19.6 %copy-start.36 = (bf16[16,48]{1,0:T(8,128)(2,1)S(1)}, bf16[16,48]{1,0:T(8,128)(2,1)}, u32[]{:S(2)}) copy-start(bf16[16,48]{1,0:T(8,128)(2,1)} %reshape.230) | copy-start | bytes 4612
  346.9 20.0 %copy-start.24 = (bf16[768,384]{0,1:T(8,128)(2,1)S(1)}, bf16[768,384]{0,1:T(8,128)(2,1)}, u32[]{:S(2)}) copy-start(bf16[768,384]{0,1:T(8,128)(2,1)} %convolution_convert_fusion.3) | copy-start | bytes 1769476
  374.8 2.8 collective-permute-start.17
  374.9 24.9 %collective-permute-start.11 = (bf16[640,768]{1,0:T(8,128)(2,1)}, bf16[640,768]{1,0:T(8,128)(2,1)}, u32[]{:S(2)}, u32[]{:S(2)}) collective-permute-start(bf16[640,768]{1,0:T(8,128)(2,1)} %get-tuple-element.38), channel_id=1, source_target_pairs={{0,1},{1,0},{2,3},{3,2},{4,5},{5,4},{6,7},{7,6},{8,9},{9,8},{10,11... | collective-permute-start | bytes 2949128 | tf_op jit(solution)/shard_map/ppermute | solution.py:552
  380.1 23.6 %collective-permute-start.18 = (bf16[4,48,1280]{2,1,0:T(8,128)(2,1)}, bf16[4,48,1280]{2,1,0:T(8,128)(2,1)}, u32[]{:S(2)}, u32[]{:S(2)}) collective-permute-start(bf16[4,48,1280]{2,1,0:T(8,128)(2,1)} %dynamic-slice_bitcast_fusion.1), channel_id=1, source_target_pairs={{0,4},{2,6},{4,0},{6,2},{8,12},{10,14},{12,8},{14,10},{16,20},{18,... | collective-permute-start | bytes 1474568 | tf_op jit(solution)/shard_map/ppermute | solution.py:552
  380.4 39.9 %collective-permute-start.12 = (bf16[640,768]{1,0:T(8,128)(2,1)}, bf16[640,768]{1,0:T(8,128)(2,1)S(1)}, u32[]{:S(2)}, u32[]{:S(2)}) collective-permute-start(bf16[640,768]{1,0:T(8,128)(2,1)} %get-tuple-element.39), channel_id=1, source_target_pairs={{0,1},{1,0},{2,3},{3,2},{4,5},{5,4},{6,7},{7,6},{8,9},{9,8},{10,11... | collective-permute-start | bytes 2949128 | tf_op jit(solution)/shard_map/ppermute | solution.py:552
  403.6 1.4 copy-start.31
  403.6 1.4 copy-start.30
  403.6 16.7 %copy-start.18 = (bf16[640,768]{1,0:T(8,128)(2,1)S(1)}, bf16[640,768]{1,0:T(8,128)(2,1)}, u32[]{:S(2)}) copy-start(bf16[640,768]{1,0:T(8,128)(2,1)} %get-tuple-element.39) | copy-start | bytes 2949124
  403.6 16.7 %copy-start.29 = (f32[768]{0:T(1024)S(1)}, f32[768]{0:T(1024)}, u32[]{:S(2)}) copy-start(f32[768]{0:T(1024)} %copy-done.27) | copy-start | bytes 9220
  404.9 7.1 %collective-permute-start.19 = (bf16[2,48,1280]{2,1,0:T(8,128)(2,1)S(1)}, bf16[2,48,1280]{2,1,0:T(8,128)(2,1)S(1)}, u32[]{:S(2)}, u32[]{:S(2)}) collective-permute-start(bf16[2,48,1280]{2,1,0:T(8,128)(2,1)S(1)} %dynamic-slice_bitcast_fusion.2), channel_id=1, source_target_pairs={{0,8},{2,10},{4,12},{6,14},{8,0},{10,2},{12,4},{14,6},{16,24},{18,... | collective-permute-start | bytes 737288 | tf_op jit(solution)/shard_map/ppermute | solution.py:552
  412.2 14.1 %collective-permute-start.20 = (bf16[1,48,1280]{2,1,0:T(8,128)(2,1)S(1)}, bf16[1,48,1280]{2,1,0:T(8,128)(2,1)S(1)}, u32[]{:S(2)}, u32[]{:S(2)}) collective-permute-start(bf16[1,48,1280]{2,1,0:T(8,128)(2,1)S(1)} %constant_dynamic-slice_fusion), channel_id=1, source_target_pairs={{0,16},{2,18},{4,20},{6,22},{8,24},{10,26},{12,28},{14,30},{16,0},... | collective-permute-start | bytes 368648 | tf_op jit(solution)/shard_map/ppermute | solution.py:552
  426.3 3.7 collective-permute-start.21
  432.3 8.3 %collective-permute-start.22 = (bf16[48,3456]{1,0:T(8,128)(2,1)S(1)}, bf16[48,3456]{1,0:T(8,128)(2,1)S(1)}, u32[]{:S(2)}, u32[]{:S(2)}) collective-permute-start(bf16[48,3456]{1,0:T(8,128)(2,1)S(1)} %split.9), channel_id=1, source_target_pairs={{0,1},{1,0},{2,3},{3,2},{4,5},{5,4},{6,7},{7,6},{8,9},{9,8},{10,11... | collective-permute-start | bytes 995336 | tf_op jit(solution)/shard_map/ppermute | solution.py:552
  (7 other events, 7.0 us)
Sparse Core Ops, SparseCore 0:
  195.1 142.7 reduce-scatter.1

commit v3 on v2

--- a/solution.py
+++ b/solution.py
@@ -1,3 +1,5 @@
+import functools
+
 import jax
 import jax.numpy as jnp
 from jax import lax
@@ -277,6 +279,8 @@
         name="attend_back",
     )(info, q, kp, vp, k, v, o, li, g, e)
 
+MESH = pl.DeviceIdType.MESH
+
 
 EPSILON = 1e-05
 D = 768
@@ -323,9 +327,9 @@
 
 
 def mid_kernel(
-    info, att_m, att_o, hid, cot, vec_u, vec_w, vec_d, w1_own, w1_got, w1_swap, w2_own, w2_got, w2_swap, wo_own, wo_got, wo_swap,
-    out_ref, gatt_m, gatt_o, gmix_ref, packed, su_ref, sw_ref, sd_ref,
-    w1, w2, wo, act_s, shp_s, dg_s, wide_s, acc_s, gmid_s, sub_s, mid_s, low_s, midt_s, cott_s, stage, sems, out_sems,
+    info, att_m, att_o, hid, cot, vec_own, vec_got, vec_d, w1_own, w1_got, w1_swap, w2_own, w2_got, w2_swap, wo_own, wo_got, wo_swap,
+    out_ref, gatt_m, gatt_o, gmix_ref, packed, su_ref, sw_ref, sd_ref, ext_ref,
+    vec_u, vec_w, w1, w2, wo, act_s, shp_s, dg_s, wide_s, acc_s, gmid_s, sub_s, mid_s, low_s, midt_s, cott_s, stage, sems, out_sems,
 ):
     core = info[0]
     units = w1_own.shape[1]
@@ -356,6 +360,13 @@
         copy.start()
         loads.append(copy)
 
+    for i in range(3):
+        for j, vec in enumerate((vec_own, vec_got)):
+            vec_u[i : i + 1, pl.ds(j * units, units)] = vec[0:1, pl.ds(i * units, units)]
+    for i in range(2):
+        for j, vec in enumerate((vec_own, vec_got)):
+            vec_w[i : i + 1, pl.ds(j * width, width)] = vec[0:1, pl.ds(3 * units + i * width, width)]
+
     a0 = att_m[...].astype(F32)
     a1 = att_o[...].astype(F32)
     center = (jnp.sum(a0, axis=1, keepdims=True) + jnp.sum(a1, axis=1, keepdims=True)) * (1.0 / D)
@@ -367,13 +378,13 @@
     low_s[...] = (sub_s[...] * sub_gain + vec_w[1:2, :]).astype(BF)
     for copy in loads[0:3]:
         copy.wait()
-    mixed = hid[...].astype(F32) + (dot_nn(low_s[...], wo[...]) + vec_d[0:1, :])
+    mixed = hid[...].astype(F32) + (dot_nn(low_s[...], wo[...]) + vec_d[0:1, pl.ds(0, D)])
     wide_s[...] = mixed
     mean = jnp.mean(mixed, axis=1, keepdims=True)
     mid_scale = lax.rsqrt(jnp.mean(mixed * mixed, axis=1, keepdims=True) - mean * mean + EPSILON)
     mid_s[...] = (mixed - mean) * mid_scale
-    mid_gain = vec_d[1:2, :]
-    mid_full = mid_s[...] * mid_gain + vec_d[2:3, :]
+    mid_gain = vec_d[0:1, pl.ds(768, D)]
+    mid_full = mid_s[...] * mid_gain + vec_d[0:1, pl.ds(1536, D)]
     mid_low = mid_full.astype(BF)
     midt_s[...] = jnp.transpose(mid_full).astype(BF)
     cot_full = cot[...].astype(F32)
@@ -450,7 +461,7 @@
     drain(units)
     shaped_mean = jnp.sum(s_sum, axis=1, keepdims=True) * (1.0 / full)
     cross_mean = jnp.sum(s_cross, axis=1, keepdims=True) * (1.0 / full)
-    out_ref[...] = (wide_s[...] + (acc_s[...] + vec_d[3:4, :])).astype(BF)
+    out_ref[...] = (wide_s[...] + (acc_s[...] + vec_d[0:1, pl.ds(2304, D)])).astype(BF)
     gmid_s[...] = jnp.zeros_like(gmid_s)
 
     def third(c, carry):
@@ -498,11 +509,36 @@
     )
     gatt_m[...] = grad_att[:, 0:width].astype(BF)
     gatt_o[...] = grad_att[:, width : 2 * width].astype(BF)
+    parts = ext_ref.shape[0]
+    if parts > 1:
+        sums_u, sums_w, sums_d = su_ref[...], sw_ref[...], sd_ref[...]
+        for i in range(parts):
+            ext_ref[i] = jnp.concatenate(
+                [
+                    window(sums_u, i * (units // parts)),
+                    window(sums_u, units + i * (units // parts)),
+                    window(sums_w, i * (width // parts)),
+                    window(sums_w, width + i * (width // parts)),
+                    window(sums_d, i * (D // parts)),
+                    jnp.zeros((8, 128), F32),
+                ],
+                axis=0,
+            ).astype(BF)
     for copy in last:
         copy.wait()
 
 
-def middle(core, att_m, att_o, hid, cot, vec_u, vec_w, vec_d, w1, w2, wo):
+def window(rows8, start):
+    base = start // 128 * 128
+    size = min(256, rows8.shape[1] - base)
+    view = rows8[:, base : base + size]
+    shift = start - base
+    if shift:
+        view = pltpu.roll(view, size - shift, 1)
+    return view[:, 0:128]
+
+
+def middle(core, att_m, att_o, hid, cot, vec_own, vec_got, vec_d, w1, w2, wo, parts):
     rows = hid.shape[0]
     units = w1[0].shape[1]
     width = wo[0].shape[0]
@@ -512,7 +548,7 @@
     return pl.pallas_call(
         mid_kernel,
         in_specs=[pl.BlockSpec(memory_space=pltpu.SMEM)] + [vmem] * 7 + [hbm] * 9,
-        out_specs=[vmem] * 4 + [hbm] + [vmem] * 3,
+        out_specs=[vmem] * 4 + [hbm] + [vmem] * 4,
         out_shape=[
             shape((rows, D), BF),
             shape((rows, width), BF),
@@ -522,8 +558,11 @@
             shape((8, 2 * units), F32),
             shape((8, 2 * width), F32),
             shape((8, D), F32),
+            shape((parts, 48, 128), BF),
         ],
         scratch_shapes=[
+            pltpu.VMEM((8, 2 * units), F32),
+            pltpu.VMEM((8, 2 * width), F32),
             pltpu.VMEM((D, 2 * units), BF),
             pltpu.VMEM((2 * units, D), BF),
             pltpu.VMEM((2 * width, D), BF),
@@ -545,7 +584,251 @@
         compiler_params=pltpu.CompilerParams(vmem_limit_bytes=62 << 20),
         cost_estimate=pl.CostEstimate(flops=21 * 10**9, bytes_accessed=30 * 10**6, transcendentals=0),
         name="middle",
-    )(core, att_m, att_o, hid, cot, vec_u, vec_w, vec_d, *w1, *w2, *wo)
+    )(core, att_m, att_o, hid, cot, vec_own, vec_got, vec_d, *w1, *w2, *wo)
+
+
+def bit_peer(device, bit):
+    step = 1 << bit
+    return device + (1 - 2 * ((device // step) % 2)) * step
+
+
+def greet(peers):
+    barrier = pltpu.get_barrier_semaphore()
+    for peer in peers:
+        pl.semaphore_signal(barrier, inc=1, device_id=peer, device_id_type=MESH)
+    pl.semaphore_wait(barrier, len(peers))
+
+
+def final_kernel(
+    bits, hid, gain, bias, dq, dk, dv, wq, wk, wv, gmix, ext, kp, vp,
+    gin, late_out, vec_out,
+    near_s, loc_s, relay_s, far_s, unit_s, mine_s, norm_s, send_c, recv_c, send_p, recv_p, give_c, give_p, late_s, small_s,
+    vec_s, vec_r, sems_a, sems_b, loc_sems, *stage_refs,
+):
+    device = lax.axis_index("dp")
+    side = lax.axis_index("tensor")
+    across = {"dp": device, "tensor": 1 - side}
+    peers = [{"dp": bit_peer(device, b), "tensor": side} for b in range(bits)]
+    rows, width = dq.shape
+    prompt = kp.shape[0] // GDEV
+    conts = rows - prompt
+    half_p, half_c = prompt // 2, conts // 2
+    own_p = pl.multiple_of(side * half_p, 128)
+    their_p = pl.multiple_of((1 - side) * half_p, 128)
+    own_c = pl.multiple_of(prompt + side * half_c, 128)
+    their_c = pl.multiple_of(prompt + (1 - side) * half_c, 128)
+    lanes = 3 * width + 128
+
+    greet(peers + [across])
+    count = [0]
+
+    def remote(src, dst, peer):
+        i = count[0]
+        count[0] += 1
+        copy = pltpu.make_async_remote_copy(
+            src_ref=src, dst_ref=dst, send_sem=sems_a.at[i], recv_sem=sems_b.at[i], device_id=peer, device_id_type=MESH
+        )
+        copy.start()
+        return copy
+
+    first = []
+    for i, part in enumerate((kp, vp)):
+        first.append(remote(part.at[pl.ds(3 * prompt, prompt), :], near_s.at[2 * i + 1], peers[0]))
+        first.append(remote(part.at[pl.ds(prompt, prompt), :], near_s.at[2 * i], peers[0]))
+    local = []
+    for i, part in enumerate((kp, vp)):
+        for j in range(2):
+            copy = pltpu.make_async_copy(part.at[pl.ds(2 * j * prompt, prompt), :], loc_s.at[2 * i + j], loc_sems.at[2 * i + j])
+            copy.start()
+            local.append(copy)
+
+    gain_f = gain[...]
+    bias_f = bias[...]
+
+    def unit_rows(at, size):
+        x = hid[pl.ds(at, size), :].astype(F32)
+        center = jnp.mean(x, axis=1, keepdims=True)
+        scale = lax.rsqrt(jnp.mean(x * x, axis=1, keepdims=True) - center * center + EPSILON)
+        return (x - center) * scale, scale
+
+    def part_of(at, size, k_rows, v_rows):
+        return dot_nt(dq[pl.ds(at, size), :], wq[...]) + dot_nt(k_rows, wk[...]) + dot_nt(v_rows, wv[...])
+
+    def gather(part, unit):
+        return column_sum(part * unit), column_sum(part)
+
+    unit, _ = unit_rows(their_c, half_c)
+    part = part_of(their_c, half_c, dk[pl.ds(their_c, half_c), :], dv[pl.ds(their_c, half_c), :])
+    send_c[...] = part.astype(BF)
+    y_cont = remote(send_c, recv_c, across)
+    gain_grad, bias_grad = gather(part, unit)
+    norm_s[:, pl.ds(their_c, half_c)] = jnp.transpose(unit * gain_f + bias_f).astype(BF)
+    unit, scale_c = unit_rows(own_c, half_c)
+    part = part_of(own_c, half_c, dk[pl.ds(own_c, half_c), :], dv[pl.ds(own_c, half_c), :])
+    mine_s[pl.ds(half_p, half_c), :] = part
+    unit_s[pl.ds(half_p, half_c), :] = unit
+    g, b = gather(part, unit)
+    gain_grad, bias_grad = gain_grad + g, bias_grad + b
+    norm_s[:, pl.ds(own_c, half_c)] = jnp.transpose(unit * gain_f + bias_f).astype(BF)
+
+    for copy in local:
+        copy.wait()
+    for copy in first:
+        copy.wait_recv()
+    second = []
+    for i in range(2):
+        relay_s[i] = (loc_s[2 * i + 1].astype(F32) + near_s[2 * i + 1].astype(F32)).astype(BF)
+        second.append(remote(relay_s.at[i], far_s.at[i], peers[1]))
+
+    unit, _ = unit_rows(their_p, half_p)
+    norm_s[:, pl.ds(their_p, half_p)] = jnp.transpose(unit * gain_f + bias_f).astype(BF)
+    unit, scale_p = unit_rows(own_p, half_p)
+    unit_s[pl.ds(0, half_p), :] = unit
+    norm_s[:, pl.ds(own_p, half_p)] = jnp.transpose(unit * gain_f + bias_f).astype(BF)
+
+    blocks = 1 << bits
+    block = D // blocks
+
+    def keep(value, lane):
+        low = value.astype(BF)
+        for i in range(blocks):
+            late_s[i // 2, i % 2, :, pl.ds(lane, width)] = low[i * block : (i + 1) * block, :]
+
+    keep(dot_nn(norm_s[...], dq[...]), 0)
+    q_bias = column_sum(dq[...].astype(F32))
+
+    def norm_back(total, unit, scale, mixed):
+        shaped = total * gain_f
+        return mixed.astype(F32) + scale * (
+            shaped - jnp.mean(shaped, axis=1, keepdims=True) - unit * jnp.mean(shaped * unit, axis=1, keepdims=True)
+        )
+
+    y_cont.wait_recv()
+    total = mine_s[pl.ds(half_p, half_c), :] + recv_c[...].astype(F32)
+    give_c[...] = norm_back(total, unit_s[pl.ds(half_p, half_c), :], scale_c, gmix[pl.ds(half_p, half_c), :]).astype(BF)
+    back_c = remote(give_c, gin.at[pl.ds(own_c, half_c), :], across)
+    keep_c = pltpu.make_async_copy(give_c, gin.at[pl.ds(own_c, half_c), :], loc_sems.at[4])
+    keep_c.start()
+
+    for copy in second:
+        copy.wait_recv()
+    for i in range(2):
+        loc_s[2 * i] = (loc_s[2 * i].astype(F32) + near_s[2 * i].astype(F32) + far_s[i].astype(F32)).astype(BF)
+    part = part_of(their_p, half_p, loc_s[0, pl.ds(their_p, half_p), :], loc_s[2, pl.ds(their_p, half_p), :])
+    send_p[...] = part.astype(BF)
+    y_prompt = remote(send_p, recv_p, across)
+    unit, _ = unit_rows(their_p, half_p)
+    g, b = gather(part, unit)
+    gain_grad, bias_grad = gain_grad + g, bias_grad + b
+    part = part_of(own_p, half_p, loc_s[0, pl.ds(own_p, half_p), :], loc_s[2, pl.ds(own_p, half_p), :])
+    mine_s[pl.ds(0, half_p), :] = part
+    g, b = gather(part, unit_s[pl.ds(0, half_p), :])
+    gain_grad, bias_grad = gain_grad + g, bias_grad + b
+
+    for i, rest in enumerate((dk, dv)):
+        keep(
+            dot_nn(norm_s[:, pl.ds(0, prompt)], loc_s[2 * i])
+            + dot_nn(norm_s[:, pl.ds(prompt, conts)], rest[pl.ds(prompt, conts), :]),
+            (i + 1) * width,
+        )
+    v_bias = column_sum(loc_s[2].astype(F32)) + column_sum(dv[pl.ds(prompt, conts), :].astype(F32))
+
+    small_s[...] = jnp.zeros_like(small_s)
+    small_s[0:1, pl.ds(0, width)] = q_bias
+    small_s[1:2, pl.ds(0, width)] = v_bias
+    small_s[2:3, pl.ds(0, D)] = gain_grad
+    small_s[3:4, pl.ds(0, D)] = bias_grad
+    small = small_s[...]
+    row_id = lax.broadcasted_iota(jnp.int32, (8, 128), 0)
+    for i in range(blocks):
+        narrow = window(small, i * (width // blocks))
+        broad = window(small, i * block)
+        tail = jnp.concatenate([ext[i, pl.ds(32, 16), :].astype(F32)[0:8], jnp.where(row_id < 2, narrow, broad)], axis=0)
+        late_s[i // 2, i % 2, pl.ds(0, 32), pl.ds(3 * width, 128)] = ext[i, pl.ds(0, 32), :]
+        late_s[i // 2, i % 2, pl.ds(32, 16), pl.ds(3 * width, 128)] = tail.astype(BF)
+
+    source = late_s
+    stages = []
+    for bit in range(bits):
+        landing, kept = stage_refs[2 * bit], stage_refs[2 * bit + 1]
+        mine = (device // (1 << bit)) % 2
+        copy = remote(source.at[:, 1 - mine], landing, peers[bit])
+        if bit == 0:
+            y_prompt.wait_recv()
+            total = mine_s[pl.ds(0, half_p), :] + recv_p[...].astype(F32)
+            give_p[...] = norm_back(total, unit_s[pl.ds(0, half_p), :], scale_p, gmix[pl.ds(0, half_p), :]).astype(BF)
+            back_p = remote(give_p, gin.at[pl.ds(own_p, half_p), :], across)
+            keep_p = pltpu.make_async_copy(give_p, gin.at[pl.ds(own_p, half_p), :], loc_sems.at[5])
+            keep_p.start()
+        copy.wait_recv()
+        stages.append(copy)
+        for i in range(landing.shape[0]):
+            kept[i // 2, i % 2] = (source[i, mine].astype(F32) + landing[i].astype(F32)).astype(BF)
+        source = kept
+    late_out[...] = source[0, 0, :, pl.ds(0, 3 * width)].astype(F32)
+    vec_s[...] = source[0, 0, :, pl.ds(3 * width, 128)]
+    swap = remote(vec_s, vec_r, across)
+    swap.wait_recv()
+    vec_out[0] = vec_s[...].astype(F32)
+    vec_out[1] = vec_r[...].astype(F32)
+    for copy in first + second + stages + [y_cont, y_prompt, swap]:
+        copy.wait_send()
+    for copy in (back_c, back_p):
+        copy.wait_recv()
+        copy.wait_send()
+    keep_c.wait()
+    keep_p.wait()
+
+
+def finish(hid, gain, bias, dq, dk, dv, wq, wk, wv, gmix, ext, kp, vp):
+    rows, width = dq.shape
+    ranks = lax.axis_size("dp")
+    bits = ranks.bit_length() - 1
+    block = D // ranks
+    prompt = kp.shape[0] // GDEV
+    conts = rows - prompt
+    lanes = 3 * width + 128
+    vmem = pl.BlockSpec(memory_space=pltpu.VMEM)
+    hbm = pl.BlockSpec(memory_space=pl.ANY)
+    shape = jax.ShapeDtypeStruct
+    copies = 11 + bits
+    stages = []
+    for bit in range(bits):
+        left = ranks >> (bit + 1)
+        stages.append(pltpu.VMEM((left, block, lanes), BF))
+        stages.append(pltpu.VMEM((max(left // 2, 1), min(left, 2), block, lanes), BF))
+    return pl.pallas_call(
+        functools.partial(final_kernel, bits),
+        in_specs=[vmem] * 11 + [hbm] * 2,
+        out_specs=[hbm, vmem, vmem],
+        out_shape=[shape((rows, D), BF), shape((block, 3 * width), F32), shape((2, block, 128), F32)],
+        scratch_shapes=[
+            pltpu.VMEM((4, prompt, width), BF),
+            pltpu.VMEM((4, prompt, width), BF),
+            pltpu.VMEM((2, prompt, width), BF),
+            pltpu.VMEM((2, prompt, width), BF),
+            pltpu.VMEM((rows // 2, D), F32),
+            pltpu.VMEM((rows // 2, D), F32),
+            pltpu.VMEM((D, rows), BF),
+            pltpu.VMEM((conts // 2, D), BF),
+            pltpu.VMEM((conts // 2, D), BF),
+            pltpu.VMEM((prompt // 2, D), BF),
+            pltpu.VMEM((prompt // 2, D), BF),
+            pltpu.VMEM((conts // 2, D), BF),
+            pltpu.VMEM((prompt // 2, D), BF),
+            pltpu.VMEM((ranks // 2, 2, block, lanes), BF),
+            pltpu.VMEM((8, D + 128), F32),
+            pltpu.VMEM((block, 128), BF),
+            pltpu.VMEM((block, 128), BF),
+            pltpu.SemaphoreType.DMA((copies,)),
+            pltpu.SemaphoreType.DMA((copies,)),
+            pltpu.SemaphoreType.DMA((6,)),
+        ]
+        + stages,
+        compiler_params=pltpu.CompilerParams(vmem_limit_bytes=56 << 20, collective_id=1, has_side_effects=True),
+        cost_estimate=pl.CostEstimate(flops=5 * 10**9, bytes_accessed=20 * 10**6, transcendentals=0),
+        name="finish",
+    )(hid, gain, bias, dq, dk, dv, wq, wk, wv, gmix, ext, kp, vp)
 
 
 def flip(value, axis, bit):
@@ -608,6 +891,23 @@
         got = flip(sent, "dp", bit)
         current = (kept.astype(F32) + got.astype(F32)).astype(BF)
     return current.reshape(rows >> bits, columns)
+
+
+def half_of(value, which):
+    prompt, conts = CHUNK // 2, (value.shape[0] - CHUNK) // 2
+    return jnp.concatenate(
+        [
+            lax.dynamic_slice_in_dim(value, which * prompt, prompt),
+            lax.dynamic_slice_in_dim(value, CHUNK + which * conts, conts),
+        ]
+    )
+
+
+def joined(which, mine, other):
+    prompt = CHUNK // 2
+    low = jnp.where(which == 0, mine, other)
+    high = jnp.where(which == 0, other, mine)
+    return jnp.concatenate([low[:prompt], high[:prompt], low[prompt:], high[prompt:]])
 
 
 def body(
@@ -647,7 +947,6 @@
     units = inner_weight.shape[1]
     pairs = width // 128
     rows = hidden_in.shape[0]
-    half = rows // 2
     prompt_rows = CHUNK
     cont_count = (rows - prompt_rows) // CONT
 
@@ -683,12 +982,9 @@
     inner_parts = (inner_weight,) + fetch(inner_weight, core, 1)
     outer_parts = (outer_weight,) + fetch(outer_weight, core, 0)
     out_parts = (out_weight,) + fetch(out_weight, core, 0)
-    vectors = jnp.concatenate([ffn_gain, ffn_bias, inner_bias, sub_gain, sub_bias])
+    vectors = jnp.concatenate([ffn_gain, ffn_bias, inner_bias, sub_gain, sub_bias]).astype(F32)
     vectors_other = flip(vectors, "tensor", 0)
-    both = jnp.stack([vectors, vectors_other]).astype(F32)
-    vec_u = both[:, : 3 * units].reshape(2, 3, units).swapaxes(0, 1).reshape(3, 2 * units)
-    vec_w = both[:, 3 * units :].reshape(2, 2, width).swapaxes(0, 1).reshape(2, 2 * width)
-    vec_d = jnp.stack([out_bias, mid_gain, mid_bias, outer_bias]).astype(F32)
+    shared = jnp.concatenate([out_bias, mid_gain, mid_bias, outer_bias]).astype(F32)[None]
 
     inputs = hidden_in.astype(F32)
     pre_gain_f = pre_gain.astype(F32)
@@ -704,18 +1000,28 @@
     queries = ((dense(pre_low, query_weight) + query_bias.astype(F32)) * 0.125).astype(BF)
     attended, weighed, inverse = attend(info, tab, queries, keys, values, prompt_pair[0], prompt_pair[1])
 
-    own_at = tensor_id * half
-    other_at = (1 - tensor_id) * half
-    att_mine = lax.dynamic_slice_in_dim(attended, own_at, half)
-    att_got = flip(lax.dynamic_slice_in_dim(attended, other_at, half), "tensor", 0)
-    hidden_rows = lax.dynamic_slice_in_dim(hidden_in, own_at, half)
-    cot_rows = lax.dynamic_slice_in_dim(cotangent, own_at, half)
-    out_half, grad_mine, grad_theirs, grad_mixed_low, packed, sum_u, sum_w, sum_d = middle(
-        core[None].astype(jnp.int32), att_mine, att_got, hidden_rows, cot_rows, vec_u, vec_w, vec_d, inner_parts, outer_parts, out_parts
+    att_mine = half_of(attended, tensor_id)
+    att_got = flip(half_of(attended, 1 - tensor_id), "tensor", 0)
+    hidden_rows = half_of(hidden_in, tensor_id)
+    cot_rows = half_of(cotangent, tensor_id)
+    fused = D % (16 * ranks) == 0
+    out_half, grad_mine, grad_theirs, grad_mixed_low, packed, sum_u, sum_w, sum_d, ext = middle(
+        core[None].astype(jnp.int32),
+        att_mine,
+        att_got,
+        hidden_rows,
+        cot_rows,
+        vectors[None],
+        vectors_other[None],
+        shared,
+        inner_parts,
+        outer_parts,
+        out_parts,
+        ranks if fused else 1,
     )
 
     grad_got = flip(grad_theirs, "tensor", 0)
-    grad_attended = in_order(tensor_id, grad_mine, grad_got, 0)
+    grad_attended = joined(tensor_id, grad_mine, grad_got)
 
     early = lax.psum_scatter(packed, "dp", scatter_dimension=0, tiled=True)
     early_mine, early_other = jnp.split(early, 2, axis=1)
@@ -724,66 +1030,90 @@
     outer_weight_grad = early_sum[:, units : 2 * units].T
     out_weight_grad = early_sum[:, 2 * units :].T
 
-    output = in_order(tensor_id, out_half, flip(out_half, "tensor", 0), 0)
+    output = joined(tensor_id, out_half, flip(out_half, "tensor", 0))
 
     grad_query_in, key_acc, value_acc, own_key_grad, own_value_grad = attend_back(
         info, queries, keys, values, prompt_pair[0], prompt_pair[1], attended, inverse, grad_attended, weighed
     )
-    acc = jnp.stack([key_acc, value_acc]).reshape(2, GDEV, prompt_rows, width)
-    near = acc[:, 0::2].astype(F32) + flip(acc[:, 1::2], "dp", 0).astype(F32)
-    summed = (near[:, 0] + flip(near[:, 1].astype(BF), "dp", 1).astype(F32)).astype(BF)
-    grad_keys = jnp.concatenate([summed[0], own_key_grad[prompt_rows:]], axis=0)
-    grad_values = jnp.concatenate([summed[1], own_value_grad[prompt_rows:]], axis=0)
-
-    query_weight_grad = contract_rows(pre_low, grad_query_in)
-    key_weight_grad = contract_rows(pre_low, grad_keys)
-    value_weight_grad = contract_rows(pre_low, grad_values)
-    query_bias_grad = jnp.sum(grad_query_in.astype(F32), axis=0)
-    value_bias_grad = jnp.sum(grad_values.astype(F32), axis=0)
-    grad_normed_part = (
-        back_project(grad_query_in, query_weight)
-        + back_project(grad_keys, key_weight)
-        + back_project(grad_values, value_weight)
-    )
-    grad_normed_low = grad_normed_part.astype(BF)
-    grad_normed = grad_normed_low.astype(F32) + flip(grad_normed_low, "tensor", 0).astype(F32)
-    pre_gain_grad = jnp.sum(grad_normed * pre_unit, axis=0)
-    pre_bias_grad = jnp.sum(grad_normed, axis=0)
-    grad_mixed_all = in_order(tensor_id, grad_mixed_low, flip(grad_mixed_low, "tensor", 0), 0).astype(F32)
-    input_low = (grad_mixed_all + norm_back(grad_normed, pre_gain_f, pre_unit, pre_scale)).astype(BF)
-
+    block = D // ranks
     per_u, per_w, per_d = units // ranks, width // ranks, D // ranks
-    vec = jnp.concatenate(
-        [
-            sum_u[:3].reshape(3, 2, ranks, per_u).transpose(2, 1, 0, 3).reshape(ranks, 6 * per_u),
-            sum_w[:2].reshape(2, 2, ranks, per_w).transpose(2, 1, 0, 3).reshape(ranks, 4 * per_w),
-            sum_d[:4].reshape(4, ranks, per_d).swapaxes(0, 1).reshape(ranks, 4 * per_d),
-            jnp.stack([query_bias_grad, value_bias_grad]).reshape(2, ranks, per_w).swapaxes(0, 1).reshape(ranks, 2 * per_w),
-            jnp.stack([pre_gain_grad, pre_bias_grad]).reshape(2, ranks, per_d).swapaxes(0, 1).reshape(ranks, 2 * per_d),
-        ],
-        axis=1,
-    )
-    count = vec.shape[1]
-    block = D // ranks
-    vec = jnp.pad(vec, ((0, 0), (0, block * 128 - count))).reshape(D, 128)
-    late = halving(
-        jnp.concatenate(
-            [p.astype(BF) for p in (query_weight_grad, key_weight_grad, value_weight_grad, vec)], axis=1
-        ),
-        device,
-    )
-    vec = late[:, 3 * width :].reshape(-1)[:count]
-    late = late[:, : 3 * width].astype(F32)
-    at_w = 6 * per_u
-    at_d = at_w + 4 * per_w
-    at_late = at_d + 4 * per_d
-    got = flip(vec[:at_late], "tensor", 0).astype(F32)
-    vec = vec.astype(F32)
-    ffn_gain_grad, ffn_bias_grad, inner_bias_grad = (vec[: 3 * per_u] + got[3 * per_u : at_w]).reshape(3, per_u)
-    sub_gain_grad, sub_bias_grad = (vec[at_w : at_w + 2 * per_w] + got[at_w + 2 * per_w : at_d]).reshape(2, per_w)
-    out_bias_grad, mid_gain_grad, mid_bias_grad, outer_bias_grad = (vec[at_d:at_late] + got[at_d:]).reshape(4, per_d)
-    query_bias_grad, value_bias_grad = vec[at_late : at_late + 2 * per_w].reshape(2, per_w)
-    pre_gain_grad, pre_bias_grad = vec[at_late + 2 * per_w :].reshape(2, per_d)
+    if fused:
+        input_low, late, vec = finish(
+            hidden_in,
+            pre_gain_f[None],
+            pre_bias.astype(F32)[None],
+            grad_query_in,
+            own_key_grad,
+            own_value_grad,
+            query_weight,
+            key_weight,
+            value_weight,
+            grad_mixed_low,
+            ext,
+            key_acc,
+            value_acc,
+        )
+        ffn_gain_grad, ffn_bias_grad, inner_bias_grad = [vec[0, i, :per_u] + vec[1, 8 + i, :per_u] for i in range(3)]
+        sub_gain_grad, sub_bias_grad = [vec[0, 16 + i, :per_w] + vec[1, 24 + i, :per_w] for i in range(2)]
+        out_bias_grad, mid_gain_grad, mid_bias_grad, outer_bias_grad = [
+            vec[0, 32 + i, :per_d] + vec[1, 32 + i, :per_d] for i in range(4)
+        ]
+        query_bias_grad, value_bias_grad = [vec[0, 40 + i, :per_w] for i in range(2)]
+        pre_gain_grad, pre_bias_grad = [vec[0, 42 + i, :per_d] + vec[1, 42 + i, :per_d] for i in range(2)]
+    else:
+        acc = jnp.stack([key_acc, value_acc]).reshape(2, GDEV, prompt_rows, width)
+        near = acc[:, 0::2].astype(F32) + flip(acc[:, 1::2], "dp", 0).astype(F32)
+        summed = (near[:, 0] + flip(near[:, 1].astype(BF), "dp", 1).astype(F32)).astype(BF)
+        grad_keys = jnp.concatenate([summed[0], own_key_grad[prompt_rows:]], axis=0)
+        grad_values = jnp.concatenate([summed[1], own_value_grad[prompt_rows:]], axis=0)
+
+        query_weight_grad = contract_rows(pre_low, grad_query_in)
+        key_weight_grad = contract_rows(pre_low, grad_keys)
+        value_weight_grad = contract_rows(pre_low, grad_values)
+        query_bias_grad = jnp.sum(grad_query_in.astype(F32), axis=0)
+        value_bias_grad = jnp.sum(grad_values.astype(F32), axis=0)
+        grad_normed_part = (
+            back_project(grad_query_in, query_weight)
+            + back_project(grad_keys, key_weight)
+            + back_project(grad_values, value_weight)
+        )
+        grad_normed_low = grad_normed_part.astype(BF)
+        grad_normed = grad_normed_low.astype(F32) + flip(grad_normed_low, "tensor", 0).astype(F32)
+        pre_gain_grad = jnp.sum(grad_normed * pre_unit, axis=0)
+        pre_bias_grad = jnp.sum(grad_normed, axis=0)
+        grad_mixed_all = joined(tensor_id, grad_mixed_low, flip(grad_mixed_low, "tensor", 0)).astype(F32)
+        input_low = (grad_mixed_all + norm_back(grad_normed, pre_gain_f, pre_unit, pre_scale)).astype(BF)
+
+        vec = jnp.concatenate(
+            [
+                sum_u[:3].reshape(3, 2, ranks, per_u).transpose(2, 1, 0, 3).reshape(ranks, 6 * per_u),
+                sum_w[:2].reshape(2, 2, ranks, per_w).transpose(2, 1, 0, 3).reshape(ranks, 4 * per_w),
+                sum_d[:4].reshape(4, ranks, per_d).swapaxes(0, 1).reshape(ranks, 4 * per_d),
+                jnp.stack([query_bias_grad, value_bias_grad]).reshape(2, ranks, per_w).swapaxes(0, 1).reshape(ranks, 2 * per_w),
+                jnp.stack([pre_gain_grad, pre_bias_grad]).reshape(2, ranks, per_d).swapaxes(0, 1).reshape(ranks, 2 * per_d),
+            ],
+            axis=1,
+        )
+        count = vec.shape[1]
+        vec = jnp.pad(vec, ((0, 0), (0, block * 128 - count))).reshape(D, 128)
+        late = halving(
+            jnp.concatenate(
+                [p.astype(BF) for p in (query_weight_grad, key_weight_grad, value_weight_grad, vec)], axis=1
+            ),
+            device,
+        )
+        vec = late[:, 3 * width :].reshape(-1)[:count]
+        late = late[:, : 3 * width].astype(F32)
+        at_w = 6 * per_u
+        at_d = at_w + 4 * per_w
+        at_late = at_d + 4 * per_d
+        got = flip(vec[:at_late], "tensor", 0).astype(F32)
+        vec = vec.astype(F32)
+        ffn_gain_grad, ffn_bias_grad, inner_bias_grad = (vec[: 3 * per_u] + got[3 * per_u : at_w]).reshape(3, per_u)
+        sub_gain_grad, sub_bias_grad = (vec[at_w : at_w + 2 * per_w] + got[at_w + 2 * per_w : at_d]).reshape(2, per_w)
+        out_bias_grad, mid_gain_grad, mid_bias_grad, outer_bias_grad = (vec[at_d:at_late] + got[at_d:]).reshape(4, per_d)
+        query_bias_grad, value_bias_grad = vec[at_late : at_late + 2 * per_w].reshape(2, per_w)
+        pre_gain_grad, pre_bias_grad = vec[at_late + 2 * per_w :].reshape(2, per_d)
     return (
         output,
         input_low,

time: 456 us -> 383 us (0.84)
  Pallas kernels: 140 us -> 243 us
  waiting for transfers between devices: 119 us -> 50.2 us
  local copies, waits for them, and re-layouts: 68.8 us -> 28 us
  starting transfers between devices: 47.4 us -> 17.6 us
  other arithmetic: 40.2 us -> 19.5 us
  matrix products: 18.7 us -> 3.6 us
    pallas_call x0 -> x1, Pallas kernels: none -> 101 us  [finish(): pl.pallas_call(functools.partial(final_kernel, bits), in_specs=[vmem] * 1...]
    ppermute x23 -> x14, waiting for transfers between devices: 119 us -> 50.2 us  [flip(): lax.ppermute(value, axis, [(i, i ^ 1 << bit) for i in range(lax.axis_size...]
    ppermute x23 -> x14, starting transfers between devices: 47.4 us -> 17.5 us  [flip(): lax.ppermute(value, axis, [(i, i ^ 1 << bit) for i in range(lax.axis_size...]
    dot_general x6 -> x0, matrix products: 13.6 us -> none  [the longest x3 8.67 us: contract_rows(): lax.dot_general(left, right, (((0,), (0,)), ((), ())), preferred_element_...]
    reshape x12 -> x0, local copies, waits for them, and re-layouts: 13.3 us -> none  [the longest x3 4.27 us: body(): sum_u[:3].reshape(3, 2, ranks, per_u).transpose(2, 1, 0, 3)]
    another operation x14 -> x0, local copies, waits for them, and re-layouts: 10.5 us -> none  [the longest x4 5.05 us: body(): vec_d = jnp.stack([out_bias, mid_gain, mid_bias, outer_bias]).astype(F32)]
    convert_element_type x10 -> x3, other arithmetic: 10.5 us -> 1.3 us  [the longest x1 0.66 us: body(): jnp.concatenate([out_bias, mid_gain, mid_bias, outer_bias]).astype(F32)]
    reduce_sum x5 -> x0, other arithmetic: 6.92 us -> none  [the longest x1 4.67 us: body(): pre_gain_grad = jnp.sum(grad_normed * pre_unit, axis=0)]
  transfers between devices with their start and end apart: 24 -> 15, of which waited for: 13 -> 5; matrix products, arithmetic and copies ran while one was open for 25% -> 9% of each run, Pallas kernels for 20% -> 50%
where the time goes in v3:
time: 383 us; the launch traced here: 378 us
  Pallas kernels  243 us (63%)
  waiting for transfers between devices  50.2 us (13%)
  local copies, waits for them, and re-layouts  28 us (7%)
  other arithmetic  19.5 us (5%)
  starting transfers between devices  17.6 us (5%)
  between operations  16.4 us (4%)
    pallas_call x1, Pallas kernels, finish(): pl.pallas_call(functools.partial(final_kernel, bits), in_specs=[vmem] * 1...  101 us
    pallas_call x1, Pallas kernels, middle(): pl.pallas_call(mid_kernel, in_specs=[pl.BlockSpec(memory_space=pltpu.SMEM...  52.7 us
    ppermute x14, waiting for transfers between devices, flip(): lax.ppermute(value, axis, [(i, i ^ 1 << bit) for i in range(lax.axis_size...  50.2 us
    pallas_call x1, Pallas kernels, attend_back(): pl.pallas_call(bwd_kernel, grid_spec=pltpu.PrefetchScalarGridSpec(num_sca...  47.3 us
    pallas_call x1, Pallas kernels, attend(): pl.pallas_call(fwd_kernel, grid_spec=pltpu.PrefetchScalarGridSpec(num_sca...  41.7 us
    ppermute x14, starting transfers between devices, flip(): lax.ppermute(value, axis, [(i, i ^ 1 << bit) for i in range(lax.axis_size...  17.5 us
    unnamed x103, local copies, waits for them, and re-layouts  11.3 us
  transfers between devices with their start and end apart: 15, of which 5 were waited for; matrix products, arithmetic and copies ran while one was open for 9% of the time, Pallas kernels for 50%

profile of v3, /device:TPU:0, one launch (start us, length us, event | category | flops | bytes accessed | tf_op | source)
XLA Modules:
  0.0 377.8 jit_solution(1009693728158466457)
XLA Ops:
  7.3 2.3 convert_reduce_fusion
  9.7 0.8 fusion.3
  10.5 0.3 copy-done.40
  10.8 1.2 convolution_convert_fusion.ko_ref
  12.2 1.2 fusion.6.vo_ref
  13.6 1.0 copy-done.6
  14.5 0.7 copy-done.15
  15.3 1.0 pad_maximum_fusion.5
  16.2 2.9 collective-permute-start.1
  19.2 2.5 constant_dynamic-slice_fusion.2
  21.8 1.6 collective-permute-start.5
  23.4 1.1 constant_dynamic-slice_fusion.1
  24.5 0.5 collective-permute-start.7
  25.0 1.7 constant_dynamic-slice_fusion
  26.7 1.5 collective-permute-start.9
  28.8 0.6 dynamic_slice.48
  30.8 0.8 add_bitcast_fusion.11
  31.7 0.7 pad_add_fusion.info
  32.6 0.8 dynamic-update-slice
  33.4 0.3 dynamic-update-slice.1
  34.5 1.3 constant_dynamic-slice_fusion.3
  35.9 1.2 collective-permute-done.1
  37.0 1.0 constant_dynamic-slice_fusion.4
  38.1 1.2 fusion.7.q_ref
  39.3 0.7 maximum_convert_fusion.vec_d
  40.0 1.8 collective-permute-start.4
  41.8 9.2 %collective-permute-done.5.w1_got = bf16[768,768]{1,0:T(8,128)(2,1)} collective-permute-done((bf16[768,768]{1,0:T(8,128)(2,1)}, bf16[768,768]{1,0:T(8,128)(2,1)}, u32[]{:S(2)}, u32[]{:S(2)}) %collective-permute-start.5) | collective-permute-done | bytes 1179680 | tf_op jit(solution)/shard_map/ppermute | solution.py:835
  51.0 25.3 %collective-permute-done.7.w2_got = bf16[768,768]{1,0:T(8,128)(2,1)} collective-permute-done((bf16[768,768]{1,0:T(8,128)(2,1)}, bf16[768,768]{1,0:T(8,128)(2,1)}, u32[]{:S(2)}, u32[]{:S(2)}) %collective-permute-start.7) | collective-permute-done | bytes 1179680 | tf_op jit(solution)/shard_map/ppermute | solution.py:835
  76.2 2.7 pad_maximum_fusion
  78.9 1.5 slice_bitcast_fusion
  80.4 41.7 %attend.1 = (bf16[1280,384]{1,0:T(8,128)(2,1)S(1)}, bf16[6,1280,2304]{2,1,0:T(8,128)(2,1)}, f32[1280,384]{1,0:T(8,128)}) custom-call(s32[7]{0:T(128)S(1)} %pad_add_fusion.info, f32[30]{0:T(128)S(1)} %reshape.220.tab, bf16[1280,384]{1,0:T(8,128)(2,1)S(1)} %fusion.7.q_ref, bf16[2048,384]{1,0:T(8,128)(2,1)S(1)} %get-tuple-element.58.kp_ref, ...), custom_call_target="tpu_custom_call" | custom-call | flops 16000000000 | bytes 60000000 | tf_op jit(solution)/shard_map/attend/pallas_call | solution.py:164
  122.3 1.6 collective-permute-start.3
  123.9 1.0 pad_maximum_fusion.2.hid
  124.9 1.0 pad_maximum_fusion.3.cot
  126.0 5.5 %collective-permute-start.10 = (bf16[192,768]{1,0:T(8,128)(2,1)}, bf16[192,768]{1,0:T(8,128)(2,1)S(1)}, u32[]{:S(2)}, u32[]{:S(2)}) collective-permute-start(bf16[192,768]{1,0:T(8,128)(2,1)} %collective-permute-done.9.wo_got), channel_id=1, source_target_pairs={{0,2},{2,0},{4,6},{6,4},{8,10},{10,8},{12,14},{14,12},{16,18},{18,... | collective-permute-start | bytes 884744 | tf_op jit(solution)/shard_map/ppermute | solution.py:835
  131.5 0.6 convert_element_type.109.vec_own
  132.1 0.6 broadcast_in_dim.9.vec_got
  132.7 0.8 pad_maximum_fusion.6.att_m
  133.6 0.7 copy-done.43
  134.4 52.7 %middle.1 = (bf16[640,768]{1,0:T(8,128)(2,1)}, bf16[640,384]{1,0:T(8,128)(2,1)}, bf16[640,384]{1,0:T(8,128)(2,1)}, bf16[640,768]{1,0:T(8,128)(2,1)}, bf16[768,69...) custom-call(s32[1]{0:T(128)} %bitcast.info, ...), custom_call_target="tpu_custom_call" | custom-call | flops 20999999488 | bytes 30000000 | tf_op jit(solution)/shard_map/middle/pallas_call | solution.py:548
  187.3 1.0 copy-done.42
  188.2 0.5 collective-permute-start.12
  188.8 0.6 broadcast_in_dim.10.gain
  189.3 0.6 broadcast_in_dim.11.bias
  189.9 1.5 collective-permute-start.11
  191.4 9.1 %collective-permute-done.12 = bf16[640,384]{1,0:T(8,128)(2,1)S(1)} collective-permute-done((bf16[640,384]{1,0:T(8,128)(2,1)S(1)}, bf16[640,384]{1,0:T(8,128)(2,1)S(1)}, u32[]{:S(2)}, u32[]{:S(2)}) %collective-permute-start.12) | collective-permute-done | bytes 491552 | tf_op jit(solution)/shard_map/ppermute | solution.py:835
  200.8 1.1 pad_maximum_fusion.4.g_ref
  201.9 0.6 copy-done.8
  202.5 0.3 copy-done.10
  202.8 47.3 %attend_back.1 = (bf16[1280,384]{1,0:T(8,128)(2,1)S(1)}, bf16[2048,384]{1,0:T(8,128)(2,1)}, bf16[2048,384]{1,0:T(8,128)(2,1)}, bf16[1280,384]{1,0:T(8,128)(2,1)S(1)}, bf16[1280,384]{1,0:T(8,128)(2,1)S(1)}) custom-call(s32[7]{0:T(128)S(1)} %pad_add_fusion.info, bf16[1280,384]{1,0:T(8,128)(2,1)S(1)} %copy-done.10, bf16[2048,384]{1,0:T(8,128)(2,1)} %copy-done.2, ...), custom_call_target="tpu_custom_call" | custom-call | flops 30000001024 | bytes 60000000 | tf_op jit(solution)/shard_map/attend_back/pallas_call | solution.py:261
  250.2 0.9 copy-done.11
  251.1 0.9 copy-done.12
  252.1 1.0 copy-done.13
  253.0 100.9 %finish.1 = (bf16[1280,768]{1,0:T(8,128)(2,1)}, f32[48,1152]{1,0:T(8,128)}, f32[2,48,128]{2,1,0:T(8,128)}) custom-call(bf16[1280,768]{1,0:T(8,128)(2,1)} %hid.1, f32[1,768]{1,0:T(1,128)} %broadcast_in_dim.10.gain, f32[1,768]{1,0:T(1,128)} %broadcast_in_dim.11.bias, bf16[1280,384]{1,0:T(8,128)(2,1)} %copy-done.11, bf16[1280,384]{1,0:T(8,128)(2,1)} %copy-done.12, ...), custom_call_target="tpu_custom_call" | custom-call | flops 5000000000 | bytes 20000000 | tf_op jit(solution)/shard_map/finish/pallas_call | solution.py:800
  354.0 1.3 add_bitcast_fusion.1
  355.3 1.3 add_bitcast_fusion.7
  356.6 1.4 add_bitcast_fusion
  358.0 1.6 fusion.23
  359.6 1.0 split.9
  361.0 1.4 pad_maximum_fusion.1
  362.4 5.4 %collective-permute-done.13 = bf16[48,3456]{1,0:T(8,128)(2,1)S(1)} collective-permute-done((bf16[48,3456]{1,0:T(8,128)(2,1)S(1)}, bf16[48,3456]{1,0:T(8,128)(2,1)S(1)}, u32[]{:S(2)}, u32[]{:S(2)}) %collective-permute-start.13) | collective-permute-done | bytes 331808 | tf_op jit(solution)/shard_map/ppermute | solution.py:835
  367.9 0.9 slice_bitcast_fusion.4
  368.8 0.6 slice_bitcast_fusion.5
  369.4 1.3 copy.65
  (145 shorter events, 3.4 us)
Async XLA Ops:
  7.2 21.0 %copy-start = (s32[6,3]{0,1:T(4,128)S(1)}, s32[6,3]{0,1:T(4,128)}, u32[]{:S(2)}) copy-start(s32[6,3]{0,1:T(4,128)} %param.30) | copy-start | bytes 220
  7.2 2.5 copy-start.14
  7.2 2.4 copy-start.27
  7.2 2.4 copy-start.28
  7.2 2.4 copy-start.36
  7.3 352.4 %reduce-scatter.2.cloned.1.call-start = ((), (), s32[]{:S(2)}) async-start(), calls=%async_computation.1 | async-start | bytes 11280384 | tf_op jit(solution)/shard_map/reduce_scatter | solution.py:1026
  9.7 1.1 copy-start.40
  10.8 1.3 copy-start.17
  10.8 1.5 copy-start.39
  12.2 68.2 %copy-start.4 = (bf16[1280,384]{1,0:T(8,128)(2,1)}, bf16[1280,384]{1,0:T(8,128)(2,1)S(1)}, u32[]{:S(2)}) copy-start(bf16[1280,384]{1,0:T(8,128)(2,1)S(1)} %convolution_convert_fusion.ko_ref) | copy-start | bytes 2949124
  13.5 1.0 copy-start.6
  14.5 0.7 copy-start.15
  16.2 20.8 %collective-permute-start.1 = (bf16[2,512,384]{2,1,0:T(8,128)(2,1)}, bf16[2,512,384]{2,1,0:T(8,128)(2,1)}, u32[]{:S(2)}, u32[]{:S(2)}) collective-permute-start(bf16[2,512,384]{2,1,0:T(8,128)(2,1)} %pad_maximum_fusion.5), channel_id=1, source_target_pairs={{0,4},{2,6},{4,0},{6,2},{8,12},{10,14},{12,8},{14,10},{16,20},{18,... | collective-permute-start | bytes 2359304 | tf_op jit(solution)/shard_map/ppermute | solution.py:835
  19.2 20.8 %collective-permute-start = (bf16[2,512,384]{2,1,0:T(8,128)(2,1)}, bf16[2,512,384]{2,1,0:T(8,128)(2,1)}, u32[]{:S(2)}, u32[]{:S(2)}) collective-permute-start(bf16[2,512,384]{2,1,0:T(8,128)(2,1)} %pad_maximum_fusion.5), channel_id=1, source_target_pairs={{0,2},{2,0},{4,6},{6,4},{8,10},{10,8},{12,14},{14,12},{16,18},{18,... | collective-permute-start | bytes 2359304 | tf_op jit(solution)/shard_map/ppermute | solution.py:835
  19.2 4.2 %copy-start.22 = (bf16[1536,768]{1,0:T(8,128)(2,1)S(1)}, bf16[1536,768]{1,0:T(8,128)(2,1)}, u32[]{:S(2)}) copy-start(bf16[1536,768]{1,0:T(8,128)(2,1)} %w2_own.1) | copy-start | bytes 7077892
  21.7 6.8 %copy-start.31 = (s32[6,3]{0,1:T(4,128)S(1)}, s32[6,3]{0,1:T(4,128)}, u32[]{:S(2)}) copy-start(s32[6,3]{0,1:T(4,128)} %param.29) | copy-start | bytes 220
  21.7 7.1 %copy-start.44 = (s32[4]{0:T(128)S(1)}, s32[4]{0:T(128)}, u32[]{:S(2)}) copy-start(s32[4]{0:T(128)} %param.27) | copy-start | bytes 52
  21.7 9.0 %copy-start.24 = (bf16[1536]{0:T(1024)(128)(2,1)S(1)}, bf16[1536]{0:T(1024)(128)(2,1)}, u32[]{:S(2)}) copy-start(bf16[1536]{0:T(1024)(128)(2,1)} %param.46) | copy-start | bytes 9220
  21.7 9.0 %copy-start.25 = (bf16[1536]{0:T(1024)(128)(2,1)S(1)}, bf16[1536]{0:T(1024)(128)(2,1)}, u32[]{:S(2)}) copy-start(bf16[1536]{0:T(1024)(128)(2,1)} %param.47) | copy-start | bytes 9220
  21.7 10.9 %copy-start.37 = (bf16[384]{0:T(512)(128)(2,1)S(1)}, bf16[384]{0:T(512)(128)(2,1)}, u32[]{:S(2)}) copy-start(bf16[384]{0:T(512)(128)(2,1)} %param.34) | copy-start | bytes 2308
  21.7 12.0 %copy-start.26 = (bf16[1536]{0:T(1024)(128)(2,1)S(1)}, bf16[1536]{0:T(1024)(128)(2,1)}, u32[]{:S(2)}) copy-start(bf16[1536]{0:T(1024)(128)(2,1)} %param.45) | copy-start | bytes 9220
  21.7 12.2 %copy-start.29 = (bf16[384]{0:T(512)(128)(2,1)S(1)}, bf16[384]{0:T(512)(128)(2,1)}, u32[]{:S(2)}) copy-start(bf16[384]{0:T(512)(128)(2,1)} %param.38) | copy-start | bytes 2308
  21.7 12.5 %copy-start.30 = (bf16[384]{0:T(512)(128)(2,1)S(1)}, bf16[384]{0:T(512)(128)(2,1)}, u32[]{:S(2)}) copy-start(bf16[384]{0:T(512)(128)(2,1)} %param.39) | copy-start | bytes 2308
  21.8 12.7 %copy-start.32 = (bf16[768]{0:T(1024)(128)(2,1)S(1)}, bf16[768]{0:T(1024)(128)(2,1)}, u32[]{:S(2)}) copy-start(bf16[768]{0:T(1024)(128)(2,1)} %param.41) | copy-start | bytes 4612
  21.8 12.7 %copy-start.33 = (bf16[768]{0:T(1024)(128)(2,1)S(1)}, bf16[768]{0:T(1024)(128)(2,1)}, u32[]{:S(2)}) copy-start(bf16[768]{0:T(1024)(128)(2,1)} %param.42) | copy-start | bytes 4612
  21.8 12.7 %copy-start.34 = (bf16[768]{0:T(1024)(128)(2,1)S(1)}, bf16[768]{0:T(1024)(128)(2,1)}, u32[]{:S(2)}) copy-start(bf16[768]{0:T(1024)(128)(2,1)} %param.43) | copy-start | bytes 4612
  21.8 12.7 %copy-start.35 = (bf16[768]{0:T(1024)(128)(2,1)S(1)}, bf16[768]{0:T(1024)(128)(2,1)}, u32[]{:S(2)}) copy-start(bf16[768]{0:T(1024)(128)(2,1)} %param.49) | copy-start | bytes 4612
  21.8 29.1 %collective-permute-start.5 = (bf16[768,768]{1,0:T(8,128)(2,1)}, bf16[768,768]{1,0:T(8,128)(2,1)}, u32[]{:S(2)}, u32[]{:S(2)}) collective-permute-start(bf16[768,768]{1,0:T(8,128)(2,1)} %constant_dynamic-slice_fusion.2), channel_id=1, source_target_pairs={{0,1},{1,0},{2,3},{3,2},{4,5},{5,4},{6,7},{7,6},{8,9},{9,8},{10,11... | collective-permute-start | bytes 3538952 | tf_op jit(solution)/shard_map/ppermute | solution.py:835
  24.5 51.7 %collective-permute-start.7 = (bf16[768,768]{1,0:T(8,128)(2,1)}, bf16[768,768]{1,0:T(8,128)(2,1)}, u32[]{:S(2)}, u32[]{:S(2)}) collective-permute-start(bf16[768,768]{1,0:T(8,128)(2,1)} %constant_dynamic-slice_fusion.1), channel_id=1, source_target_pairs={{0,1},{1,0},{2,3},{3,2},{4,5},{5,4},{6,7},{7,6},{8,9},{9,8},{10,11... | collective-permute-start | bytes 3538952 | tf_op jit(solution)/shard_map/ppermute | solution.py:835
  26.7 99.3 %collective-permute-start.9 = (bf16[192,768]{1,0:T(8,128)(2,1)}, bf16[192,768]{1,0:T(8,128)(2,1)}, u32[]{:S(2)}, u32[]{:S(2)}) collective-permute-start(bf16[192,768]{1,0:T(8,128)(2,1)} %constant_dynamic-slice_fusion), channel_id=1, source_target_pairs={{0,1},{1,0},{2,3},{3,2},{4,5},{5,4},{6,7},{7,6},{8,9},{9,8},{10,11... | collective-permute-start | bytes 884744 | tf_op jit(solution)/shard_map/ppermute | solution.py:835
  34.5 3.6 copy-start.18
  34.5 3.6 copy-start.38
  37.0 39.2 %collective-permute-start.2 = (bf16[2,512,384]{2,1,0:T(8,128)(2,1)}, bf16[2,512,384]{2,1,0:T(8,128)(2,1)S(1)}, u32[]{:S(2)}, u32[]{:S(2)}) collective-permute-start(bf16[2,512,384]{2,1,0:T(8,128)(2,1)} %collective-permute-done.1), channel_id=1, source_target_pairs={{0,2},{2,0},{4,6},{6,4},{8,10},{10,8},{12,14},{14,12},{16,18},{18,... | collective-permute-start | bytes 2359304 | tf_op jit(solution)/shard_map/ppermute | solution.py:835
  38.1 38.1 %copy-start.16 = (bf16[1,512,384]{2,1,0:T(8,128)(2,1)S(1)}, bf16[1,512,384]{2,1,0:T(8,128)(2,1)}, u32[]{:S(2)}) copy-start(bf16[1,512,384]{2,1,0:T(8,128)(2,1)} %copy-done.15) | copy-start | bytes 1179652
  39.3 41.1 %copy-start.9 = (bf16[1280,384]{1,0:T(8,128)(2,1)}, bf16[1280,384]{1,0:T(8,128)(2,1)S(1)}, u32[]{:S(2)}) copy-start(bf16[1280,384]{1,0:T(8,128)(2,1)S(1)} %fusion.7.q_ref) | copy-start | bytes 2949124
  40.0 92.1 %collective-permute-start.4 = (f32[5376]{0:T(1024)S(1)}, f32[5376]{0:T(1024)S(1)}, u32[]{:S(2)}, u32[]{:S(2)}) collective-permute-start(f32[5376]{0:T(1024)S(1)} %convert_element_type.110), channel_id=1, source_target_pairs={{0,1},{1,0},{2,3},{3,2},{4,5},{5,4},{6,7},{7,6},{8,9},{9,8},{10,11... | collective-permute-start | bytes 64520 | tf_op jit(solution)/shard_map/ppermute | solution.py:835
  51.0 82.6 %collective-permute-start.6 = (bf16[768,768]{1,0:T(8,128)(2,1)}, bf16[768,768]{1,0:T(8,128)(2,1)}, u32[]{:S(2)}, u32[]{:S(2)}) collective-permute-start(bf16[768,768]{1,0:T(8,128)(2,1)} %collective-permute-done.5.w1_got), channel_id=1, source_target_pairs={{0,2},{2,0},{4,6},{6,4},{8,10},{10,8},{12,14},{14,12},{16,18},{18,... | collective-permute-start | bytes 3538952 | tf_op jit(solution)/shard_map/ppermute | solution.py:835
  76.2 57.4 %collective-permute-start.8 = (bf16[768,768]{1,0:T(8,128)(2,1)}, bf16[768,768]{1,0:T(8,128)(2,1)}, u32[]{:S(2)}, u32[]{:S(2)}) collective-permute-start(bf16[768,768]{1,0:T(8,128)(2,1)} %collective-permute-done.7.w2_got), channel_id=1, source_target_pairs={{0,2},{2,0},{4,6},{6,4},{8,10},{10,8},{12,14},{14,12},{16,18},{18,... | collective-permute-start | bytes 3538952 | tf_op jit(solution)/shard_map/ppermute | solution.py:835
  78.9 1.5 copy-start.7
  80.4 41.7 %copy-start.2 = (bf16[2048,384]{1,0:T(8,128)(2,1)}, bf16[2048,384]{1,0:T(8,128)(2,1)S(1)}, u32[]{:S(2)}) copy-start(bf16[2048,384]{1,0:T(8,128)(2,1)S(1)} %get-tuple-element.58.kp_ref) | copy-start | bytes 4718596
  122.1 2.8 copy-start.3
  122.3 11.2 %collective-permute-start.3 = (bf16[640,384]{1,0:T(8,128)(2,1)S(1)}, bf16[640,384]{1,0:T(8,128)(2,1)S(1)}, u32[]{:S(2)}, u32[]{:S(2)}) collective-permute-start(bf16[640,384]{1,0:T(8,128)(2,1)S(1)} %pad_maximum_fusion.7), channel_id=1, source_target_pairs={{0,1},{1,0},{2,3},{3,2},{4,5},{5,4},{6,7},{7,6},{8,9},{9,8},{10,11... | collective-permute-start | bytes 1474568 | tf_op jit(solution)/shard_map/ppermute | solution.py:835
  126.0 7.6 %collective-permute-start.10 = (bf16[192,768]{1,0:T(8,128)(2,1)}, bf16[192,768]{1,0:T(8,128)(2,1)S(1)}, u32[]{:S(2)}, u32[]{:S(2)}) collective-permute-start(bf16[192,768]{1,0:T(8,128)(2,1)} %collective-permute-done.9.wo_got), channel_id=1, source_target_pairs={{0,2},{2,0},{4,6},{6,4},{8,10},{10,8},{12,14},{14,12},{16,18},{18,... | collective-permute-start | bytes 884744 | tf_op jit(solution)/shard_map/ppermute | solution.py:835
  133.6 0.7 copy-start.43
  133.6 0.9 copy-start.41
  187.2 1.0 copy-start.42
  187.2 2.7 copy-start.20
  187.2 13.3 %copy-start.23 = (bf16[640,384]{1,0:T(8,128)(2,1)S(1)}, bf16[640,384]{1,0:T(8,128)(2,1)}, u32[]{:S(2)}) copy-start(bf16[640,384]{1,0:T(8,128)(2,1)} %get-tuple-element.41) | copy-start | bytes 1474564
  188.2 12.3 %collective-permute-start.12 = (bf16[640,384]{1,0:T(8,128)(2,1)S(1)}, bf16[640,384]{1,0:T(8,128)(2,1)S(1)}, u32[]{:S(2)}, u32[]{:S(2)}) collective-permute-start(bf16[640,384]{1,0:T(8,128)(2,1)S(1)} %copy-done.42), channel_id=1, source_target_pairs={{0,1},{1,0},{2,3},{3,2},{4,5},{5,4},{6,7},{7,6},{8,9},{9,8},{10,11... | collective-permute-start | bytes 1474568 | tf_op jit(solution)/shard_map/ppermute | solution.py:835
  189.9 170.8 %collective-permute-start.11 = (bf16[640,768]{1,0:T(8,128)(2,1)S(1)}, bf16[640,768]{1,0:T(8,128)(2,1)S(1)}, u32[]{:S(2)}, u32[]{:S(2)}) collective-permute-start(bf16[640,768]{1,0:T(8,128)(2,1)S(1)} %copy-done.20), channel_id=1, source_target_pairs={{0,1},{1,0},{2,3},{3,2},{4,5},{5,4},{6,7},{7,6},{8,9},{9,8},{10,11... | collective-permute-start | bytes 2949128 | tf_op jit(solution)/shard_map/ppermute | solution.py:835
  200.7 1.2 copy-start.5
  200.7 1.8 copy-start.8
  200.7 2.1 copy-start.10
  250.2 0.9 copy-start.11
  251.1 0.9 copy-start.12
  252.0 1.0 copy-start.13
  360.6 7.2 %collective-permute-start.13 = (bf16[48,3456]{1,0:T(8,128)(2,1)S(1)}, bf16[48,3456]{1,0:T(8,128)(2,1)S(1)}, u32[]{:S(2)}, u32[]{:S(2)}) collective-permute-start(bf16[48,3456]{1,0:T(8,128)(2,1)S(1)} %split.9), channel_id=1, source_target_pairs={{0,1},{1,0},{2,3},{3,2},{4,5},{5,4},{6,7},{7,6},{8,9},{9,8},{10,11... | collective-permute-start | bytes 995336 | tf_op jit(solution)/shard_map/ppermute | solution.py:835
  361.0 6.8 %copy-start.21 = (bf16[48,6912]{1,0:T(8,128)(2,1)S(1)}, bf16[48,6912]{1,0:T(8,128)(2,1)}, u32[]{:S(2)}) copy-start(bf16[48,6912]{1,0:T(8,128)(2,1)} %reduce-scatter.2.cloned.1.call-done) | copy-start | bytes 1990660
  362.4 7.0 %copy-start.19 = (bf16[1280,768]{1,0:T(8,128)(2,1)S(1)}, bf16[1280,768]{1,0:T(8,128)(2,1)}, u32[]{:S(2)}) copy-start(bf16[1280,768]{1,0:T(8,128)(2,1)} %get-tuple-element.132) | copy-start | bytes 5898244
  369.4 1.3 copy-start.1
Sparse Core Ops, SparseCore 0:
  187.4 138.3 reduce-scatter.1
